TPU v7x, 32 devices: a whole 2x2x4 slice. The times are simulated.
32 devices in a mesh: groups: 2 (over y), ctx: 4 (over z), tp: 2 (over x), dp: 2 (over core).
Axes of the slice: x: 2, y: 2, z: 4, core: 2. Of those that a mesh axis runs over, the one named last changes fastest.
Arguments:
- hyena_in: bfloat16 [4, 576, 3, 8192], P(('groups', 'dp'), 'ctx', None, 'tp'), parts along dimension 0, may hold values from -6 to 6
- short_filter: bfloat16 [3, 7, 8192], P(None, None, 'tp'), may hold values from -2 to 2
- long_filter: bfloat16 [128, 512], P(None, 'tp'), may hold values from -0.5 to 0.5
- qkv: bfloat16 [4, 576, 3, 8192], P(('groups', 'dp'), 'ctx', None, 'tp'), parts along dimension 0, may hold values from -8 to 8
- lengths: int32 [4, 4], P(('groups', 'dp')), parts along dimension 0, may hold values from 1 to 432, 576 in all within a row
Outputs:
- hyena_out: bfloat16 [4, 576, 8192], P(('groups', 'dp'), 'ctx', 'tp'), parts along dimension 0
- attn_out: bfloat16 [4, 576, 8192], P(('groups', 'dp'), 'ctx', 'tp'), parts along dimension 0
There are 2 independent parts, one for each index of `groups`. A program takes and returns all parts, laid end to end along the dimension named above; an argument that names none is the same for every part. Nothing has to cross between parts.
Inputs may be any that keep to these rules, and one draw needn't show every extreme that they name: Each stream is 4 packed sequences laid end to end from its first token, with lengths summing to 576; the longest is exactly 432.
All inputs are finite; a program needn't handle non-finite values.
Results may differ from a plain program's by a relative error of at most 0.005.
Values may be sent and summed in bfloat16 or wider, within the bound.
No kernel may reach another device: no remote copies, remote signals or barrier semaphores. Data moves between devices by JAX's collectives and lax.ppermute only.
A program may use at most 128 MiB of HBM per device.

v0:
```python
from functools import partial
import math

import jax
import jax.numpy as jnp
from jax import lax
from jax.experimental import pallas as pl
from jax.experimental.pallas import tpu as pltpu
from jax.sharding import PartitionSpec as P

H = 64
LANES = 128
CHUNKS = 2
NEG = -1e30
FLOOR = -1e29


def bounds_of(lengths_ref):
    ends, total = [], 0
    for i in range(lengths_ref.shape[1] - 1):
        total = total + lengths_ref[0, i]
        ends.append(total)
    return ends


def start_of(places, ends):
    start = jnp.zeros(places.shape, jnp.int32)
    for end in ends:
        start = jnp.where(places >= end, end, start)
    return start


def tail_kernel(where_ref, lengths_ref, x_ref, taps_ref, out_ref, line, keep):
    count = x_ref.shape[1]
    reach = line.shape[1]
    first = count - reach
    short = taps_ref.shape[1]
    ends = bounds_of(lengths_ref)
    anchor = where_ref[0] * count

    @pl.when(pl.program_id(0) == 0)
    def _():
        place = anchor + first + lax.broadcasted_iota(jnp.int32, (reach, LANES), 0)
        start = start_of(place, ends)
        for tap in range(short):
            keep[tap] = (place - tap >= start).astype(jnp.float32)

    def one(i, carry):
        lanes = pl.ds(pl.multiple_of(i * LANES, LANES), LANES)
        mixed = []
        for which, slot in enumerate((0, 2)):
            line[which] = x_ref[slot, first:count, lanes].astype(jnp.float32)
            head = x_ref[slot, first - 16:first, lanes].astype(jnp.float32)
            total = taps_ref[slot, 0:1, lanes].astype(jnp.float32) * line[which]
            joined = jnp.concatenate([head[8:], line[which]], axis=0)
            for tap in range(1, short):
                total = total + (
                    taps_ref[slot, tap:tap + 1, lanes].astype(jnp.float32)
                    * joined[8 - tap:8 - tap + reach]
                    * keep[tap]
                )
            mixed.append(total)
        out_ref[0:reach, lanes] = (mixed[0] * mixed[1]).astype(out_ref.dtype)
        for slot in range(3):
            out_ref[reach + 16 * slot:reach + 16 * (slot + 1), lanes] = x_ref[
                slot, count - 16:count, lanes
            ]
        return carry

    lax.fori_loop(0, x_ref.shape[2] // LANES, one, 0)


def mixer_tail(index, lengths, inputs, short_filter, reach):
    slots, count, width = inputs.shape
    block = min(width, 1024)
    short = short_filter.shape[1]
    rows = reach + 16 * slots
    return pl.pallas_call(
        tail_kernel,
        out_shape=jax.ShapeDtypeStruct((rows, width), inputs.dtype),
        grid_spec=pltpu.PrefetchScalarGridSpec(
            num_scalar_prefetch=2,
            grid=(width // block,),
            in_specs=[
                pl.BlockSpec((slots, count, block), lambda i, *_: (0, 0, i)),
                pl.BlockSpec((slots, short, block), lambda i, *_: (0, 0, i)),
            ],
            out_specs=pl.BlockSpec((rows, block), lambda i, *_: (0, i)),
            scratch_shapes=[
                pltpu.VMEM((2, reach, LANES), jnp.float32),
                pltpu.VMEM((short, reach, LANES), jnp.float32),
            ],
        ),
        name="mixer_tail",
    )(index, lengths, inputs, short_filter)


def mixer_kernel(where_ref, lengths_ref, x_ref, taps_ref, base_ref, halo_ref, out_ref,
                 line, keep, band_mask, band, window):
    slots, count, width = x_ref.shape
    reach = base_ref.shape[1]
    rest = count - reach
    short = taps_ref.shape[1]
    groups = band.shape[0] // count
    share = LANES // groups
    ends = bounds_of(lengths_ref)
    anchor = where_ref[0] * count

    @pl.when(pl.program_id(0) == 0)
    def _():
        row = lax.broadcasted_iota(jnp.int32, (count, LANES), 0)
        lane = lax.broadcasted_iota(jnp.int32, (count, LANES), 1)
        place = anchor + row
        start = start_of(place, ends)
        for tap in range(short):
            keep[tap] = (place - tap >= start).astype(jnp.float32)
        under = jnp.where(row >= reach, row - reach, row)
        shift = jnp.where(row >= reach, reach, 0)
        source = anchor - reach + shift + lane
        older = (lane > under) & (source >= start)
        newer = (lane <= under) & (source + reach >= start)
        band_mask[:, 0:LANES] = older.astype(jnp.float32).astype(band_mask.dtype)
        band_mask[:, LANES:2 * LANES] = newer.astype(jnp.float32).astype(band_mask.dtype)
        window[reach + count:, :] = jnp.zeros((reach - rest, LANES), window.dtype)

    def one(i, carry):
        lanes = pl.ds(pl.multiple_of(i * LANES, LANES), LANES)
        mixed = []
        for slot in range(slots):
            before = halo_ref[reach + 16 * slot:reach + 16 * (slot + 1), lanes]
            line[slot, 0:8] = before.astype(jnp.float32)[8:]
            line[slot, 8:8 + count] = x_ref[slot, :, lanes].astype(jnp.float32)
            total = taps_ref[slot, 0:1, lanes].astype(jnp.float32) * line[slot, 8:8 + count]
            for tap in range(1, short):
                total = total + (
                    taps_ref[slot, tap:tap + 1, lanes].astype(jnp.float32)
                    * line[slot, 8 - tap:8 - tap + count]
                    * keep[tap]
                )
            mixed.append(total)
        window[0:reach, :] = halo_ref[0:reach, lanes]
        window[reach:reach + count, :] = (mixed[0] * mixed[2]).astype(window.dtype)
        for g in range(groups):
            taps = base_ref[pl.ds(i * groups + g, 1), :]
            circle = pltpu.roll(
                jnp.broadcast_to(taps, (reach, reach)), 0, 1, stride=1, stride_axis=0
            ).astype(band.dtype)
            for half in range(2):
                cols = slice(half * LANES, (half + 1) * LANES)
                band[g * reach:(g + 1) * reach, cols] = circle * band_mask[0:reach, cols]
                band[groups * reach + g * rest:groups * reach + (g + 1) * rest, cols] = (
                    circle[0:rest] * band_mask[reach:count, cols]
                )
        upper = jnp.dot(band[0:groups * reach, :], window[0:2 * reach, :],
                        preferred_element_type=jnp.float32)
        lower = jnp.dot(band[groups * reach:, :], window[reach:3 * reach, :],
                        preferred_element_type=jnp.float32)
        owner = lax.broadcasted_iota(jnp.int32, (1, LANES), 1) // share
        top, bottom = upper[0:reach], lower[0:rest]
        for g in range(1, groups):
            top = jnp.where(owner == g, upper[g * reach:(g + 1) * reach], top)
            bottom = jnp.where(owner == g, lower[g * rest:(g + 1) * rest], bottom)
        out_ref[0:reach, lanes] = (mixed[1][0:reach] * top).astype(out_ref.dtype)
        out_ref[reach:count, lanes] = (mixed[1][reach:count] * bottom).astype(out_ref.dtype)
        return carry

    lax.fori_loop(0, width // LANES, one, 0)


def mixer(index, lengths, inputs, short_filter, base, halo):
    slots, count, width = inputs.shape
    filters, reach = base.shape
    block = min(width, 512)
    short = short_filter.shape[1]
    groups = LANES * filters // width
    rows = halo.shape[0]
    return pl.pallas_call(
        mixer_kernel,
        out_shape=jax.ShapeDtypeStruct((count, width), inputs.dtype),
        grid_spec=pltpu.PrefetchScalarGridSpec(
            num_scalar_prefetch=2,
            grid=(width // block,),
            in_specs=[
                pl.BlockSpec((slots, count, block), lambda i, *_: (0, 0, i)),
                pl.BlockSpec((slots, short, block), lambda i, *_: (0, 0, i)),
                pl.BlockSpec((filters * block // width, reach), lambda i, *_: (i, 0)),
                pl.BlockSpec((rows, block), lambda i, *_: (0, i)),
            ],
            out_specs=pl.BlockSpec((count, block), lambda i, *_: (0, i)),
            scratch_shapes=[
                pltpu.VMEM((slots, 8 + count, LANES), jnp.float32),
                pltpu.VMEM((short, count, LANES), jnp.float32),
                pltpu.VMEM((count, 2 * LANES), inputs.dtype),
                pltpu.VMEM((groups * count, 2 * LANES), inputs.dtype),
                pltpu.VMEM((3 * reach, LANES), inputs.dtype),
            ],
        ),
        name="mixer",
    )(index, lengths, inputs, short_filter, base, halo)


def parts_of(value):
    high = value.astype(jnp.bfloat16)
    rest = value - high.astype(jnp.float32)
    middle = rest.astype(jnp.bfloat16)
    low = (rest - middle.astype(jnp.float32)).astype(jnp.bfloat16)
    return high, middle, low


def attend_kernel(where_ref, lengths_ref, own_ref, near_ref, far_ref, prior_ref,
                  out_ref, out_norm_ref, near_out_ref, far_out_ref,
                  bias, norms):
    count = own_ref.shape[1]
    depth = own_ref.shape[2]
    scale = 1.0 / math.sqrt(depth)
    step = pl.program_id(0)
    last = pl.num_programs(0) - 1
    index = where_ref[0]
    ends = bounds_of(lengths_ref)
    pivot = index == 1
    helps = (index == 1) | (index == 2)

    @pl.when(step == 0)
    def _():
        row = lax.broadcasted_iota(jnp.int32, (count, 2 * count), 0)
        col = lax.broadcasted_iota(jnp.int32, (count, 2 * count), 1)
        source = (index - 1) * count + col
        held = pivot | (col >= count)
        for which in range(3):
            place = (index + which) * count + row
            ok = (source <= place) & (source >= start_of(place, ends)) & held
            bias[which] = jnp.where(ok, 0.0, NEG)
        norms[...] = jnp.zeros(norms.shape, jnp.float32)

    def head(which, queries):
        keys = jnp.concatenate([prior_ref[0], own_ref[1]], axis=0)
        values = jnp.concatenate([prior_ref[1], own_ref[2]], axis=0)
        scores = lax.dot_general(queries, keys, (((1,), (1,)), ((), ())),
                                 preferred_element_type=jnp.float32)
        scores = scores * scale + bias[which]
        peak = jnp.maximum(jnp.max(scores, axis=1, keepdims=True), FLOOR)
        weights = jnp.exp(scores - peak)
        total = jnp.sum(weights, axis=1, keepdims=True)
        mixed = jnp.dot(weights.astype(jnp.bfloat16), values, preferred_element_type=jnp.float32)
        some = total > 0.0
        safe = jnp.where(some, total, 1.0)
        norm = jnp.where(some, peak + jnp.log(safe), NEG)
        lane = lax.broadcasted_iota(jnp.int32, (count, LANES), 1)
        norms[which] = jnp.where(lane == step, norm, norms[which])
        return mixed / safe

    @pl.when(step < last)
    def _():
        out_ref[...] = head(0, own_ref[0])

        @pl.when(helps)
        def _():
            near_out_ref[...] = head(1, near_ref[...]).astype(near_out_ref.dtype)

        @pl.when(pivot)
        def _():
            far_out_ref[...] = head(2, far_ref[...]).astype(far_out_ref.dtype)

    @pl.when(step == last)
    def _():
        out_norm_ref[...] = norms[0]
        for which, ref in ((1, near_out_ref), (2, far_out_ref)):
            high, middle, low = parts_of(norms[which])
            spread = LANES // 4
            total = high.astype(jnp.float32)
            total = total + pltpu.roll(middle.astype(jnp.float32), spread, 1)
            total = total + pltpu.roll(low.astype(jnp.float32), 2 * spread, 1)
            ref[...] = total.astype(ref.dtype)


def attend_part(index, lengths, blocks, near, far, prior, first):
    slots, count, _ = blocks.shape
    width = near.shape[1]
    heads = width // LANES
    clamp = lambda i: jnp.minimum(i, heads - 1)
    return pl.pallas_call(
        attend_kernel,
        out_shape=(
            jax.ShapeDtypeStruct((count, width), jnp.float32),
            jax.ShapeDtypeStruct((count, LANES), jnp.float32),
            jax.ShapeDtypeStruct((count, width + LANES), near.dtype),
            jax.ShapeDtypeStruct((count, width + LANES), near.dtype),
        ),
        grid_spec=pltpu.PrefetchScalarGridSpec(
            num_scalar_prefetch=2,
            grid=(heads + 1,),
            in_specs=[
                pl.BlockSpec((slots, count, LANES), lambda i, *_: (0, 0, first + clamp(i))),
                pl.BlockSpec((count, LANES), lambda i, *_: (0, clamp(i))),
                pl.BlockSpec((count, LANES), lambda i, *_: (0, clamp(i))),
                pl.BlockSpec((2, count, LANES), lambda i, *_: (0, 0, clamp(i))),
            ],
            out_specs=(
                pl.BlockSpec((count, LANES), lambda i, *_: (0, clamp(i))),
                pl.BlockSpec((count, LANES), lambda i, *_: (0, 0)),
                pl.BlockSpec((count, LANES), lambda i, *_: (0, i)),
                pl.BlockSpec((count, LANES), lambda i, *_: (0, i)),
            ),
            scratch_shapes=[
                pltpu.VMEM((3, count, 2 * count), jnp.float32),
                pltpu.VMEM((3, count, LANES), jnp.float32),
            ],
        ),
        name="attend_part",
    )(index, lengths, blocks, near, far, prior)


def merge_kernel(where_ref, own_ref, own_norm_ref, near_ref, far_ref, out_ref):
    count, width = own_ref.shape
    heads = width // LANES
    index = where_ref[0]
    spread = LANES // 4

    def norm_of(ref, used):
        packed = ref[:, width:width + LANES].astype(jnp.float32)
        total = packed + pltpu.roll(packed, LANES - spread, 1)
        total = total + pltpu.roll(packed, LANES - 2 * spread, 1)
        return jnp.where(used, total, NEG)

    @pl.when(index < 2)
    def _():
        out_ref[...] = own_ref[...].astype(out_ref.dtype)

    @pl.when(index >= 2)
    def _():
        own = own_norm_ref[...]
        near = norm_of(near_ref, index >= 2)
        far = norm_of(far_ref, index == 3)
        peak = jnp.maximum(own, jnp.maximum(near, far))
        own_part = jnp.exp(own - peak)
        near_part = jnp.exp(near - peak)
        far_part = jnp.exp(far - peak)
        whole = own_part + near_part + far_part
        own_part, near_part, far_part = own_part / whole, near_part / whole, far_part / whole
        for h in range(heads):
            lanes = slice(h * LANES, (h + 1) * LANES)
            mixed = own_ref[:, lanes] * own_part[:, h:h + 1]
            mixed = mixed + near_ref[:, lanes].astype(jnp.float32) * near_part[:, h:h + 1]
            mixed = mixed + jnp.where(
                index == 3, far_ref[:, lanes].astype(jnp.float32) * far_part[:, h:h + 1], 0.0
            )
            out_ref[:, lanes] = mixed.astype(out_ref.dtype)


def merge_part(index, own, own_norm, near, far):
    count, width = own.shape
    return pl.pallas_call(
        merge_kernel,
        out_shape=jax.ShapeDtypeStruct((count, width), near.dtype),
        grid_spec=pltpu.PrefetchScalarGridSpec(
            num_scalar_prefetch=1,
            grid=(1,),
            in_specs=[
                pl.BlockSpec((count, width), lambda i, *_: (0, 0)),
                pl.BlockSpec((count, LANES), lambda i, *_: (0, 0)),
                pl.BlockSpec((count, width + LANES), lambda i, *_: (0, 0)),
                pl.BlockSpec((count, width + LANES), lambda i, *_: (0, 0)),
            ],
            out_specs=pl.BlockSpec((count, width), lambda i, *_: (0, 0)),
        ),
        name="merge_part",
    )(index, own, own_norm, near, far)


def attend_four(index, lengths, blocks):
    slots, count, width = blocks.shape
    part = width // CHUNKS
    outs = []
    for c in range(CHUNKS):
        cols = slice(c * part, (c + 1) * part)
        prior = lax.ppermute(blocks[1:3, :, cols], "ctx", [(0, 1)])
        near = lax.ppermute(blocks[0, :, cols], "ctx", [(2, 1), (3, 2)])
        far = lax.ppermute(blocks[0, :, cols], "ctx", [(3, 1)])
        own, own_norm, near_out, far_out = attend_part(
            index, lengths, blocks, near, far, prior, c * part // LANES
        )
        near_in = lax.ppermute(near_out, "ctx", [(1, 2), (2, 3)])
        far_in = lax.ppermute(far_out, "ctx", [(1, 3)])
        outs.append(merge_part(index, own, own_norm, near_in, far_in))
    return jnp.concatenate(outs, axis=1)


def attend_any(lengths, blocks, heads):
    count, width = blocks.shape[1:]
    depth = width // heads
    bounds = jnp.cumsum(lengths[0])[:-1]
    gathered = lax.all_gather(blocks[1:3], "ctx", axis=1, tiled=True)
    extent = gathered.shape[1]
    place = lax.axis_index("ctx") * count + jnp.arange(count, dtype=jnp.int32)
    source = jnp.arange(extent, dtype=jnp.int32)
    start = jnp.max(jnp.where(place[:, None] >= bounds[None, :], bounds[None, :], 0), axis=1)
    admit = (source[None, :] <= place[:, None]) & (source[None, :] >= start[:, None])
    queries = blocks[0].reshape(count, heads, depth)
    keys = gathered[0].reshape(extent, heads, depth)
    values = gathered[1].reshape(extent, heads, depth)
    scores = jnp.einsum("thd,shd->hts", queries, keys, preferred_element_type=jnp.float32)
    scores = jnp.where(admit[None], scores * (1.0 / math.sqrt(depth)), NEG)
    peak = jnp.max(scores, axis=2, keepdims=True)
    weights = jnp.where(admit[None], jnp.exp(scores - peak), 0.0)
    total = jnp.sum(weights, axis=2)
    mixed = jnp.einsum("hts,shd->htd", weights.astype(jnp.bfloat16), values,
                       preferred_element_type=jnp.float32)
    mixed = mixed / total[:, :, None]
    return mixed.transpose(1, 0, 2).reshape(count, width).astype(jnp.bfloat16)


def on_device(hyena_in, short_filter, long_filter, qkv, lengths):
    size = lax.axis_size("ctx")
    index = lax.axis_index("ctx").astype(jnp.int32).reshape(1)
    inputs = hyena_in[0].transpose(1, 0, 2)
    blocks = qkv[0].transpose(1, 0, 2)
    reach = long_filter.shape[0]
    taps = long_filter.astype(jnp.float32).T
    base = jnp.concatenate([taps[:, :1], taps[:, :0:-1]], axis=1)
    tail = mixer_tail(index, lengths, inputs, short_filter, reach)
    halo = lax.ppermute(tail, "ctx", [(i, i + 1) for i in range(size - 1)])
    hyena_out = mixer(index, lengths, inputs, short_filter, base, halo)
    heads = H // lax.axis_size("tp")
    if size == 4:
        attn_out = attend_four(index, lengths, blocks)
    else:
        attn_out = attend_any(lengths, blocks, heads)
    return (hyena_out[None], attn_out[None])


def solution(mesh):
    in_specs = (
        P(("groups", "dp"), "ctx", None, "tp"),
        P(None, None, "tp"),
        P(None, "tp"),
        P(("groups", "dp"), "ctx", None, "tp"),
        P(("groups", "dp"), None),
    )
    out_specs = (P(("groups", "dp"), "ctx", "tp"), P(("groups", "dp"), "ctx", "tp"))
    return jax.shard_map(
        on_device, mesh=mesh, in_specs=in_specs, out_specs=out_specs, check_vma=False
    )
```

profile of v0, /device:TPU:16, one launch (start us, length us, event | category | flops | bytes accessed | tf_op | source)
XLA Modules:
  0.0 125.9 jit_solution(2043127616212137291)
XLA Ops:
  0.6 2.9 %fusion = (bf16[2,144,2048]{2,1,0:T(8,128)(2,1)}, bf16[2,144,2048]{2,1,0:T(8,128)(2,1)S(1)}) fusion(bf16[3,144,4096]{2,1,0:T(8,128)(2,1)} %bitcast.17), kind=kLoop, calls=%fused_computation.5 | loop fusion | bytes 4718592 | tf_op jit(solution)/shard_map/slice | solution.py:376
  3.5 1.7 %collective-permute-start.3 = (bf16[2,144,2048]{2,1,0:T(8,128)(2,1)}, bf16[2,144,2048]{2,1,0:T(8,128)(2,1)}, u32[]{:S(2)}, u32[]{:S(2)}) collective-permute-start(bf16[2,144,2048]{2,1,0:T(8,128)(2,1)} %get-tuple-element.18), channel_id=1, source_target_pairs={{0,4},{1,5},{2,6},{3,7},{16,20},{17,21},{18,22},{19,23}} | collective-permute-start | bytes 3538952 | tf_op jit(solution)/shard_map/ppermute | solution.py:376
  5.2 2.4 %slice_bitcast_fusion.1 = (bf16[144,2048]{1,0:T(8,128)(2,1)}, bf16[144,2048]{1,0:T(8,128)(2,1)}) fusion(bf16[3,144,4096]{2,1,0:T(8,128)(2,1)} %bitcast.18), kind=kLoop, calls=%fused_computation.2 | loop fusion | bytes 2359296 | tf_op jit(solution)/shard_map/squeeze | solution.py:377
  7.6 2.0 %collective-permute-start.1 = (bf16[144,2048]{1,0:T(8,128)(2,1)}, bf16[144,2048]{1,0:T(8,128)(2,1)S(1)}, u32[]{:S(2)}, u32[]{:S(2)}) collective-permute-start(bf16[144,2048]{1,0:T(8,128)(2,1)} %get-tuple-element.20), channel_id=1, source_target_pairs={{8,4},{12,8},{9,5},{13,9},{10,6},{14,10},{11,7},{15,11},{24,20},{2... | collective-permute-start | bytes 1769480 | tf_op jit(solution)/shard_map/ppermute | solution.py:377
  9.5 1.5 %collective-permute-start.2 = (bf16[144,2048]{1,0:T(8,128)(2,1)}, bf16[144,2048]{1,0:T(8,128)(2,1)}, u32[]{:S(2)}, u32[]{:S(2)}) collective-permute-start(bf16[144,2048]{1,0:T(8,128)(2,1)} %get-tuple-element.20), channel_id=1, source_target_pairs={{12,4},{13,5},{14,6},{15,7},{28,20},{29,21},{30,22},{31,23}} | collective-permute-start | bytes 1769480 | tf_op jit(solution)/shard_map/ppermute | solution.py:378
  11.0 1.7 %collective-permute-start.8 = (bf16[2,144,2048]{2,1,0:T(8,128)(2,1)S(1)}, bf16[2,144,2048]{2,1,0:T(8,128)(2,1)}, u32[]{:S(2)}, u32[]{:S(2)}) collective-permute-start(bf16[2,144,2048]{2,1,0:T(8,128)(2,1)S(1)} %get-tuple-element.19), channel_id=1, source_target_pairs={{0,4},{1,5},{2,6},{3,7},{16,20},{17,21},{18,22},{19,23}} | collective-permute-start | bytes 3538952 | tf_op jit(solution)/shard_map/ppermute | solution.py:376
  12.7 9.1 %mixer_tail.1 = bf16[176,4096]{1,0:T(8,128)(2,1)} custom-call(s32[1]{0:T(128)} %bitcast.where_ref, s32[1,4]{1,0:T(1,128)} %lengths_ref.7, bf16[3,144,4096]{2,1,0:T(8,128)(2,1)} %bitcast.21, bf16[3,7,4096]{2,1,0:T(8,128)(2,1)} %taps_ref.3), custom_call_target="tpu_custom_call" | custom-call | tf_op jit(solution)/shard_map/mixer_tail/pallas_call | solution.py:78
  21.7 4.5 %collective-permute-start = (bf16[176,4096]{1,0:T(8,128)(2,1)}, bf16[176,4096]{1,0:T(8,128)(2,1)S(1)}, u32[]{:S(2)}, u32[]{:S(2)}) collective-permute-start(bf16[176,4096]{1,0:T(8,128)(2,1)} %mixer_tail.1), channel_id=1, source_target_pairs={{0,4},{4,8},{8,12},{1,5},{5,9},{9,13},{2,6},{6,10},{10,14},{3,7},{... | collective-permute-start | bytes 4325384 | tf_op jit(solution)/shard_map/ppermute | solution.py:421
  26.3 1.9 %collective-permute-start.6 = (bf16[144,2048]{1,0:T(8,128)(2,1)}, bf16[144,2048]{1,0:T(8,128)(2,1)}, u32[]{:S(2)}, u32[]{:S(2)}) collective-permute-start(bf16[144,2048]{1,0:T(8,128)(2,1)} %get-tuple-element.21), channel_id=1, source_target_pairs={{8,4},{12,8},{9,5},{13,9},{10,6},{14,10},{11,7},{15,11},{24,20},{2... | collective-permute-start | bytes 1769480 | tf_op jit(solution)/shard_map/ppermute | solution.py:377
  28.2 1.5 %collective-permute-start.7 = (bf16[144,2048]{1,0:T(8,128)(2,1)}, bf16[144,2048]{1,0:T(8,128)(2,1)}, u32[]{:S(2)}, u32[]{:S(2)}) collective-permute-start(bf16[144,2048]{1,0:T(8,128)(2,1)} %get-tuple-element.21), channel_id=1, source_target_pairs={{12,4},{13,5},{14,6},{15,7},{28,20},{29,21},{30,22},{31,23}} | collective-permute-start | bytes 1769480 | tf_op jit(solution)/shard_map/ppermute | solution.py:378
  29.8 17.9 %attend_part.2 = (f32[144,2048]{1,0:T(8,128)}, f32[144,128]{1,0:T(8,128)}, bf16[144,2176]{1,0:T(8,128)(2,1)}, bf16[144,2176]{1,0:T(8,128)(2,1)}) custom-call(s32[1]{0:T(128)} %bitcast.where_ref, s32[1,4]{1,0:T(1,128)} %lengths_ref.7, bf16[3,144,4096]{2,1,0:T(8,128)(2,1)} %bitcast.19, bf16[144,2048]{1,0:T(8,128)(2,1)} %copy-done.4, ...), custom_call_target="tpu_custom_call" | custom-call | tf_op jit(solution)/shard_map/attend_part/pallas_call | solution.py:281
  47.7 12.9 %collective-permute-start.4 = (bf16[144,2176]{1,0:T(8,128)(2,1)}, bf16[144,2176]{1,0:T(8,128)(2,1)S(1)}, u32[]{:S(2)}, u32[]{:S(2)}) collective-permute-start(bf16[144,2176]{1,0:T(8,128)(2,1)} %get-tuple-element.12), channel_id=1, source_target_pairs={{4,8},{8,12},{5,9},{9,13},{6,10},{10,14},{7,11},{11,15},{20,24},{2... | collective-permute-start | bytes 1880072 | tf_op jit(solution)/shard_map/ppermute | solution.py:382
  60.7 1.6 %collective-permute-start.5 = (bf16[144,2176]{1,0:T(8,128)(2,1)}, bf16[144,2176]{1,0:T(8,128)(2,1)}, u32[]{:S(2)}, u32[]{:S(2)}) collective-permute-start(bf16[144,2176]{1,0:T(8,128)(2,1)} %get-tuple-element.13), channel_id=1, source_target_pairs={{4,12},{5,13},{6,14},{7,15},{20,28},{21,29},{22,30},{23,31}} | collective-permute-start | bytes 1880072 | tf_op jit(solution)/shard_map/ppermute | solution.py:383
  62.3 17.9 %attend_part.3 = (f32[144,2048]{1,0:T(8,128)}, f32[144,128]{1,0:T(8,128)}, bf16[144,2176]{1,0:T(8,128)(2,1)}, bf16[144,2176]{1,0:T(8,128)(2,1)}) custom-call(s32[1]{0:T(128)} %bitcast.where_ref, s32[1,4]{1,0:T(1,128)} %lengths_ref.7, bf16[3,144,4096]{2,1,0:T(8,128)(2,1)} %bitcast.20, bf16[144,2048]{1,0:T(8,128)(2,1)} %collective-permute-done.6.near_ref, ...), custom_call_target="tpu_custom_call" | custom-call | tf_op jit(solution)/shard_map/attend_part/pallas_call | solution.py:281
  80.2 0.7 collective-permute-start.10
  80.9 1.9 %collective-permute-start.9 = (bf16[144,2176]{1,0:T(8,128)(2,1)}, bf16[144,2176]{1,0:T(8,128)(2,1)}, u32[]{:S(2)}, u32[]{:S(2)}) collective-permute-start(bf16[144,2176]{1,0:T(8,128)(2,1)} %get-tuple-element.16), channel_id=1, source_target_pairs={{4,8},{8,12},{5,9},{9,13},{6,10},{10,14},{7,11},{11,15},{20,24},{2... | collective-permute-start | bytes 1880072 | tf_op jit(solution)/shard_map/ppermute | solution.py:382
  83.3 0.8 pad_maximum_fusion.base_ref
  84.0 1.1 copy-done.1
  85.1 17.4 %mixer.1 = bf16[144,4096]{1,0:T(8,128)(2,1)} custom-call(s32[1]{0:T(128)} %bitcast.where_ref, s32[1,4]{1,0:T(1,128)} %lengths_ref.7, bf16[3,144,4096]{2,1,0:T(8,128)(2,1)} %bitcast.22, bf16[3,7,4096]{2,1,0:T(8,128)(2,1)} %taps_ref.3, f32[256,128]{1,0:T(8,128)} %pad_maximum_fusion.base_ref, bf16[176,4096]{1,0:T(8,128)(2,1)} %copy-done.1), custom_call_target="tpu_custom_call" | custom-call | tf_op jit(solution)/shard_map/mixer/pallas_call | solution.py:177
  102.6 0.8 copy-done.2
  103.4 3.7 %merge_part.2 = bf16[144,2048]{1,0:T(8,128)(2,1)} custom-call(s32[1]{0:T(128)} %bitcast.where_ref, f32[144,2048]{1,0:T(8,128)} %get-tuple-element.10.own_ref, f32[144,128]{1,0:T(8,128)} %get-tuple-element.11.own_norm_ref, bf16[144,2176]{1,0:T(8,128)(2,1)} %copy-done.2, bf16[144,2176]{1,0:T(8,128)(2,1)} %collective-permute-done.5.far_ref), custom_call_target="tpu_custom_call" | custom-call | tf_op jit(solution)/shard_map/merge_part/pallas_call | solution.py:352
  107.1 13.0 %collective-permute-done.9.near_ref = bf16[144,2176]{1,0:T(8,128)(2,1)} collective-permute-done((bf16[144,2176]{1,0:T(8,128)(2,1)}, bf16[144,2176]{1,0:T(8,128)(2,1)}, u32[]{:S(2)}, u32[]{:S(2)}) %collective-permute-start.9) | collective-permute-done | bytes 626720 | tf_op jit(solution)/shard_map/ppermute | solution.py:382
  120.1 3.7 %merge_part.3 = bf16[144,2048]{1,0:T(8,128)(2,1)} custom-call(s32[1]{0:T(128)} %bitcast.where_ref, f32[144,2048]{1,0:T(8,128)} %get-tuple-element.14.own_ref, f32[144,128]{1,0:T(8,128)} %get-tuple-element.15.own_norm_ref, bf16[144,2176]{1,0:T(8,128)(2,1)} %collective-permute-done.9.near_ref, bf16[144,2176]{1,0:T(8,128)(2,1)} %copy-done.3), custom_call_target="tpu_custom_call" | custom-call | tf_op jit(solution)/shard_map/merge_part/pallas_call | solution.py:352
  123.8 2.2 %maximum_bitcast_fusion = bf16[1,144,4096]{2,1,0:T(8,128)(2,1)} fusion(bf16[144,2048]{1,0:T(8,128)(2,1)} %merge_part.3, bf16[144,2048]{1,0:T(8,128)(2,1)S(1)} %copy-done), kind=kLoop, calls=%fused_computation | loop fusion | flops 2359296 | bytes 2359296 | tf_op jit(solution)/shard_map/broadcast_in_dim | solution.py:428
  (24 shorter events, 0.4 us)
Async XLA Ops:
  3.5 26.3 %collective-permute-start.3 = (bf16[2,144,2048]{2,1,0:T(8,128)(2,1)}, bf16[2,144,2048]{2,1,0:T(8,128)(2,1)}, u32[]{:S(2)}, u32[]{:S(2)}) collective-permute-start(bf16[2,144,2048]{2,1,0:T(8,128)(2,1)} %get-tuple-element.18), channel_id=1, source_target_pairs={{0,4},{1,5},{2,6},{3,7},{16,20},{17,21},{18,22},{19,23}} | collective-permute-start | bytes 3538952 | tf_op jit(solution)/shard_map/ppermute | solution.py:376
  7.6 18.7 %collective-permute-start.1 = (bf16[144,2048]{1,0:T(8,128)(2,1)}, bf16[144,2048]{1,0:T(8,128)(2,1)S(1)}, u32[]{:S(2)}, u32[]{:S(2)}) collective-permute-start(bf16[144,2048]{1,0:T(8,128)(2,1)} %get-tuple-element.20), channel_id=1, source_target_pairs={{8,4},{12,8},{9,5},{13,9},{10,6},{14,10},{11,7},{15,11},{24,20},{2... | collective-permute-start | bytes 1769480 | tf_op jit(solution)/shard_map/ppermute | solution.py:377
  9.5 18.7 %collective-permute-start.2 = (bf16[144,2048]{1,0:T(8,128)(2,1)}, bf16[144,2048]{1,0:T(8,128)(2,1)}, u32[]{:S(2)}, u32[]{:S(2)}) collective-permute-start(bf16[144,2048]{1,0:T(8,128)(2,1)} %get-tuple-element.20), channel_id=1, source_target_pairs={{12,4},{13,5},{14,6},{15,7},{28,20},{29,21},{30,22},{31,23}} | collective-permute-start | bytes 1769480 | tf_op jit(solution)/shard_map/ppermute | solution.py:378
  11.0 51.3 %collective-permute-start.8 = (bf16[2,144,2048]{2,1,0:T(8,128)(2,1)S(1)}, bf16[2,144,2048]{2,1,0:T(8,128)(2,1)}, u32[]{:S(2)}, u32[]{:S(2)}) collective-permute-start(bf16[2,144,2048]{2,1,0:T(8,128)(2,1)S(1)} %get-tuple-element.19), channel_id=1, source_target_pairs={{0,4},{1,5},{2,6},{3,7},{16,20},{17,21},{18,22},{19,23}} | collective-permute-start | bytes 3538952 | tf_op jit(solution)/shard_map/ppermute | solution.py:376
  21.7 62.3 %collective-permute-start = (bf16[176,4096]{1,0:T(8,128)(2,1)}, bf16[176,4096]{1,0:T(8,128)(2,1)S(1)}, u32[]{:S(2)}, u32[]{:S(2)}) collective-permute-start(bf16[176,4096]{1,0:T(8,128)(2,1)} %mixer_tail.1), channel_id=1, source_target_pairs={{0,4},{4,8},{8,12},{1,5},{5,9},{9,13},{2,6},{6,10},{10,14},{3,7},{... | collective-permute-start | bytes 4325384 | tf_op jit(solution)/shard_map/ppermute | solution.py:421
  26.3 3.5 %copy-start.4 = (bf16[144,2048]{1,0:T(8,128)(2,1)}, bf16[144,2048]{1,0:T(8,128)(2,1)S(1)}, u32[]{:S(2)}) copy-start(bf16[144,2048]{1,0:T(8,128)(2,1)S(1)} %collective-permute-done.1.near_ref) | copy-start | bytes 1769476
  26.3 34.4 %collective-permute-start.6 = (bf16[144,2048]{1,0:T(8,128)(2,1)}, bf16[144,2048]{1,0:T(8,128)(2,1)}, u32[]{:S(2)}, u32[]{:S(2)}) collective-permute-start(bf16[144,2048]{1,0:T(8,128)(2,1)} %get-tuple-element.21), channel_id=1, source_target_pairs={{8,4},{12,8},{9,5},{13,9},{10,6},{14,10},{11,7},{15,11},{24,20},{2... | collective-permute-start | bytes 1769480 | tf_op jit(solution)/shard_map/ppermute | solution.py:377
  28.2 34.1 %collective-permute-start.7 = (bf16[144,2048]{1,0:T(8,128)(2,1)}, bf16[144,2048]{1,0:T(8,128)(2,1)}, u32[]{:S(2)}, u32[]{:S(2)}) collective-permute-start(bf16[144,2048]{1,0:T(8,128)(2,1)} %get-tuple-element.21), channel_id=1, source_target_pairs={{12,4},{13,5},{14,6},{15,7},{28,20},{29,21},{30,22},{31,23}} | collective-permute-start | bytes 1769480 | tf_op jit(solution)/shard_map/ppermute | solution.py:378
  47.7 54.9 %collective-permute-start.4 = (bf16[144,2176]{1,0:T(8,128)(2,1)}, bf16[144,2176]{1,0:T(8,128)(2,1)S(1)}, u32[]{:S(2)}, u32[]{:S(2)}) collective-permute-start(bf16[144,2176]{1,0:T(8,128)(2,1)} %get-tuple-element.12), channel_id=1, source_target_pairs={{4,8},{8,12},{5,9},{9,13},{6,10},{10,14},{7,11},{11,15},{20,24},{2... | collective-permute-start | bytes 1880072 | tf_op jit(solution)/shard_map/ppermute | solution.py:382
  60.7 22.2 %copy-start.5 = (bf16[128,256]{1,0:T(8,128)(2,1)S(1)}, bf16[128,256]{1,0:T(8,128)(2,1)}, u32[]{:S(2)}) copy-start(bf16[128,256]{1,0:T(8,128)(2,1)} %param.7) | copy-start | bytes 196612
  60.7 41.9 %collective-permute-start.5 = (bf16[144,2176]{1,0:T(8,128)(2,1)}, bf16[144,2176]{1,0:T(8,128)(2,1)}, u32[]{:S(2)}, u32[]{:S(2)}) collective-permute-start(bf16[144,2176]{1,0:T(8,128)(2,1)} %get-tuple-element.13), channel_id=1, source_target_pairs={{4,12},{5,13},{6,14},{7,15},{20,28},{21,29},{22,30},{23,31}} | collective-permute-start | bytes 1880072 | tf_op jit(solution)/shard_map/ppermute | solution.py:383
  80.2 26.9 %collective-permute-start.10 = (bf16[144,2176]{1,0:T(8,128)(2,1)}, bf16[144,2176]{1,0:T(8,128)(2,1)S(1)}, u32[]{:S(2)}, u32[]{:S(2)}) collective-permute-start(bf16[144,2176]{1,0:T(8,128)(2,1)} %get-tuple-element.17), channel_id=1, source_target_pairs={{4,12},{5,13},{6,14},{7,15},{20,28},{21,29},{22,30},{23,31}} | collective-permute-start | bytes 1880072 | tf_op jit(solution)/shard_map/ppermute | solution.py:383
  80.9 39.2 %collective-permute-start.9 = (bf16[144,2176]{1,0:T(8,128)(2,1)}, bf16[144,2176]{1,0:T(8,128)(2,1)}, u32[]{:S(2)}, u32[]{:S(2)}) collective-permute-start(bf16[144,2176]{1,0:T(8,128)(2,1)} %get-tuple-element.16), channel_id=1, source_target_pairs={{4,8},{8,12},{5,9},{9,13},{6,10},{10,14},{7,11},{11,15},{20,24},{2... | collective-permute-start | bytes 1880072 | tf_op jit(solution)/shard_map/ppermute | solution.py:382
  84.0 1.1 copy-start.1
  102.6 0.8 copy-start.2
  107.1 13.0 %copy-start.3 = (bf16[144,2176]{1,0:T(8,128)(2,1)}, bf16[144,2176]{1,0:T(8,128)(2,1)S(1)}, u32[]{:S(2)}) copy-start(bf16[144,2176]{1,0:T(8,128)(2,1)S(1)} %collective-permute-done.10.far_ref) | copy-start | bytes 1880068
  120.1 3.7 %copy-start = (bf16[144,2048]{1,0:T(8,128)(2,1)S(1)}, bf16[144,2048]{1,0:T(8,128)(2,1)}, u32[]{:S(2)}) copy-start(bf16[144,2048]{1,0:T(8,128)(2,1)} %merge_part.2) | copy-start | bytes 1769476
where the time goes:
time: 128 us; the launch traced here: 126 us
  Pallas kernels  69.6 us (54%)
  starting transfers between devices  31.9 us (25%)
  waiting for transfers between devices  13 us (10%)
  local copies, waits for them, and re-layouts  7.6 us (6%)
  other arithmetic  2.95 us (2%)
    pallas_call x2, Pallas kernels, attend_part(): pl.pallas_call(attend_kernel, out_shape=(jax.ShapeDtypeStruct((count, wid...  35.8 us
    pallas_call x1, Pallas kernels, mixer(): pl.pallas_call(mixer_kernel, out_shape=jax.ShapeDtypeStruct((count, width...  17.4 us
    ppermute x2, starting transfers between devices, attend_four(): near_in = lax.ppermute(near_out, 'ctx', [(1, 2), (2, 3)])  14.8 us
    ppermute x2, waiting for transfers between devices, attend_four(): near_in = lax.ppermute(near_out, 'ctx', [(1, 2), (2, 3)])  13 us
    pallas_call x1, Pallas kernels, mixer_tail(): pl.pallas_call(tail_kernel, out_shape=jax.ShapeDtypeStruct((rows, width),...  9.06 us
    pallas_call x2, Pallas kernels, merge_part(): pl.pallas_call(merge_kernel, out_shape=jax.ShapeDtypeStruct((count, width...  7.34 us
    ppermute x1, starting transfers between devices, on_device(): halo = lax.ppermute(tail, 'ctx', [(i, i + 1) for i in range(size - 1)])  4.52 us
    ppermute x2, starting transfers between devices, attend_four(): near = lax.ppermute(blocks[0, :, cols], 'ctx', [(2, 1), (3, 2)])  3.88 us
  transfers between devices with their start and end apart: 11, of which 1 were waited for; matrix products, arithmetic and copies ran while one was open for 3% of the time, Pallas kernels for 52%

commit v1 on v0

v1 whole, which is shorter than its diff:
```python
from functools import partial
import math

import jax
import jax.numpy as jnp
from jax import lax
from jax.experimental import pallas as pl
from jax.experimental.pallas import tpu as pltpu
from jax.sharding import PartitionSpec as P

H = 64
LANES = 128
ROWS = 32
TAIL_BLOCK = 1024
MIX_BLOCK = 512
HEADS_AT_ONCE = 4
CHUNKS = 2
SPREAD = LANES // 6
NEG = -1e30
FLOOR = -1e29


def bounds_of(lengths_ref):
    ends, total = [], 0
    for i in range(lengths_ref.shape[1] - 1):
        total = total + lengths_ref[0, i]
        ends.append(total)
    return ends


def start_of(places, ends):
    start = jnp.zeros(places.shape, jnp.int32)
    for end in ends:
        start = jnp.where(places >= end, end, start)
    return start


def filtered(line, offset, taps, keep, first, rows):
    outs = []
    for part in range(line.shape[0]):
        lanes = slice(part * LANES, (part + 1) * LANES)
        total = taps[0:1, lanes] * line[part, offset + first:offset + first + rows]
        for tap in range(1, keep.shape[0]):
            at = offset + first - tap
            total = total + taps[tap:tap + 1, lanes] * (
                line[part, at:at + rows] * keep[tap, first:first + rows]
            )
        outs.append(total)
    return jnp.concatenate(outs, axis=1)


def keep_taps(keep, anchor, ends):
    short, count, _ = keep.shape
    place = anchor + lax.broadcasted_iota(jnp.int32, (count, LANES), 0)
    start = start_of(place, ends)
    for tap in range(short):
        keep[tap] = (place - tap >= start).astype(jnp.float32)


def tail_kernel(where_ref, lengths_ref, gate_ref, value_ref, last_ref, taps_ref, *refs):
    *refs, line, keep, taps = refs
    extra = len(refs) // 2
    slab_refs, out_ref, message_refs = refs[:extra], refs[extra], refs[extra + 1:]
    count, width = gate_ref.shape
    reach = out_ref.shape[0] - 32
    first = count - reach
    short = taps_ref.shape[1]
    parts = line.shape[1]
    wide = parts * LANES

    @pl.when(pl.program_id(0) == 0)
    def _():
        keep_taps(keep, where_ref[0] * count, bounds_of(lengths_ref))

    taps[:, 0:short] = taps_ref[...].astype(jnp.float32)
    ends = [ref[ref.shape[0] - 16:].astype(jnp.float32)[8:] for ref in (gate_ref, last_ref, value_ref)]
    ends = jnp.concatenate(ends + [jnp.zeros((8, width), jnp.float32)], axis=0)
    out_ref[reach:reach + 32] = ends.astype(out_ref.dtype)

    def one(i, carry):
        lanes = pl.ds(pl.multiple_of(i * wide, LANES), wide)
        for which, ref in enumerate((gate_ref, value_ref)):
            for part in range(parts):
                here = pl.ds(pl.multiple_of(i * wide + part * LANES, LANES), LANES)
                line[which, part] = ref[:, here].astype(jnp.float32)
        for at in range(first, count, ROWS):
            gate = filtered(line.at[0], 0, taps[0, :, lanes], keep, at, ROWS)
            value = filtered(line.at[1], 0, taps[2, :, lanes], keep, at, ROWS)
            out_ref[at - first:at - first + ROWS, lanes] = (gate * value).astype(out_ref.dtype)
        return carry

    lax.fori_loop(0, width // wide, one, 0)

    for slab_ref, message_ref in zip(slab_refs, message_refs):
        @pl.when(where_ref[0] == 0)
        def _():
            message_ref[0:count] = slab_ref[...]
            message_ref[count:] = jnp.zeros((reach + 32 - count, width), message_ref.dtype)

        @pl.when(where_ref[0] != 0)
        def _():
            message_ref[...] = out_ref[...]


def mixer_tail(index, lengths, inputs, short_filter, reach, first, cols, blocks=None, slab=0):
    slots, count, _ = inputs.shape
    block = min(cols, 1024)
    short = short_filter.shape[1]
    rows = reach + 32
    start = first // block
    out = jax.ShapeDtypeStruct((rows, cols), inputs.dtype)
    out_spec = pl.BlockSpec((rows, block), lambda i, *_: (0, i))
    extra = () if blocks is None else (blocks,)
    return pl.pallas_call(
        tail_kernel,
        out_shape=(out,) * (1 + len(extra)),
        grid_spec=pltpu.PrefetchScalarGridSpec(
            num_scalar_prefetch=2,
            grid=(cols // block,),
            in_specs=[
                pl.BlockSpec((None, count, block), lambda i, *_: (0, 0, start + i)),
                pl.BlockSpec((None, count, block), lambda i, *_: (2, 0, start + i)),
                pl.BlockSpec((None, 16, block), lambda i, *_: (1, count // 16 - 1, start + i)),
                pl.BlockSpec((slots, short, block), lambda i, *_: (0, 0, start + i)),
            ]
            + [pl.BlockSpec((None, count, block), lambda i, *_: (1 + i, 0, slab))] * len(extra),
            out_specs=(out_spec,) * (1 + len(extra)),
            scratch_shapes=[
                pltpu.VMEM((2, 2, count, LANES), jnp.float32),
                pltpu.VMEM((short, count, LANES), jnp.float32),
                pltpu.VMEM((slots, 8, block), jnp.float32),
            ],
        ),
        name="mixer_tail",
    )(index, lengths, inputs, inputs, inputs, short_filter, *extra)


def mixer_kernel(where_ref, lengths_ref, x1_ref, x2_ref, v_ref, taps_ref, base_ref, tail_ref, *refs):
    *halo_refs, out_ref, line, keep, taps, band_mask, band, window, gate = refs
    halo_refs = [ref for ref in halo_refs if ref.shape == tail_ref.shape]
    slots = taps_ref.shape[0]
    count, width = x2_ref.shape
    reach = base_ref.shape[1]
    rest = count - reach
    short = taps_ref.shape[1]
    parts = line.shape[1]
    wide = parts * LANES
    groups = band.shape[1] // count
    share = LANES // groups
    ends = bounds_of(lengths_ref)
    anchor = where_ref[0] * count

    @pl.when(pl.program_id(0) == 0)
    def _():
        keep_taps(keep, anchor, ends)
        row = lax.broadcasted_iota(jnp.int32, (count, LANES), 0)
        lane = lax.broadcasted_iota(jnp.int32, (count, LANES), 1)
        start = start_of(anchor + row, ends)
        under = jnp.where(row >= reach, row - reach, row)
        shift = jnp.where(row >= reach, reach, 0)
        source = anchor - reach + shift + lane
        older = (lane > under) & (source >= start)
        newer = (lane <= under) & (source + reach >= start)
        band_mask[:, 0:LANES] = older.astype(jnp.float32).astype(band_mask.dtype)
        band_mask[:, LANES:2 * LANES] = newer.astype(jnp.float32).astype(band_mask.dtype)
        window[reach + count:, :] = jnp.zeros((reach - rest, wide), window.dtype)

    taps[:, 0:short] = taps_ref[...].astype(jnp.float32)
    owner = lax.broadcasted_iota(jnp.int32, (1, LANES), 1) // share

    def halo(rows, lanes):
        total = halo_refs[0][rows, lanes]
        for ref in halo_refs[1:]:
            total = jnp.where(where_ref[0] == 1, ref[rows, lanes], total)
        return total

    def one(i, carry):
        lanes = pl.ds(pl.multiple_of(i * wide, LANES), wide)
        for part in range(parts):
            here = pl.ds(pl.multiple_of(i * wide + part * LANES, LANES), LANES)
            for slot, ref in enumerate((x1_ref, x2_ref, v_ref)):
                line[slot, part, 8:16] = halo(slice(reach, reach + 32), here).astype(jnp.float32)[
                    8 * slot:8 * slot + 8
                ]
                line[slot, part, 16:16 + ref.shape[0]] = ref[:, here].astype(jnp.float32)
        first = [filtered(line.at[slot], 16, taps[slot, :, lanes], keep, 0, rest) for slot in (0, 2)]
        window[0:reach] = halo(slice(0, reach), lanes)
        window[reach:reach + rest] = (first[0] * first[1]).astype(window.dtype)
        window[reach + rest:reach + count] = tail_ref[0:reach, lanes]
        for at in range(0, count, 48):
            gate[at:at + 48] = filtered(line.at[1], 16, taps[1, :, lanes], keep, at, 48)
        for part in range(wide // LANES):
            held = band.at[part]
            for g in range(groups):
                row = base_ref[pl.ds((i * (wide // LANES) + part) * groups + g, 1), :]
                circle = pltpu.roll(
                    jnp.broadcast_to(row, (reach, reach)), 0, 1, stride=1, stride_axis=0
                ).astype(band.dtype)
                for half in range(2):
                    cols = slice(half * LANES, (half + 1) * LANES)
                    held[g * reach:(g + 1) * reach, cols] = circle * band_mask[0:reach, cols]
                    held[groups * reach + g * rest:groups * reach + (g + 1) * rest, cols] = (
                        circle[0:rest] * band_mask[reach:count, cols]
                    )
            here = slice(part * LANES, (part + 1) * LANES)
            upper = jnp.dot(held[0:groups * reach, :], window[0:2 * reach, here],
                            preferred_element_type=jnp.float32)
            lower = jnp.dot(held[groups * reach:, :], window[reach:3 * reach, here],
                            preferred_element_type=jnp.float32)
            top, bottom = upper[0:reach], lower[0:rest]
            for g in range(1, groups):
                top = jnp.where(owner == g, upper[g * reach:(g + 1) * reach], top)
                bottom = jnp.where(owner == g, lower[g * rest:(g + 1) * rest], bottom)
            out_lanes = pl.ds(pl.multiple_of(i * wide + part * LANES, LANES), LANES)
            out_ref[0:reach, out_lanes] = (gate[0:reach, here] * top).astype(out_ref.dtype)
            out_ref[reach:count, out_lanes] = (gate[reach:count, here] * bottom).astype(out_ref.dtype)
        return carry

    lax.fori_loop(0, width // wide, one, 0)


def mixer(index, lengths, inputs, short_filter, base, tail, halos, first=0, held=None):
    slots, count, width = inputs.shape
    filters, reach = base.shape
    rows, cols = tail.shape
    block = min(cols, 512)
    short = short_filter.shape[1]
    groups = LANES * filters // width
    wide = 2 * LANES
    start = first // block
    extra = () if held is None else (held,)
    operands = (index, lengths, inputs, inputs, inputs, short_filter, base, tail, *halos, *extra)
    return pl.pallas_call(
        mixer_kernel,
        out_shape=jax.ShapeDtypeStruct((count, width), inputs.dtype),
        grid_spec=pltpu.PrefetchScalarGridSpec(
            num_scalar_prefetch=2,
            grid=(cols // block,),
            in_specs=[
                pl.BlockSpec((None, count - reach, block), lambda i, *_: (0, 0, start + i)),
                pl.BlockSpec((None, count, block), lambda i, *_: (1, 0, start + i)),
                pl.BlockSpec((None, count - reach, block), lambda i, *_: (2, 0, start + i)),
                pl.BlockSpec((slots, short, block), lambda i, *_: (0, 0, start + i)),
                pl.BlockSpec((filters * block // width, reach), lambda i, *_: (start + i, 0)),
                pl.BlockSpec((rows, block), lambda i, *_: (0, i)),
            ]
            + [pl.BlockSpec((rows, block), lambda i, *_: (0, i))] * len(halos)
            + [pl.BlockSpec(memory_space=pl.ANY)] * len(extra),
            out_specs=pl.BlockSpec((count, block), lambda i, *_: (0, start + i)),
            scratch_shapes=[
                pltpu.VMEM((slots, wide // LANES, 16 + count, LANES), jnp.float32),
                pltpu.VMEM((short, count, LANES), jnp.float32),
                pltpu.VMEM((slots, 8, block), jnp.float32),
                pltpu.VMEM((count, 2 * LANES), inputs.dtype),
                pltpu.VMEM((wide // LANES, groups * count, 2 * LANES), inputs.dtype),
                pltpu.VMEM((3 * reach, wide), inputs.dtype),
                pltpu.VMEM((count, wide), jnp.float32),
            ],
        ),
        input_output_aliases={len(operands) - 1: 0} if extra else {},
        name="mixer",
    )(*operands)


def parts_of(value):
    high = value.astype(jnp.bfloat16)
    rest = value - high.astype(jnp.float32)
    middle = rest.astype(jnp.bfloat16)
    low = (rest - middle.astype(jnp.float32)).astype(jnp.bfloat16)
    return high, middle, low


def attend_kernel(where_ref, lengths_ref, own_ref, near_ref, far_ref, prior_ref,
                  out_ref, out_peak_ref, out_total_ref, near_out_ref, far_out_ref, bias, peaks, totals):
    count = own_ref.shape[1]
    width = near_ref.shape[1]
    heads = width // LANES
    scale = 1.0 / math.sqrt(LANES)
    index = where_ref[0]
    ends = bounds_of(lengths_ref)
    pivot = index == 1

    def mask(groups, keys, first):
        row = lax.broadcasted_iota(jnp.int32, (count, keys), 0)
        source = first + lax.broadcasted_iota(jnp.int32, (count, keys), 1)
        for which in range(groups):
            place = (index + which) * count + row
            ok = (source <= place) & (source >= start_of(place, ends))
            bias[which * count:(which + 1) * count, 0:keys] = jnp.where(ok, 0.0, NEG)

    rate = scale * math.log2(math.e)

    def softmax(queries, keys, values):
        rows, extent = queries.shape[0], keys.shape[0]
        scores = lax.dot_general(queries, keys, (((1,), (1,)), ((), ())),
                                 preferred_element_type=jnp.float32)
        scores = scores + bias[0:rows, 0:extent]
        peak = jnp.maximum(jnp.max(scores, axis=1, keepdims=True), FLOOR)
        weights = jnp.exp2((scores - peak) * rate).astype(jnp.bfloat16)
        wide = jnp.concatenate([values, jnp.ones(values.shape, values.dtype)], axis=1)
        mixed = jnp.dot(weights, wide, preferred_element_type=jnp.float32)
        return mixed[:, :LANES], peak, mixed[:, LANES:]

    lane = lax.broadcasted_iota(jnp.int32, (1, LANES), 1)

    def several(one, rows):
        peaks[0:rows] = jnp.zeros((rows, LANES), jnp.float32)
        totals[0:rows] = jnp.zeros((rows, LANES), jnp.float32)
        def body(i, carry):
            peak_of, total_of = peaks[0:rows], totals[0:rows]
            for u in range(HEADS_AT_ONCE):
                h = i * HEADS_AT_ONCE + u
                peak, total = one(h)
                peak_of = jnp.where(lane == h, peak, peak_of)
                total_of = jnp.where(lane == h, total, total_of)
            peaks[0:rows], totals[0:rows] = peak_of, total_of
            return carry
        lax.fori_loop(0, heads // HEADS_AT_ONCE, body, 0)

    @pl.when(pivot)
    def _():
        mask(3, 2 * count, (index - 1) * count)
        def one(h):
            lanes = pl.ds(pl.multiple_of(h * LANES, LANES), LANES)
            queries = jnp.concatenate([own_ref[0, :, lanes], near_ref[:, lanes], far_ref[:, lanes]], axis=0)
            if len(prior_ref.shape) == 3:
                before = prior_ref[0, :, lanes], prior_ref[1, :, lanes]
            else:
                beside = pl.ds(pl.multiple_of(width + h * LANES, LANES), LANES)
                before = prior_ref[0:count, lanes], prior_ref[0:count, beside]
            keys = jnp.concatenate([before[0], own_ref[1, :, lanes]], axis=0)
            values = jnp.concatenate([before[1], own_ref[2, :, lanes]], axis=0)
            mixed, peak, total = softmax(queries, keys, values)
            out_ref[:, lanes] = mixed[0:count]
            near_out_ref[:, lanes] = mixed[count:2 * count].astype(near_out_ref.dtype)
            far_out_ref[:, lanes] = mixed[2 * count:].astype(far_out_ref.dtype)
            return peak, total
        several(one, 3 * count)

    @pl.when(jnp.logical_not(pivot))
    def _():
        mask(2, count, index * count)
        def one(h):
            lanes = pl.ds(pl.multiple_of(h * LANES, LANES), LANES)
            queries = jnp.concatenate([own_ref[0, :, lanes], near_ref[:, lanes]], axis=0)
            mixed, peak, total = softmax(queries, own_ref[1, :, lanes], own_ref[2, :, lanes])
            out_ref[:, lanes] = mixed[0:count]
            near_out_ref[:, lanes] = mixed[count:].astype(near_out_ref.dtype)
            return peak, total
        several(one, 2 * count)

    out_peak_ref[...] = peaks[0:count]
    out_total_ref[...] = totals[0:count]
    for which, ref in ((1, near_out_ref), (2, far_out_ref)):
        rows = slice(which * count, (which + 1) * count)
        packed = jnp.zeros((count, LANES), jnp.float32)
        for at, piece in enumerate(parts_of(peaks[rows]) + parts_of(totals[rows])):
            piece = piece.astype(jnp.float32)
            packed = packed + (pltpu.roll(piece, at * SPREAD, 1) if at else piece)
        ref[:, width:width + LANES] = packed.astype(ref.dtype)

def attend_part(index, lengths, blocks, near, far, prior, first, width, at):
    slots, count, _ = blocks.shape
    whole = lambda i, *_: (0, 0)
    return pl.pallas_call(
        attend_kernel,
        out_shape=(
            jax.ShapeDtypeStruct((count, width), jnp.float32),
            jax.ShapeDtypeStruct((count, LANES), jnp.float32),
            jax.ShapeDtypeStruct((count, LANES), jnp.float32),
            jax.ShapeDtypeStruct((count, width + LANES), near.dtype),
            jax.ShapeDtypeStruct((count, width + LANES), near.dtype),
        ),
        grid_spec=pltpu.PrefetchScalarGridSpec(
            num_scalar_prefetch=2,
            grid=(1,),
            in_specs=[
                pl.BlockSpec((slots, count, width), lambda i, *_: (0, 0, first)),
                pl.BlockSpec((count, width), lambda i, *_: (0, at)),
                pl.BlockSpec((count, width), lambda i, *_: (0, at)),
                pl.BlockSpec(prior.shape, lambda i, *_: (0,) * prior.ndim),
            ],
            out_specs=(
                pl.BlockSpec((count, width), whole),
                pl.BlockSpec((count, LANES), whole),
                pl.BlockSpec((count, LANES), whole),
                pl.BlockSpec((count, width + LANES), whole),
                pl.BlockSpec((count, width + LANES), whole),
            ),
            scratch_shapes=[
                pltpu.VMEM((3 * count, 2 * count), jnp.float32),
                pltpu.VMEM((3 * count, LANES), jnp.float32),
                pltpu.VMEM((3 * count, LANES), jnp.float32),
            ],
        ),
        compiler_params=pltpu.CompilerParams(vmem_limit_bytes=48 << 20),
        name="attend_part",
    )(index, lengths, blocks, near, far, prior)

def merge_kernel(where_ref, own_ref, own_peak_ref, own_total_ref, near_ref, far_ref, *refs):
    out_ref = refs[-1]
    count, width = own_ref.shape
    index = where_ref[0]
    rate = math.log2(math.e) / math.sqrt(LANES)

    def stats(ref):
        packed = ref[:, width:width + LANES].astype(jnp.float32)
        pieces = [packed] + [pltpu.roll(packed, LANES - at * SPREAD, 1) for at in range(1, 6)]
        return pieces[0] + pieces[1] + pieces[2], pieces[3] + pieces[4] + pieces[5]

    @pl.when(index < 2)
    def _():
        part = 1.0 / jnp.where(own_total_ref[...] > 0.0, own_total_ref[...], 1.0)
        for h in range(width // LANES):
            lanes = slice(h * LANES, (h + 1) * LANES)
            out_ref[:, lanes] = (own_ref[:, lanes] * part[:, h:h + 1]).astype(out_ref.dtype)

    @pl.when(index >= 2)
    def _():
        both = index == 3
        own, total = own_peak_ref[...], own_total_ref[...]
        near, near_total = stats(near_ref)
        far, far_total = stats(far_ref)
        far = jnp.where(both, far, NEG)
        peak = jnp.maximum(own, jnp.maximum(near, far))
        own_part = jnp.exp2((own - peak) * rate)
        near_part = jnp.exp2((near - peak) * rate)
        far_part = jnp.exp2((far - peak) * rate)
        whole = own_part * total + near_part * near_total
        whole = whole + jnp.where(both, far_part * far_total, 0.0)
        whole = 1.0 / jnp.where(whole > 0.0, whole, 1.0)
        own_part, near_part, far_part = own_part * whole, near_part * whole, far_part * whole
        for h in range(width // LANES):
            lanes = slice(h * LANES, (h + 1) * LANES)
            mixed = own_ref[:, lanes] * own_part[:, h:h + 1]
            mixed = mixed + near_ref[:, lanes].astype(jnp.float32) * near_part[:, h:h + 1]
            mixed = mixed + jnp.where(
                both, far_ref[:, lanes].astype(jnp.float32) * far_part[:, h:h + 1], 0.0
            )
            out_ref[:, lanes] = mixed.astype(out_ref.dtype)


def merge_part(index, own, own_peak, own_total, near, far, first, full, held):
    count, width = own.shape
    whole = lambda i, *_: (0, 0)
    extra = () if held is None else (held,)
    return pl.pallas_call(
        merge_kernel,
        out_shape=jax.ShapeDtypeStruct((count, full), near.dtype),
        grid_spec=pltpu.PrefetchScalarGridSpec(
            num_scalar_prefetch=1,
            grid=(1,),
            in_specs=[
                pl.BlockSpec((count, width), whole),
                pl.BlockSpec((count, LANES), whole),
                pl.BlockSpec((count, LANES), whole),
                pl.BlockSpec((count, width + LANES), whole),
                pl.BlockSpec((count, width + LANES), whole),
            ]
            + [pl.BlockSpec(memory_space=pl.ANY)] * len(extra),
            out_specs=pl.BlockSpec((count, width), lambda i, *_: (0, first)),
        ),
        input_output_aliases={6: 0} if extra else {},
        name="merge_part",
    )(index, own, own_peak, own_total, near, far, *extra)


def layer_four(index, lengths, inputs, short_filter, base, blocks):
    reach = base.shape[1]
    width = blocks.shape[2]
    part = width // CHUNKS
    after = lax.optimization_barrier
    moved = []
    for c in range(CHUNKS):
        cols = slice(c * part, (c + 1) * part)
        prior = lax.ppermute(blocks[1:3, :, cols], "ctx", [(0, 1)])
        near = lax.ppermute(blocks[0, :, cols], "ctx", [(2, 1), (3, 2)])
        far = lax.ppermute(blocks[0, :, cols], "ctx", [(3, 1)])
        moved.append((near, far, prior))
    (tail,) = mixer_tail(index, lengths, inputs, short_filter, reach, 0, width)
    halo = lax.ppermute(tail, "ctx", [(0, 1), (1, 2), (2, 3)])
    sent, last = [], None
    for c in range(CHUNKS):
        near, far, prior = moved[c]
        if c:
            near, far, prior, _ = after((near, far, prior, last))
        own, peak, total, near_out, far_out = attend_part(
            index, lengths, blocks, near, far, prior, c, part, 0
        )
        last = near_out
        near_in = lax.ppermute(near_out, "ctx", [(1, 2), (2, 3)])
        far_in = lax.ppermute(far_out, "ctx", [(1, 3)])
        sent.append((own, peak, total, near_in, far_in))
    halo, _ = after((halo, last))
    hyena_out = mixer(index, lengths, inputs, short_filter, base, tail, [halo])
    held = None
    for c in range(CHUNKS):
        if c == CHUNKS - 1:
            held, hyena_out = after((held, hyena_out))
        held = merge_part(index, *sent[c], c, width, held)
    return hyena_out, held


def attend_any(lengths, blocks, heads):
    count, width = blocks.shape[1:]
    depth = width // heads
    bounds = jnp.cumsum(lengths[0])[:-1]
    gathered = lax.all_gather(blocks[1:3], "ctx", axis=1, tiled=True)
    extent = gathered.shape[1]
    place = lax.axis_index("ctx") * count + jnp.arange(count, dtype=jnp.int32)
    source = jnp.arange(extent, dtype=jnp.int32)
    start = jnp.max(jnp.where(place[:, None] >= bounds[None, :], bounds[None, :], 0), axis=1)
    admit = (source[None, :] <= place[:, None]) & (source[None, :] >= start[:, None])
    queries = blocks[0].reshape(count, heads, depth)
    keys = gathered[0].reshape(extent, heads, depth)
    values = gathered[1].reshape(extent, heads, depth)
    scores = jnp.einsum("thd,shd->hts", queries, keys, preferred_element_type=jnp.float32)
    scores = jnp.where(admit[None], scores * (1.0 / math.sqrt(depth)), NEG)
    peak = jnp.max(scores, axis=2, keepdims=True)
    weights = jnp.where(admit[None], jnp.exp(scores - peak), 0.0)
    total = jnp.sum(weights, axis=2)
    mixed = jnp.einsum("hts,shd->htd", weights.astype(jnp.bfloat16), values,
                       preferred_element_type=jnp.float32)
    mixed = mixed / total[:, :, None]
    return mixed.transpose(1, 0, 2).reshape(count, width).astype(jnp.bfloat16)


def on_device(hyena_in, short_filter, long_filter, qkv, lengths):
    size = lax.axis_size("ctx")
    index = lax.axis_index("ctx").astype(jnp.int32).reshape(1)
    inputs = hyena_in[0].transpose(1, 0, 2)
    blocks = qkv[0].transpose(1, 0, 2)
    reach = long_filter.shape[0]
    taps = long_filter.astype(jnp.float32).T
    base = jnp.concatenate([taps[:, :1], taps[:, :0:-1]], axis=1)
    heads = H // lax.axis_size("tp")
    if size == 4:
        hyena_out, attn_out = layer_four(index, lengths, inputs, short_filter, base, blocks)
    else:
        (tail,) = mixer_tail(index, lengths, inputs, short_filter, reach, 0, inputs.shape[2])
        halo = lax.ppermute(tail, "ctx", [(i, i + 1) for i in range(size - 1)])
        hyena_out = mixer(index, lengths, inputs, short_filter, base, tail, [halo])
        attn_out = attend_any(lengths, blocks, heads)
    return (hyena_out[None], attn_out[None])


def solution(mesh):
    in_specs = (
        P(("groups", "dp"), "ctx", None, "tp"),
        P(None, None, "tp"),
        P(None, "tp"),
        P(("groups", "dp"), "ctx", None, "tp"),
        P(("groups", "dp"), None),
    )
    out_specs = (P(("groups", "dp"), "ctx", "tp"), P(("groups", "dp"), "ctx", "tp"))
    return jax.shard_map(
        on_device, mesh=mesh, in_specs=in_specs, out_specs=out_specs, check_vma=False
    )
```

time: 128 us -> 112 us (0.88)
  the two profiles are of different devices: /device:TPU:16 before, /device:TPU:24 now
where the time goes in v1:
time: 112 us; the launch traced here: 111 us
  Pallas kernels  39.6 us (35%)
  waiting for transfers between devices  36.7 us (33%)
  starting transfers between devices  21.6 us (19%)
  local copies, waits for them, and re-layouts  11.5 us (10%)
    ppermute x2, waiting for transfers between devices, layer_four(): far = lax.ppermute(blocks[0, :, cols], 'ctx', [(3, 1)])  15.4 us
    pallas_call x1, Pallas kernels, mixer(): pl.pallas_call(mixer_kernel, out_shape=jax.ShapeDtypeStruct((count, width...  13 us
    pallas_call x2, Pallas kernels, attend_part(): pl.pallas_call(attend_kernel, out_shape=(jax.ShapeDtypeStruct((count, wid...  12.7 us
    ppermute x2, waiting for transfers between devices, layer_four(): far_in = lax.ppermute(far_out, 'ctx', [(1, 3)])  10.6 us
    pallas_call x2, Pallas kernels, merge_part(): pl.pallas_call(merge_kernel, out_shape=jax.ShapeDtypeStruct((count, full)...  7.4 us
    ppermute x2, waiting for transfers between devices, layer_four(): near_in = lax.ppermute(near_out, 'ctx', [(1, 2), (2, 3)])  7.07 us
    ppermute x2, starting transfers between devices, layer_four(): far = lax.ppermute(blocks[0, :, cols], 'ctx', [(3, 1)])  6.94 us
    ppermute x2, starting transfers between devices, layer_four(): near = lax.ppermute(blocks[0, :, cols], 'ctx', [(2, 1), (3, 2)])  6.68 us
  transfers between devices with their start and end apart: 11, of which 5 were waited for; matrix products, arithmetic and copies ran while one was open for 3% of the time, Pallas kernels for 32%

profile of v1, /device:TPU:24, one launch (start us, length us, event | category | flops | bytes accessed | tf_op | source)
XLA Modules:
  0.0 111.1 jit_solution(2304378942139508495)
XLA Ops:
  0.6 3.3 %fusion = (bf16[2,144,2048]{2,1,0:T(8,128)(2,1)}, bf16[2,144,2048]{2,1,0:T(8,128)(2,1)}) fusion(bf16[3,144,4096]{2,1,0:T(8,128)(2,1)} %bitcast.22), kind=kLoop, calls=%fused_computation.4 | loop fusion | bytes 4718592 | tf_op jit(solution)/shard_map/slice | solution.py:476
  4.7 2.4 %slice_bitcast_fusion = (bf16[144,2048]{1,0:T(8,128)(2,1)}, bf16[144,2048]{1,0:T(8,128)(2,1)}) fusion(bf16[3,144,4096]{2,1,0:T(8,128)(2,1)} %bitcast.23), kind=kLoop, calls=%fused_computation | loop fusion | bytes 2359296 | tf_op jit(solution)/shard_map/squeeze | solution.py:477
  7.1 2.4 %collective-permute-start = (bf16[144,2048]{1,0:T(8,128)(2,1)}, bf16[144,2048]{1,0:T(8,128)(2,1)S(1)}, u32[]{:S(2)}, u32[]{:S(2)}) collective-permute-start(bf16[144,2048]{1,0:T(8,128)(2,1)} %get-tuple-element.37), channel_id=1, source_target_pairs={{8,4},{12,8},{9,5},{13,9},{10,6},{14,10},{11,7},{15,11},{24,20},{2... | collective-permute-start | bytes 1769480 | tf_op jit(solution)/shard_map/ppermute | solution.py:477
  9.5 1.7 %collective-permute-start.1 = (bf16[144,2048]{1,0:T(8,128)(2,1)}, bf16[144,2048]{1,0:T(8,128)(2,1)S(1)}, u32[]{:S(2)}, u32[]{:S(2)}) collective-permute-start(bf16[144,2048]{1,0:T(8,128)(2,1)} %get-tuple-element.37), channel_id=1, source_target_pairs={{12,4},{13,5},{14,6},{15,7},{28,20},{29,21},{30,22},{31,23}} | collective-permute-start | bytes 1769480 | tf_op jit(solution)/shard_map/ppermute | solution.py:478
  12.0 6.5 %mixer_tail.1.tail_ref = bf16[160,4096]{1,0:T(8,128)(2,1)} custom-call(s32[1]{0:T(128)} %bitcast.where_ref, s32[1,4]{1,0:T(1,128)} %lengths_ref.7, bf16[3,144,4096]{2,1,0:T(8,128)(2,1)} %bitcast.16, bf16[3,144,4096]{2,1,0:T(8,128)(2,1)} %bitcast.17, bf16[3,144,4096]{2,1,0:T(8,128)(2,1)} %bitcast.18, bf16[3,7,4096]{2,1,0:T(8,128)(2,1)} %taps_ref.3), custom_call_target="tpu_custom_call" | custom-call | tf_op jit(solution)/shard_map/mixer_tail/pallas_call | solution.py:114
  18.5 1.3 %collective-permute-start.5 = (bf16[160,4096]{1,0:T(8,128)(2,1)}, bf16[160,4096]{1,0:T(8,128)(2,1)}, u32[]{:S(2)}, u32[]{:S(2)}) collective-permute-start(bf16[160,4096]{1,0:T(8,128)(2,1)} %mixer_tail.1.tail_ref), channel_id=1, source_target_pairs={{0,4},{4,8},{8,12},{1,5},{5,9},{9,13},{2,6},{6,10},{10,14},{3,7},{... | collective-permute-start | bytes 3932168 | tf_op jit(solution)/shard_map/ppermute | solution.py:481
  19.8 3.7 %collective-permute-done.near_ref = bf16[144,2048]{1,0:T(8,128)(2,1)S(1)} collective-permute-done((bf16[144,2048]{1,0:T(8,128)(2,1)}, bf16[144,2048]{1,0:T(8,128)(2,1)S(1)}, u32[]{:S(2)}, u32[]{:S(2)}) %collective-permute-start) | collective-permute-done | bytes 589856 | tf_op jit(solution)/shard_map/ppermute | solution.py:477
  23.5 4.3 %collective-permute-start.6 = (bf16[144,2048]{1,0:T(8,128)(2,1)}, bf16[144,2048]{1,0:T(8,128)(2,1)S(1)}, u32[]{:S(2)}, u32[]{:S(2)}) collective-permute-start(bf16[144,2048]{1,0:T(8,128)(2,1)} %get-tuple-element.36), channel_id=1, source_target_pairs={{8,4},{12,8},{9,5},{13,9},{10,6},{14,10},{11,7},{15,11},{24,20},{2... | collective-permute-start | bytes 1769480 | tf_op jit(solution)/shard_map/ppermute | solution.py:477
  27.8 8.4 %collective-permute-done.1.far_ref = bf16[144,2048]{1,0:T(8,128)(2,1)S(1)} collective-permute-done((bf16[144,2048]{1,0:T(8,128)(2,1)}, bf16[144,2048]{1,0:T(8,128)(2,1)S(1)}, u32[]{:S(2)}, u32[]{:S(2)}) %collective-permute-start.1) | collective-permute-done | bytes 589856 | tf_op jit(solution)/shard_map/ppermute | solution.py:478
  36.1 5.2 %collective-permute-start.7 = (bf16[144,2048]{1,0:T(8,128)(2,1)}, bf16[144,2048]{1,0:T(8,128)(2,1)S(1)}, u32[]{:S(2)}, u32[]{:S(2)}) collective-permute-start(bf16[144,2048]{1,0:T(8,128)(2,1)} %get-tuple-element.36), channel_id=1, source_target_pairs={{12,4},{13,5},{14,6},{15,7},{28,20},{29,21},{30,22},{31,23}} | collective-permute-start | bytes 1769480 | tf_op jit(solution)/shard_map/ppermute | solution.py:478
  41.4 6.9 %attend_part.2 = (f32[144,2048]{1,0:T(8,128)S(1)}, f32[144,128]{1,0:T(8,128)S(1)}, f32[144,128]{1,0:T(8,128)S(1)}, bf16[144,2176]{1,0:T(8,128)(2,1)}, bf16[144,2176]{1,0:T(8,128)(2,1)}) custom-call(s32[1]{0:T(128)} %bitcast.where_ref, s32[1,4]{1,0:T(1,128)S(1)} %copy-done.6, bf16[3,144,4096]{2,1,0:T(8,128)(2,1)} %bitcast.24, ...), custom_call_target="tpu_custom_call" | custom-call | tf_op jit(solution)/shard_map/attend_part/pallas_call | solution.py:365
  48.2 1.0 copy-done.1
  50.5 1.3 %collective-permute-start.3 = (bf16[144,2176]{1,0:T(8,128)(2,1)}, bf16[144,2176]{1,0:T(8,128)(2,1)}, u32[]{:S(2)}, u32[]{:S(2)}) collective-permute-start(bf16[144,2176]{1,0:T(8,128)(2,1)} %get-tuple-element.21), channel_id=1, source_target_pairs={{4,8},{8,12},{5,9},{9,13},{6,10},{10,14},{7,11},{11,15},{20,24},{2... | collective-permute-start | bytes 1880072 | tf_op jit(solution)/shard_map/ppermute | solution.py:491
  51.8 1.4 %collective-permute-start.4 = (bf16[144,2176]{1,0:T(8,128)(2,1)}, bf16[144,2176]{1,0:T(8,128)(2,1)}, u32[]{:S(2)}, u32[]{:S(2)}) collective-permute-start(bf16[144,2176]{1,0:T(8,128)(2,1)} %get-tuple-element.22), channel_id=1, source_target_pairs={{4,12},{5,13},{6,14},{7,15},{20,28},{21,29},{22,30},{23,31}} | collective-permute-start | bytes 1880072 | tf_op jit(solution)/shard_map/ppermute | solution.py:492
  53.2 7.0 %collective-permute-done.7.far_ref = bf16[144,2048]{1,0:T(8,128)(2,1)S(1)} collective-permute-done((bf16[144,2048]{1,0:T(8,128)(2,1)}, bf16[144,2048]{1,0:T(8,128)(2,1)S(1)}, u32[]{:S(2)}, u32[]{:S(2)}) %collective-permute-start.7) | collective-permute-done | bytes 589856 | tf_op jit(solution)/shard_map/ppermute | solution.py:478
  60.3 5.8 %attend_part.3 = (f32[144,2048]{1,0:T(8,128)S(1)}, f32[144,128]{1,0:T(8,128)S(1)}, f32[144,128]{1,0:T(8,128)S(1)}, bf16[144,2176]{1,0:T(8,128)(2,1)S(1)}, bf16[144,2176]{1,0:T(8,128)(2,1)S(1)}) custom-call(s32[1]{0:T(128)} %bitcast.where_ref, s32[1,4]{1,0:T(1,128)S(1)} %copy-done.6, bf16[3,144,4096]{2,1,0:T(8,128)(2,1)} %bitcast.25, ...), custom_call_target="tpu_custom_call" | custom-call | tf_op jit(solution)/shard_map/attend_part/pallas_call | solution.py:365
  66.1 1.0 copy-done
  68.4 1.3 %collective-permute-start.9 = (bf16[144,2176]{1,0:T(8,128)(2,1)S(1)}, bf16[144,2176]{1,0:T(8,128)(2,1)S(1)}, u32[]{:S(2)}, u32[]{:S(2)}) collective-permute-start(bf16[144,2176]{1,0:T(8,128)(2,1)S(1)} %get-tuple-element.26), channel_id=1, source_target_pairs={{4,8},{8,12},{5,9},{9,13},{6,10},{10,14},{7,11},{11,15},{20,24},{2... | collective-permute-start | bytes 1880072 | tf_op jit(solution)/shard_map/ppermute | solution.py:491
  69.7 1.3 %collective-permute-start.10 = (bf16[144,2176]{1,0:T(8,128)(2,1)S(1)}, bf16[144,2176]{1,0:T(8,128)(2,1)S(1)}, u32[]{:S(2)}, u32[]{:S(2)}) collective-permute-start(bf16[144,2176]{1,0:T(8,128)(2,1)S(1)} %get-tuple-element.32), channel_id=1, source_target_pairs={{4,12},{5,13},{6,14},{7,15},{20,28},{21,29},{22,30},{23,31}} | collective-permute-start | bytes 1880072 | tf_op jit(solution)/shard_map/ppermute | solution.py:492
  72.2 13.0 %mixer.1 = bf16[144,4096]{1,0:T(8,128)(2,1)} custom-call(s32[1]{0:T(128)} %bitcast.where_ref, s32[1,4]{1,0:T(1,128)} %lengths_ref.7, bf16[3,144,4096]{2,1,0:T(8,128)(2,1)} %bitcast.19, bf16[3,144,4096]{2,1,0:T(8,128)(2,1)} %bitcast.20, bf16[3,144,4096]{2,1,0:T(8,128)(2,1)} %bitcast.21, bf16[3,7,4096]{2,1,0:T(8,128)(2,1)} %taps_ref.3, ...), custom_call_target="tpu_custom_call" | custom-call | tf_op jit(solution)/shard_map/mixer/pallas_call | solution.py:233
  85.2 3.7 %merge_part.2.refs_0_ = bf16[144,4096]{1,0:T(8,128)(2,1)} custom-call(s32[1]{0:T(128)} %bitcast.where_ref, f32[144,2048]{1,0:T(8,128)} %copy-done.1, f32[144,128]{1,0:T(8,128)} %copy-done.2, f32[144,128]{1,0:T(8,128)} %copy-done.3, bf16[144,2176]{1,0:T(8,128)(2,1)} %collective-permute-done.3.near_ref, bf16[144,2176]{1,0:T(8,128)(2,1)} %collective-permute-done.4.far_ref), custom_call_target="tpu_custom_call" | custom-call | tf_op jit(solution)/shard_map/merge_part/pallas_call | solution.py:447
  88.9 7.1 %collective-permute-done.9.near_ref = bf16[144,2176]{1,0:T(8,128)(2,1)S(1)} collective-permute-done((bf16[144,2176]{1,0:T(8,128)(2,1)S(1)}, bf16[144,2176]{1,0:T(8,128)(2,1)S(1)}, u32[]{:S(2)}, u32[]{:S(2)}) %collective-permute-start.9) | collective-permute-done | bytes 626720 | tf_op jit(solution)/shard_map/ppermute | solution.py:491
  96.0 10.6 %collective-permute-done.10.far_ref = bf16[144,2176]{1,0:T(8,128)(2,1)S(1)} collective-permute-done((bf16[144,2176]{1,0:T(8,128)(2,1)S(1)}, bf16[144,2176]{1,0:T(8,128)(2,1)S(1)}, u32[]{:S(2)}, u32[]{:S(2)}) %collective-permute-start.10) | collective-permute-done | bytes 626720 | tf_op jit(solution)/shard_map/ppermute | solution.py:492
  107.4 3.7 %merge_part.3 = bf16[144,4096]{1,0:T(8,128)(2,1)} custom-call(s32[1]{0:T(128)} %bitcast.where_ref, f32[144,2048]{1,0:T(8,128)} %copy-done, f32[144,128]{1,0:T(8,128)} %copy-done.4, f32[144,128]{1,0:T(8,128)} %copy-done.5, bf16[144,2176]{1,0:T(8,128)(2,1)} %copy-done.7, bf16[144,2176]{1,0:T(8,128)(2,1)} %copy-done.8, ...), custom_call_target="tpu_custom_call", output_to_operand_aliasing={{}: (6, {})} | custom-call | tf_op jit(solution)/shard_map/merge_part/pallas_call | solution.py:447
  (31 shorter events, 6.0 us)
Async XLA Ops:
  3.9 37.4 %collective-permute-start.2 = (bf16[2,144,2048]{2,1,0:T(8,128)(2,1)}, bf16[2,144,2048]{2,1,0:T(8,128)(2,1)S(1)}, u32[]{:S(2)}, u32[]{:S(2)}) collective-permute-start(bf16[2,144,2048]{2,1,0:T(8,128)(2,1)} %get-tuple-element.35), channel_id=1, source_target_pairs={{0,4},{1,5},{2,6},{3,7},{16,20},{17,21},{18,22},{19,23}} | collective-permute-start | bytes 3538952 | tf_op jit(solution)/shard_map/ppermute | solution.py:476
  7.1 16.4 %collective-permute-start = (bf16[144,2048]{1,0:T(8,128)(2,1)}, bf16[144,2048]{1,0:T(8,128)(2,1)S(1)}, u32[]{:S(2)}, u32[]{:S(2)}) collective-permute-start(bf16[144,2048]{1,0:T(8,128)(2,1)} %get-tuple-element.37), channel_id=1, source_target_pairs={{8,4},{12,8},{9,5},{13,9},{10,6},{14,10},{11,7},{15,11},{24,20},{2... | collective-permute-start | bytes 1769480 | tf_op jit(solution)/shard_map/ppermute | solution.py:477
  9.5 26.7 %collective-permute-start.1 = (bf16[144,2048]{1,0:T(8,128)(2,1)}, bf16[144,2048]{1,0:T(8,128)(2,1)S(1)}, u32[]{:S(2)}, u32[]{:S(2)}) collective-permute-start(bf16[144,2048]{1,0:T(8,128)(2,1)} %get-tuple-element.37), channel_id=1, source_target_pairs={{12,4},{13,5},{14,6},{15,7},{28,20},{29,21},{30,22},{31,23}} | collective-permute-start | bytes 1769480 | tf_op jit(solution)/shard_map/ppermute | solution.py:478
  11.2 49.1 %collective-permute-start.8 = (bf16[2,144,2048]{2,1,0:T(8,128)(2,1)}, bf16[2,144,2048]{2,1,0:T(8,128)(2,1)S(1)}, u32[]{:S(2)}, u32[]{:S(2)}) collective-permute-start(bf16[2,144,2048]{2,1,0:T(8,128)(2,1)} %get-tuple-element.34), channel_id=1, source_target_pairs={{0,4},{1,5},{2,6},{3,7},{16,20},{17,21},{18,22},{19,23}} | collective-permute-start | bytes 3538952 | tf_op jit(solution)/shard_map/ppermute | solution.py:476
  12.0 29.4 %copy-start.6 = (s32[1,4]{1,0:T(1,128)S(1)}, s32[1,4]{1,0:T(1,128)}, u32[]{:S(2)}) copy-start(s32[1,4]{1,0:T(1,128)} %lengths_ref.7) | copy-start | bytes 52
  18.5 53.7 %collective-permute-start.5 = (bf16[160,4096]{1,0:T(8,128)(2,1)}, bf16[160,4096]{1,0:T(8,128)(2,1)}, u32[]{:S(2)}, u32[]{:S(2)}) collective-permute-start(bf16[160,4096]{1,0:T(8,128)(2,1)} %mixer_tail.1.tail_ref), channel_id=1, source_target_pairs={{0,4},{4,8},{8,12},{1,5},{5,9},{9,13},{2,6},{6,10},{10,14},{3,7},{... | collective-permute-start | bytes 3932168 | tf_op jit(solution)/shard_map/ppermute | solution.py:481
  23.5 28.3 %collective-permute-start.6 = (bf16[144,2048]{1,0:T(8,128)(2,1)}, bf16[144,2048]{1,0:T(8,128)(2,1)S(1)}, u32[]{:S(2)}, u32[]{:S(2)}) collective-permute-start(bf16[144,2048]{1,0:T(8,128)(2,1)} %get-tuple-element.36), channel_id=1, source_target_pairs={{8,4},{12,8},{9,5},{13,9},{10,6},{14,10},{11,7},{15,11},{24,20},{2... | collective-permute-start | bytes 1769480 | tf_op jit(solution)/shard_map/ppermute | solution.py:477
  36.1 24.1 %collective-permute-start.7 = (bf16[144,2048]{1,0:T(8,128)(2,1)}, bf16[144,2048]{1,0:T(8,128)(2,1)S(1)}, u32[]{:S(2)}, u32[]{:S(2)}) collective-permute-start(bf16[144,2048]{1,0:T(8,128)(2,1)} %get-tuple-element.36), channel_id=1, source_target_pairs={{12,4},{13,5},{14,6},{15,7},{28,20},{29,21},{30,22},{31,23}} | collective-permute-start | bytes 1769480 | tf_op jit(solution)/shard_map/ppermute | solution.py:478
  48.2 1.0 copy-start.1
  49.2 0.6 copy-start.2
  49.9 0.6 copy-start.3
  50.5 34.7 %collective-permute-start.3 = (bf16[144,2176]{1,0:T(8,128)(2,1)}, bf16[144,2176]{1,0:T(8,128)(2,1)}, u32[]{:S(2)}, u32[]{:S(2)}) collective-permute-start(bf16[144,2176]{1,0:T(8,128)(2,1)} %get-tuple-element.21), channel_id=1, source_target_pairs={{4,8},{8,12},{5,9},{9,13},{6,10},{10,14},{7,11},{11,15},{20,24},{2... | collective-permute-start | bytes 1880072 | tf_op jit(solution)/shard_map/ppermute | solution.py:491
  51.8 19.2 %copy-start.9 = (bf16[128,256]{1,0:T(8,128)(2,1)S(1)}, bf16[128,256]{1,0:T(8,128)(2,1)}, u32[]{:S(2)}) copy-start(bf16[128,256]{1,0:T(8,128)(2,1)} %param.7) | copy-start | bytes 196612
  51.8 33.4 %collective-permute-start.4 = (bf16[144,2176]{1,0:T(8,128)(2,1)}, bf16[144,2176]{1,0:T(8,128)(2,1)}, u32[]{:S(2)}, u32[]{:S(2)}) collective-permute-start(bf16[144,2176]{1,0:T(8,128)(2,1)} %get-tuple-element.22), channel_id=1, source_target_pairs={{4,12},{5,13},{6,14},{7,15},{20,28},{21,29},{22,30},{23,31}} | collective-permute-start | bytes 1880072 | tf_op jit(solution)/shard_map/ppermute | solution.py:492
  66.1 1.0 copy-start
  67.1 0.6 copy-start.4
  67.8 0.6 copy-start.5
  68.4 27.6 %collective-permute-start.9 = (bf16[144,2176]{1,0:T(8,128)(2,1)S(1)}, bf16[144,2176]{1,0:T(8,128)(2,1)S(1)}, u32[]{:S(2)}, u32[]{:S(2)}) collective-permute-start(bf16[144,2176]{1,0:T(8,128)(2,1)S(1)} %get-tuple-element.26), channel_id=1, source_target_pairs={{4,8},{8,12},{5,9},{9,13},{6,10},{10,14},{7,11},{11,15},{20,24},{2... | collective-permute-start | bytes 1880072 | tf_op jit(solution)/shard_map/ppermute | solution.py:491
  69.7 36.9 %collective-permute-start.10 = (bf16[144,2176]{1,0:T(8,128)(2,1)S(1)}, bf16[144,2176]{1,0:T(8,128)(2,1)S(1)}, u32[]{:S(2)}, u32[]{:S(2)}) collective-permute-start(bf16[144,2176]{1,0:T(8,128)(2,1)S(1)} %get-tuple-element.32), channel_id=1, source_target_pairs={{4,12},{5,13},{6,14},{7,15},{20,28},{21,29},{22,30},{23,31}} | collective-permute-start | bytes 1880072 | tf_op jit(solution)/shard_map/ppermute | solution.py:492
  96.0 10.6 %copy-start.7 = (bf16[144,2176]{1,0:T(8,128)(2,1)}, bf16[144,2176]{1,0:T(8,128)(2,1)S(1)}, u32[]{:S(2)}) copy-start(bf16[144,2176]{1,0:T(8,128)(2,1)S(1)} %collective-permute-done.9.near_ref) | copy-start | bytes 1880068
  106.5 0.8 copy-start.8

commit v2 on v1

--- a/solution.py
+++ b/solution.py
@@ -13,8 +13,7 @@
 ROWS = 32
 TAIL_BLOCK = 1024
 MIX_BLOCK = 512
-HEADS_AT_ONCE = 4
-CHUNKS = 2
+HEADS_AT_ONCE = 8
 SPREAD = LANES // 6
 NEG = -1e30
 FLOOR = -1e29
@@ -62,7 +61,7 @@
     extra = len(refs) // 2
     slab_refs, out_ref, message_refs = refs[:extra], refs[extra], refs[extra + 1:]
     count, width = gate_ref.shape
-    reach = out_ref.shape[0] - 32
+    reach = out_ref.shape[0] - 24
     first = count - reach
     short = taps_ref.shape[1]
     parts = line.shape[1]
@@ -74,8 +73,7 @@
 
     taps[:, 0:short] = taps_ref[...].astype(jnp.float32)
     ends = [ref[ref.shape[0] - 16:].astype(jnp.float32)[8:] for ref in (gate_ref, last_ref, value_ref)]
-    ends = jnp.concatenate(ends + [jnp.zeros((8, width), jnp.float32)], axis=0)
-    out_ref[reach:reach + 32] = ends.astype(out_ref.dtype)
+    out_ref[reach:reach + 24] = jnp.concatenate(ends, axis=0).astype(out_ref.dtype)
 
     def one(i, carry):
         lanes = pl.ds(pl.multiple_of(i * wide, LANES), wide)
@@ -95,20 +93,20 @@
         @pl.when(where_ref[0] == 0)
         def _():
             message_ref[0:count] = slab_ref[...]
-            message_ref[count:] = jnp.zeros((reach + 32 - count, width), message_ref.dtype)
+            message_ref[count:] = jnp.zeros((reach + 24 - count, width), message_ref.dtype)
 
         @pl.when(where_ref[0] != 0)
         def _():
             message_ref[...] = out_ref[...]
 
 
-def mixer_tail(index, lengths, inputs, short_filter, reach, first, cols, blocks=None, slab=0):
-    slots, count, _ = inputs.shape
-    block = min(cols, 1024)
+def mixer_tail(index, lengths, inputs, short_filter, reach, blocks=None, slab=0):
+    slots, count, width = inputs.shape
+    block = min(width, 1024)
     short = short_filter.shape[1]
-    rows = reach + 32
-    start = first // block
-    out = jax.ShapeDtypeStruct((rows, cols), inputs.dtype)
+    rows = reach + 24
+    each = width // 2 // block
+    out = jax.ShapeDtypeStruct((rows, width), inputs.dtype)
     out_spec = pl.BlockSpec((rows, block), lambda i, *_: (0, i))
     extra = () if blocks is None else (blocks,)
     return pl.pallas_call(
@@ -116,14 +114,19 @@
         out_shape=(out,) * (1 + len(extra)),
         grid_spec=pltpu.PrefetchScalarGridSpec(
             num_scalar_prefetch=2,
-            grid=(cols // block,),
+            grid=(width // block,),
             in_specs=[
-                pl.BlockSpec((None, count, block), lambda i, *_: (0, 0, start + i)),
-                pl.BlockSpec((None, count, block), lambda i, *_: (2, 0, start + i)),
-                pl.BlockSpec((None, 16, block), lambda i, *_: (1, count // 16 - 1, start + i)),
-                pl.BlockSpec((slots, short, block), lambda i, *_: (0, 0, start + i)),
+                pl.BlockSpec((None, count, block), lambda i, *_: (0, 0, i)),
+                pl.BlockSpec((None, count, block), lambda i, *_: (2, 0, i)),
+                pl.BlockSpec((None, 16, block), lambda i, *_: (1, count // 16 - 1, i)),
+                pl.BlockSpec((slots, short, block), lambda i, *_: (0, 0, i)),
             ]
-            + [pl.BlockSpec((None, count, block), lambda i, *_: (1 + i, 0, slab))] * len(extra),
+            + [
+                pl.BlockSpec(
+                    (None, count, block), lambda i, *_: (1 + i // each, 0, slab * each + i % each)
+                )
+            ]
+            * len(extra),
             out_specs=(out_spec,) * (1 + len(extra)),
             scratch_shapes=[
                 pltpu.VMEM((2, 2, count, LANES), jnp.float32),
@@ -135,9 +138,9 @@
     )(index, lengths, inputs, inputs, inputs, short_filter, *extra)
 
 
-def mixer_kernel(where_ref, lengths_ref, x1_ref, x2_ref, v_ref, taps_ref, base_ref, tail_ref, *refs):
+def mixer_kernel(halos, where_ref, lengths_ref, x1_ref, x2_ref, v_ref, taps_ref, base_ref, tail_ref, *refs):
     *halo_refs, out_ref, line, keep, taps, band_mask, band, window, gate = refs
-    halo_refs = [ref for ref in halo_refs if ref.shape == tail_ref.shape]
+    halo_refs = halo_refs[:halos]
     slots = taps_ref.shape[0]
     count, width = x2_ref.shape
     reach = base_ref.shape[1]
@@ -179,7 +182,7 @@
         for part in range(parts):
             here = pl.ds(pl.multiple_of(i * wide + part * LANES, LANES), LANES)
             for slot, ref in enumerate((x1_ref, x2_ref, v_ref)):
-                line[slot, part, 8:16] = halo(slice(reach, reach + 32), here).astype(jnp.float32)[
+                line[slot, part, 8:16] = halo(slice(reach, reach + 24), here).astype(jnp.float32)[
                     8 * slot:8 * slot + 8
                 ]
                 line[slot, part, 16:16 + ref.shape[0]] = ref[:, here].astype(jnp.float32)
@@ -219,19 +222,25 @@
     lax.fori_loop(0, width // wide, one, 0)
 
 
-def mixer(index, lengths, inputs, short_filter, base, tail, halos, first=0, held=None):
+def mixer(index, lengths, inputs, short_filter, base, tail, halos, first, cols, held=None):
     slots, count, width = inputs.shape
     filters, reach = base.shape
-    rows, cols = tail.shape
+    rows = tail.shape[0]
     block = min(cols, 512)
     short = short_filter.shape[1]
     groups = LANES * filters // width
     wide = 2 * LANES
     start = first // block
     extra = () if held is None else (held,)
-    operands = (index, lengths, inputs, inputs, inputs, short_filter, base, tail, *halos, *extra)
+    received = [array for array, _ in halos]
+    operands = (index, lengths, inputs, inputs, inputs, short_filter, base, tail, *received, *extra)
+
+    def columns(at):
+        at = at // block
+        return pl.BlockSpec((rows, block), lambda i, *_: (0, at + i))
+
     return pl.pallas_call(
-        mixer_kernel,
+        partial(mixer_kernel, len(halos)),
         out_shape=jax.ShapeDtypeStruct((count, width), inputs.dtype),
         grid_spec=pltpu.PrefetchScalarGridSpec(
             num_scalar_prefetch=2,
@@ -242,9 +251,9 @@
                 pl.BlockSpec((None, count - reach, block), lambda i, *_: (2, 0, start + i)),
                 pl.BlockSpec((slots, short, block), lambda i, *_: (0, 0, start + i)),
                 pl.BlockSpec((filters * block // width, reach), lambda i, *_: (start + i, 0)),
-                pl.BlockSpec((rows, block), lambda i, *_: (0, i)),
+                columns(first),
             ]
-            + [pl.BlockSpec((rows, block), lambda i, *_: (0, i))] * len(halos)
+            + [columns(at) for _, at in halos]
             + [pl.BlockSpec(memory_space=pl.ANY)] * len(extra),
             out_specs=pl.BlockSpec((count, block), lambda i, *_: (0, start + i)),
             scratch_shapes=[
@@ -270,23 +279,43 @@
     return high, middle, low
 
 
-def attend_kernel(where_ref, lengths_ref, own_ref, near_ref, far_ref, prior_ref,
-                  out_ref, out_peak_ref, out_total_ref, near_out_ref, far_out_ref, bias, peaks, totals):
+def attend_kernel(groups, priors, tails, where_ref, lengths_ref, own_ref, *refs):
+    sent = [g for g in groups if g]
+    *refs, bias, peaks, totals = refs
+    query_refs = dict(zip(sent, refs))
+    prior_refs = refs[len(sent):len(sent) + priors]
+    tail_refs = refs[len(sent) + priors:len(sent) + priors + tails]
+    outs = refs[len(sent) + priors + tails:]
+    if 0 in groups:
+        out_ref, out_peak_ref, out_total_ref, *outs = outs
+    sent_refs = dict(zip(sent, outs))
     count = own_ref.shape[1]
-    width = near_ref.shape[1]
+    width = own_ref.shape[2]
     heads = width // LANES
     scale = 1.0 / math.sqrt(LANES)
     index = where_ref[0]
     ends = bounds_of(lengths_ref)
     pivot = index == 1
 
-    def mask(groups, keys, first):
+    def mask(active, keys, first):
         row = lax.broadcasted_iota(jnp.int32, (count, keys), 0)
         source = first + lax.broadcasted_iota(jnp.int32, (count, keys), 1)
-        for which in range(groups):
+        for at, which in enumerate(active):
             place = (index + which) * count + row
             ok = (source <= place) & (source >= start_of(place, ends))
-            bias[which * count:(which + 1) * count, 0:keys] = jnp.where(ok, 0.0, NEG)
+            bias[at * count:(at + 1) * count, 0:keys] = jnp.where(ok, 0.0, NEG)
+
+    def queries_of(active, lanes):
+        parts = [query_refs[g][:, lanes] if g else own_ref[0, :, lanes] for g in active]
+        return jnp.concatenate(parts, axis=0)
+
+    def store(active, lanes, mixed):
+        for at, g in enumerate(active):
+            value = mixed[at * count:(at + 1) * count]
+            if g:
+                sent_refs[g][0:count, lanes] = value.astype(sent_refs[g].dtype)
+            else:
+                out_ref[:, lanes] = value
 
     rate = scale * math.log2(math.e)
 
@@ -306,96 +335,98 @@
     def several(one, rows):
         peaks[0:rows] = jnp.zeros((rows, LANES), jnp.float32)
         totals[0:rows] = jnp.zeros((rows, LANES), jnp.float32)
-        def body(i, carry):
-            peak_of, total_of = peaks[0:rows], totals[0:rows]
-            for u in range(HEADS_AT_ONCE):
-                h = i * HEADS_AT_ONCE + u
-                peak, total = one(h)
-                peak_of = jnp.where(lane == h, peak, peak_of)
-                total_of = jnp.where(lane == h, total, total_of)
-            peaks[0:rows], totals[0:rows] = peak_of, total_of
-            return carry
-        lax.fori_loop(0, heads // HEADS_AT_ONCE, body, 0)
+        for prior, begin in zip(prior_refs, range(0, heads, heads // priors)):
+            def body(i, carry):
+                peak_of, total_of = peaks[0:rows], totals[0:rows]
+                for u in range(HEADS_AT_ONCE):
+                    here = i * HEADS_AT_ONCE + u
+                    h = begin + here
+                    peak, total = one(pl.ds(pl.multiple_of(h * LANES, LANES), LANES), prior, here)
+                    peak_of = jnp.where(lane == h, peak, peak_of)
+                    total_of = jnp.where(lane == h, total, total_of)
+                peaks[0:rows], totals[0:rows] = peak_of, total_of
+                return carry
+            lax.fori_loop(0, heads // priors // HEADS_AT_ONCE, body, 0)
+
+    def run(active, before):
+        mask(active, (1 + before) * count, (index - before) * count)
+
+        def one(lanes, prior, h):
+            keys, values = own_ref[1, :, lanes], own_ref[2, :, lanes]
+            if before:
+                here = pl.ds(pl.multiple_of(h * LANES, LANES), LANES)
+                beside = pl.ds(pl.multiple_of(prior.shape[1] // 2 + h * LANES, LANES), LANES)
+                keys = jnp.concatenate([prior[0:count, here], keys], axis=0)
+                values = jnp.concatenate([prior[0:count, beside], values], axis=0)
+            mixed, peak, total = softmax(queries_of(active, lanes), keys, values)
+            store(active, lanes, mixed)
+            return peak, total
+
+        several(one, len(active) * count)
 
     @pl.when(pivot)
     def _():
-        mask(3, 2 * count, (index - 1) * count)
-        def one(h):
-            lanes = pl.ds(pl.multiple_of(h * LANES, LANES), LANES)
-            queries = jnp.concatenate([own_ref[0, :, lanes], near_ref[:, lanes], far_ref[:, lanes]], axis=0)
-            if len(prior_ref.shape) == 3:
-                before = prior_ref[0, :, lanes], prior_ref[1, :, lanes]
-            else:
-                beside = pl.ds(pl.multiple_of(width + h * LANES, LANES), LANES)
-                before = prior_ref[0:count, lanes], prior_ref[0:count, beside]
-            keys = jnp.concatenate([before[0], own_ref[1, :, lanes]], axis=0)
-            values = jnp.concatenate([before[1], own_ref[2, :, lanes]], axis=0)
-            mixed, peak, total = softmax(queries, keys, values)
-            out_ref[:, lanes] = mixed[0:count]
-            near_out_ref[:, lanes] = mixed[count:2 * count].astype(near_out_ref.dtype)
-            far_out_ref[:, lanes] = mixed[2 * count:].astype(far_out_ref.dtype)
-            return peak, total
-        several(one, 3 * count)
+        run(groups, 1)
 
     @pl.when(jnp.logical_not(pivot))
     def _():
-        mask(2, count, index * count)
-        def one(h):
-            lanes = pl.ds(pl.multiple_of(h * LANES, LANES), LANES)
-            queries = jnp.concatenate([own_ref[0, :, lanes], near_ref[:, lanes]], axis=0)
-            mixed, peak, total = softmax(queries, own_ref[1, :, lanes], own_ref[2, :, lanes])
-            out_ref[:, lanes] = mixed[0:count]
-            near_out_ref[:, lanes] = mixed[count:].astype(near_out_ref.dtype)
-            return peak, total
-        several(one, 2 * count)
-
-    out_peak_ref[...] = peaks[0:count]
-    out_total_ref[...] = totals[0:count]
-    for which, ref in ((1, near_out_ref), (2, far_out_ref)):
-        rows = slice(which * count, (which + 1) * count)
-        packed = jnp.zeros((count, LANES), jnp.float32)
-        for at, piece in enumerate(parts_of(peaks[rows]) + parts_of(totals[rows])):
-            piece = piece.astype(jnp.float32)
-            packed = packed + (pltpu.roll(piece, at * SPREAD, 1) if at else piece)
-        ref[:, width:width + LANES] = packed.astype(ref.dtype)
-
-def attend_part(index, lengths, blocks, near, far, prior, first, width, at):
+        run([g for g in groups if g < 2], 0)
+
+    if 0 in groups:
+        out_peak_ref[...] = peaks[0:count]
+        out_total_ref[...] = totals[0:count]
+    for at, g in enumerate(groups):
+        if g:
+            rows = slice(at * count, (at + 1) * count)
+            packed = jnp.zeros((count, LANES), jnp.float32)
+            for n, piece in enumerate(parts_of(peaks[rows]) + parts_of(totals[rows])):
+                piece = piece.astype(jnp.float32)
+                packed = packed + (pltpu.roll(piece, n * SPREAD, 1) if n else piece)
+            sent_refs[g][0:count, width:width + LANES] = packed.astype(sent_refs[g].dtype)
+
+    for tail_ref, g in zip(tail_refs, sent):
+        @pl.when(index == 0)
+        def _():
+            sent_refs[g][:, 0:width] = tail_ref[...]
+
+
+def attend_part(index, lengths, blocks, groups, queries, priors, part, tails=()):
     slots, count, _ = blocks.shape
+    width = queries[0].shape[1]
+    rows = tails[0][0].shape[0] if tails else count
     whole = lambda i, *_: (0, 0)
+    kind = queries[0].dtype
+    out_shape = [jax.ShapeDtypeStruct((rows, width + LANES), kind) for _ in queries]
+    out_specs = [pl.BlockSpec((rows, width + LANES), whole) for _ in queries]
+    if 0 in groups:
+        shapes = [(count, width), (count, LANES), (count, LANES)]
+        out_shape = [pltpu.HBM(shape, jnp.float32) for shape in shapes] + out_shape
+        out_specs = [pl.BlockSpec(shape, whole) for shape in shapes] + out_specs
+
+    def tail_spec(at):
+        return pl.BlockSpec((rows, width), lambda i, *_: (0, at))
+
     return pl.pallas_call(
-        attend_kernel,
-        out_shape=(
-            jax.ShapeDtypeStruct((count, width), jnp.float32),
-            jax.ShapeDtypeStruct((count, LANES), jnp.float32),
-            jax.ShapeDtypeStruct((count, LANES), jnp.float32),
-            jax.ShapeDtypeStruct((count, width + LANES), near.dtype),
-            jax.ShapeDtypeStruct((count, width + LANES), near.dtype),
-        ),
+        partial(attend_kernel, groups, len(priors), len(tails)),
+        out_shape=out_shape,
         grid_spec=pltpu.PrefetchScalarGridSpec(
             num_scalar_prefetch=2,
             grid=(1,),
-            in_specs=[
-                pl.BlockSpec((slots, count, width), lambda i, *_: (0, 0, first)),
-                pl.BlockSpec((count, width), lambda i, *_: (0, at)),
-                pl.BlockSpec((count, width), lambda i, *_: (0, at)),
-                pl.BlockSpec(prior.shape, lambda i, *_: (0,) * prior.ndim),
-            ],
-            out_specs=(
-                pl.BlockSpec((count, width), whole),
-                pl.BlockSpec((count, LANES), whole),
-                pl.BlockSpec((count, LANES), whole),
-                pl.BlockSpec((count, width + LANES), whole),
-                pl.BlockSpec((count, width + LANES), whole),
-            ),
+            in_specs=[pl.BlockSpec((slots, count, width), lambda i, *_: (0, 0, part))]
+            + [pl.BlockSpec((count, width), whole) for _ in queries]
+            + [pl.BlockSpec(prior.shape, whole) for prior in priors]
+            + [tail_spec(at) for _, at in tails],
+            out_specs=out_specs,
             scratch_shapes=[
-                pltpu.VMEM((3 * count, 2 * count), jnp.float32),
-                pltpu.VMEM((3 * count, LANES), jnp.float32),
-                pltpu.VMEM((3 * count, LANES), jnp.float32),
+                pltpu.VMEM((len(groups) * count, 2 * count), jnp.float32),
+                pltpu.VMEM((len(groups) * count, LANES), jnp.float32),
+                pltpu.VMEM((len(groups) * count, LANES), jnp.float32),
             ],
         ),
-        compiler_params=pltpu.CompilerParams(vmem_limit_bytes=48 << 20),
+        compiler_params=pltpu.CompilerParams(vmem_limit_bytes=24 << 20),
         name="attend_part",
-    )(index, lengths, blocks, near, far, prior)
+    )(index, lengths, blocks, *queries, *priors, *[array for array, _ in tails])
+
 
 def merge_kernel(where_ref, own_ref, own_peak_ref, own_total_ref, near_ref, far_ref, *refs):
     out_ref = refs[-1]
@@ -468,36 +499,55 @@
 def layer_four(index, lengths, inputs, short_filter, base, blocks):
     reach = base.shape[1]
     width = blocks.shape[2]
-    part = width // CHUNKS
+    half = width // 2
     after = lax.optimization_barrier
-    moved = []
-    for c in range(CHUNKS):
-        cols = slice(c * part, (c + 1) * part)
-        prior = lax.ppermute(blocks[1:3, :, cols], "ctx", [(0, 1)])
-        near = lax.ppermute(blocks[0, :, cols], "ctx", [(2, 1), (3, 2)])
-        far = lax.ppermute(blocks[0, :, cols], "ctx", [(3, 1)])
-        moved.append((near, far, prior))
-    (tail,) = mixer_tail(index, lengths, inputs, short_filter, reach, 0, width)
-    halo = lax.ppermute(tail, "ctx", [(0, 1), (1, 2), (2, 3)])
-    sent, last = [], None
-    for c in range(CHUNKS):
-        near, far, prior = moved[c]
-        if c:
-            near, far, prior, _ = after((near, far, prior, last))
-        own, peak, total, near_out, far_out = attend_part(
-            index, lengths, blocks, near, far, prior, c, part, 0
-        )
-        last = near_out
-        near_in = lax.ppermute(near_out, "ctx", [(1, 2), (2, 3)])
-        far_in = lax.ppermute(far_out, "ctx", [(1, 3)])
-        sent.append((own, peak, total, near_in, far_in))
-    halo, _ = after((halo, last))
-    hyena_out = mixer(index, lengths, inputs, short_filter, base, tail, [halo])
-    held = None
-    for c in range(CHUNKS):
-        if c == CHUNKS - 1:
-            held, hyena_out = after((held, hyena_out))
-        held = merge_part(index, *sent[c], c, width, held)
+
+    def queries(held, c):
+        mine = held[0, :, c * half:(c + 1) * half]
+        near = lax.ppermute(mine, "ctx", [(2, 1), (3, 2)])
+        return near, lax.ppermute(mine, "ctx", [(3, 1)])
+
+    def keys(held, c):
+        cols = slice(c * half, (c + 1) * half)
+        beside = jnp.concatenate([held[1, :, cols], held[2, :, cols]], axis=1)
+        return lax.ppermute(beside, "ctx", [(0, 1)])
+
+    def send(part, axis_pairs):
+        return lax.ppermute(part, "ctx", axis_pairs)
+
+    forward = [(0, 1), (1, 2), (2, 3)]
+    near_a, far_a = queries(blocks, 0)
+    prior_a = keys(blocks, 0)
+    tail, message = mixer_tail(index, lengths, inputs, short_filter, reach, blocks, 1)
+    moved = send(message, forward)
+    held, near_a, tail = after((blocks, near_a, tail))
+    near_b = send(held[0, :, half:], [(2, 1), (3, 2)])
+    held, far_a, prior_a = after((held, far_a, prior_a))
+    far_b = send(held[0, :, half:], [(3, 1)])
+    *own_a, near_out, far_out = attend_part(
+        index, lengths, blocks, (0, 1, 2), [near_a, far_a], [prior_a], 0, [(tail, 0), (tail, 1)]
+    )
+    near_in_a = send(near_out, forward)
+    far_in_a = send(far_out, [(0, 1), (1, 3)])
+    near_b, far_b, moved, _ = after((near_b, far_b, moved, far_out))
+    *own_b, near_out, far_out = attend_part(
+        index, lengths, blocks, (0, 1, 2), [near_b, far_b], [moved], 1
+    )
+    near_in_b = send(near_out, forward[1:])
+    far_out, far_in_a = after((far_out, far_in_a))
+    far_in_b = send(far_out, [(1, 3)])
+    halo, far_in_a, _ = after((moved, far_in_a, near_out))
+    hyena_out = mixer(
+        index, lengths, inputs, short_filter, base, tail, [(halo, half), (far_in_a, 0)], half, half
+    )
+    far_in_a, near_in_a, _ = after((far_in_a, near_in_a, hyena_out))
+    held = merge_part(index, *own_a, near_in_a, far_in_a, 0, width, None)
+    tail, _ = after((tail, held))
+    hyena_out = mixer(
+        index, lengths, inputs, short_filter, base, tail, [(halo, 0), (near_in_a, 0)], 0, half, hyena_out
+    )
+    held, hyena_out = after((held, hyena_out))
+    held = merge_part(index, *own_b, near_in_b, far_in_b, 1, width, held)
     return hyena_out, held
 
 
@@ -537,9 +587,11 @@
     if size == 4:
         hyena_out, attn_out = layer_four(index, lengths, inputs, short_filter, base, blocks)
     else:
-        (tail,) = mixer_tail(index, lengths, inputs, short_filter, reach, 0, inputs.shape[2])
+        (tail,) = mixer_tail(index, lengths, inputs, short_filter, reach)
         halo = lax.ppermute(tail, "ctx", [(i, i + 1) for i in range(size - 1)])
-        hyena_out = mixer(index, lengths, inputs, short_filter, base, tail, [halo])
+        hyena_out = mixer(
+            index, lengths, inputs, short_filter, base, tail, [(halo, 0)], 0, inputs.shape[2]
+        )
         attn_out = attend_any(lengths, blocks, heads)
     return (hyena_out[None], attn_out[None])
 

time: 112 us -> 110 us (0.982)
  waiting for transfers between devices: 36.7 us -> 31.9 us
  starting transfers between devices: 21.6 us -> 26.4 us
  local copies, waits for them, and re-layouts: 11.5 us -> 6.91 us
  Pallas kernels: 39.6 us -> 41.6 us
    ppermute x11 -> x10, waiting for transfers between devices: 36.7 us -> 31.9 us  [the longest x7 21.4 us: send(): return lax.ppermute(part, 'ctx', axis_pairs)]
    ppermute x11 -> x10, starting transfers between devices: 21.6 us -> 26.4 us  [the longest x7 19.5 us: send(): return lax.ppermute(part, 'ctx', axis_pairs)]
    slice x1 -> x0, local copies, waits for them, and re-layouts: 3.32 us -> none  [layer_four(): prior = lax.ppermute(blocks[1:3, :, cols], 'ctx', [(0, 1)])]
    unnamed x21 -> x15, local copies, waits for them, and re-layouts: 5.49 us -> 4.16 us
    pallas_call x3 -> x4, Pallas kernels: 25.7 us -> 26.7 us  [the longest x2 15.8 us: mixer(): pl.pallas_call(partial(mixer_kernel, len(halos)), out_shape=jax.ShapeDtyp...]
    squeeze x1 -> x3, local copies, waits for them, and re-layouts: 2.4 us -> 2.47 us  [the longest x1 2.38 us: keys(): beside = jnp.concatenate([held[1, :, cols], held[2, :, cols]], axis=1)]
  transfers between devices with their start and end apart: 11 -> 10, of which waited for: 5 -> 5; matrix products, arithmetic and copies ran while one was open for 3% -> 2% of each run, Pallas kernels for 32% -> 35%
where the time goes in v2:
time: 110 us; the launch traced here: 109 us
  Pallas kernels  41.6 us (38%)
  waiting for transfers between devices  31.9 us (29%)
  starting transfers between devices  26.4 us (24%)
  local copies, waits for them, and re-layouts  6.91 us (6%)
  other arithmetic  1.88 us (2%)
    ppermute x7, waiting for transfers between devices, send(): return lax.ppermute(part, 'ctx', axis_pairs)  21.4 us
    ppermute x7, starting transfers between devices, send(): return lax.ppermute(part, 'ctx', axis_pairs)  19.5 us
    pallas_call x2, Pallas kernels, mixer(): pl.pallas_call(partial(mixer_kernel, len(halos)), out_shape=jax.ShapeDtyp...  15.8 us
    pallas_call x2, Pallas kernels, attend_part(): pl.pallas_call(partial(attend_kernel, groups, len(priors), len(tails)), o...  10.9 us
    ppermute x1, waiting for transfers between devices, queries(): return (near, lax.ppermute(mine, 'ctx', [(3, 1)]))  8.2 us
    pallas_call x1, Pallas kernels, mixer_tail(): pl.pallas_call(tail_kernel, out_shape=(out,) * (1 + len(extra)), grid_spe...  7.48 us
    pallas_call x2, Pallas kernels, merge_part(): pl.pallas_call(merge_kernel, out_shape=jax.ShapeDtypeStruct((count, full)...  7.4 us
    unnamed x15, local copies, waits for them, and re-layouts  4.16 us
  transfers between devices with their start and end apart: 10, of which 5 were waited for; matrix products, arithmetic and copies ran while one was open for 2% of the time, Pallas kernels for 35%

profile of v2, /device:TPU:24, one launch (start us, length us, event | category | flops | bytes accessed | tf_op | source)
XLA Modules:
  0.0 109.5 jit_solution(7327860982736840061)
XLA Ops:
  0.6 2.4 %slice_bitcast_fusion.1 = (bf16[144,2048]{1,0:T(8,128)(2,1)S(1)}, bf16[144,2048]{1,0:T(8,128)(2,1)S(1)}, bf16[144,2048]{1,0:T(8,128)(2,1)}) fusion(bf16[3,144,4096]{2,1,0:T(8,128)(2,1)} %bitcast.22), kind=kLoop, calls=%fused_computation.2 | loop fusion | bytes 3538944 | tf_op jit(solution)/shard_map/squeeze | solution.py:512
  3.0 1.1 pad_maximum_fusion
  4.1 1.7 %collective-permute-start.2 = (bf16[144,4096]{1,0:T(8,128)(2,1)}, bf16[144,4096]{1,0:T(8,128)(2,1)}, u32[]{:S(2)}, u32[]{:S(2)}) collective-permute-start(bf16[144,4096]{1,0:T(8,128)(2,1)} %pad_maximum_fusion), channel_id=1, source_target_pairs={{0,4},{1,5},{2,6},{3,7},{16,20},{17,21},{18,22},{19,23}} | collective-permute-start | bytes 3538952 | tf_op jit(solution)/shard_map/ppermute | solution.py:513
  5.8 3.2 %collective-permute-start = (bf16[144,2048]{1,0:T(8,128)(2,1)}, bf16[144,2048]{1,0:T(8,128)(2,1)}, u32[]{:S(2)}, u32[]{:S(2)}) collective-permute-start(bf16[144,2048]{1,0:T(8,128)(2,1)} %get-tuple-element.64), channel_id=1, source_target_pairs={{8,4},{12,8},{9,5},{13,9},{10,6},{14,10},{11,7},{15,11},{24,20},{2... | collective-permute-start | bytes 1769480 | tf_op jit(solution)/shard_map/ppermute | solution.py:507
  9.0 2.1 %collective-permute-start.1 = (bf16[144,2048]{1,0:T(8,128)(2,1)}, bf16[144,2048]{1,0:T(8,128)(2,1)}, u32[]{:S(2)}, u32[]{:S(2)}) collective-permute-start(bf16[144,2048]{1,0:T(8,128)(2,1)} %get-tuple-element.64), channel_id=1, source_target_pairs={{12,4},{13,5},{14,6},{15,7},{28,20},{29,21},{30,22},{31,23}} | collective-permute-start | bytes 1769480 | tf_op jit(solution)/shard_map/ppermute | solution.py:508
  11.1 7.5 %mixer_tail.1 = (bf16[152,4096]{1,0:T(8,128)(2,1)}, bf16[152,4096]{1,0:T(8,128)(2,1)}) custom-call(s32[1]{0:T(128)} %bitcast.where_ref, s32[1,4]{1,0:T(1,128)} %lengths_ref.9, bf16[3,144,4096]{2,1,0:T(8,128)(2,1)} %bitcast.28, bf16[3,144,4096]{2,1,0:T(8,128)(2,1)} %bitcast.29, bf16[3,144,4096]{2,1,0:T(8,128)(2,1)} %bitcast.30, bf16[3,7,4096]{2,1,0:T(8,128)(2,1)} %taps_ref.5, ...), custom_call_target="tpu_custom_call" | custom-call | tf_op jit(solution)/shard_map/mixer_tail/pallas_call | solution.py:112
  18.6 1.3 %collective-permute-start.5 = (bf16[152,4096]{1,0:T(8,128)(2,1)}, bf16[152,4096]{1,0:T(8,128)(2,1)S(1)}, u32[]{:S(2)}, u32[]{:S(2)}) collective-permute-start(bf16[152,4096]{1,0:T(8,128)(2,1)} %get-tuple-element.42), channel_id=1, source_target_pairs={{0,4},{4,8},{8,12},{1,5},{5,9},{9,13},{2,6},{6,10},{10,14},{3,7},{... | collective-permute-start | bytes 3735560 | tf_op jit(solution)/shard_map/ppermute | solution.py:516
  19.8 2.3 %collective-permute-done.refs_0_ = bf16[144,2048]{1,0:T(8,128)(2,1)} collective-permute-done((bf16[144,2048]{1,0:T(8,128)(2,1)}, bf16[144,2048]{1,0:T(8,128)(2,1)}, u32[]{:S(2)}, u32[]{:S(2)}) %collective-permute-start) | collective-permute-done | bytes 589856 | tf_op jit(solution)/shard_map/ppermute | solution.py:507
  22.2 4.4 %collective-permute-start.3 = (bf16[144,2048]{1,0:T(8,128)(2,1)S(1)}, bf16[144,2048]{1,0:T(8,128)(2,1)S(1)}, u32[]{:S(2)}, u32[]{:S(2)}) collective-permute-start(bf16[144,2048]{1,0:T(8,128)(2,1)S(1)} %slice_bitcast_fusion.4), channel_id=1, source_target_pairs={{8,4},{12,8},{9,5},{13,9},{10,6},{14,10},{11,7},{15,11},{24,20},{2... | collective-permute-start | bytes 1769480 | tf_op jit(solution)/shard_map/ppermute | solution.py:516
  26.6 8.2 %collective-permute-done.1.refs_1_ = bf16[144,2048]{1,0:T(8,128)(2,1)} collective-permute-done((bf16[144,2048]{1,0:T(8,128)(2,1)}, bf16[144,2048]{1,0:T(8,128)(2,1)}, u32[]{:S(2)}, u32[]{:S(2)}) %collective-permute-start.1) | collective-permute-done | bytes 589856 | tf_op jit(solution)/shard_map/ppermute | solution.py:508
  34.8 1.3 %copy-done.1 = bf16[152,4096]{1,0:T(8,128)(2,1)S(1)} copy-done((bf16[152,4096]{1,0:T(8,128)(2,1)S(1)}, bf16[152,4096]{1,0:T(8,128)(2,1)}, u32[]{:S(2)}) %copy-start.1) | copy-done | bytes 1245208
  36.1 6.2 %attend_part.2 = (f32[144,2048]{1,0:T(8,128)}, f32[144,128]{1,0:T(8,128)}, f32[144,128]{1,0:T(8,128)}, bf16[152,2176]{1,0:T(8,128)(2,1)}, bf16[152,2176]{1,0:T(8,128)(2,1)S(1)}) custom-call(s32[1]{0:T(128)} %bitcast.where_ref, s32[1,4]{1,0:T(1,128)S(1)} %copy-done.3, bf16[3,144,4096]{2,1,0:T(8,128)(2,1)S(1)} %bitcast.25, ...), custom_call_target="tpu_custom_call" | custom-call | tf_op jit(solution)/shard_map/attend_part/pallas_call | solution.py:409
  42.4 1.3 %collective-permute-start.6 = (bf16[152,2176]{1,0:T(8,128)(2,1)S(1)}, bf16[152,2176]{1,0:T(8,128)(2,1)S(1)}, u32[]{:S(2)}, u32[]{:S(2)}) collective-permute-start(bf16[152,2176]{1,0:T(8,128)(2,1)S(1)} %get-tuple-element.43), channel_id=1, source_target_pairs={{0,4},{4,12},{1,5},{5,13},{2,6},{6,14},{3,7},{7,15},{16,20},{20,28... | collective-permute-start | bytes 1984520 | tf_op jit(solution)/shard_map/ppermute | solution.py:516
  43.7 8.6 %collective-permute-start.4 = (bf16[144,2048]{1,0:T(8,128)(2,1)S(1)}, bf16[144,2048]{1,0:T(8,128)(2,1)S(1)}, u32[]{:S(2)}, u32[]{:S(2)}) collective-permute-start(bf16[144,2048]{1,0:T(8,128)(2,1)S(1)} %slice_bitcast_fusion.3), channel_id=1, source_target_pairs={{12,4},{13,5},{14,6},{15,7},{28,20},{29,21},{30,22},{31,23}} | collective-permute-start | bytes 1769480 | tf_op jit(solution)/shard_map/ppermute | solution.py:516
  52.4 1.3 %collective-permute-start.7 = (bf16[152,2176]{1,0:T(8,128)(2,1)}, bf16[152,2176]{1,0:T(8,128)(2,1)}, u32[]{:S(2)}, u32[]{:S(2)}) collective-permute-start(bf16[152,2176]{1,0:T(8,128)(2,1)} %get-tuple-element.51), channel_id=1, source_target_pairs={{0,4},{4,8},{8,12},{1,5},{5,9},{9,13},{2,6},{6,10},{10,14},{3,7},{... | collective-permute-start | bytes 1984520 | tf_op jit(solution)/shard_map/ppermute | solution.py:516
  53.7 8.2 %collective-permute-done.5.refs_2_.refs_0_ = bf16[152,4096]{1,0:T(8,128)(2,1)S(1)} collective-permute-done((bf16[152,4096]{1,0:T(8,128)(2,1)}, bf16[152,4096]{1,0:T(8,128)(2,1)S(1)}, u32[]{:S(2)}, u32[]{:S(2)}) %collective-permute-start.5) | collective-permute-done | bytes 1245216 | tf_op jit(solution)/shard_map/ppermute | solution.py:516
  62.9 4.7 %attend_part.3 = (f32[144,2048]{1,0:T(8,128)}, f32[144,128]{1,0:T(8,128)}, f32[144,128]{1,0:T(8,128)}, bf16[144,2176]{1,0:T(8,128)(2,1)}, bf16[144,2176]{1,0:T(8,128)(2,1)}) custom-call(s32[1]{0:T(128)} %bitcast.where_ref, s32[1,4]{1,0:T(1,128)S(1)} %copy-done.3, bf16[3,144,4096]{2,1,0:T(8,128)(2,1)S(1)} %bitcast.27, ...), custom_call_target="tpu_custom_call" | custom-call | tf_op jit(solution)/shard_map/attend_part/pallas_call | solution.py:409
  67.5 1.3 %collective-permute-start.8 = (bf16[144,2176]{1,0:T(8,128)(2,1)}, bf16[144,2176]{1,0:T(8,128)(2,1)S(1)}, u32[]{:S(2)}, u32[]{:S(2)}) collective-permute-start(bf16[144,2176]{1,0:T(8,128)(2,1)} %get-tuple-element.49), channel_id=1, source_target_pairs={{4,8},{8,12},{5,9},{9,13},{6,10},{10,14},{7,11},{11,15},{20,24},{2... | collective-permute-start | bytes 1880072 | tf_op jit(solution)/shard_map/ppermute | solution.py:516
  69.7 1.3 %collective-permute-start.9 = (bf16[144,2176]{1,0:T(8,128)(2,1)}, bf16[144,2176]{1,0:T(8,128)(2,1)S(1)}, u32[]{:S(2)}, u32[]{:S(2)}) collective-permute-start(bf16[144,2176]{1,0:T(8,128)(2,1)} %get-tuple-element.60), channel_id=1, source_target_pairs={{4,12},{5,13},{6,14},{7,15},{20,28},{21,29},{22,30},{23,31}} | collective-permute-start | bytes 1880072 | tf_op jit(solution)/shard_map/ppermute | solution.py:516
  73.0 7.9 %mixer.2.refs_2_ = bf16[144,4096]{1,0:T(8,128)(2,1)} custom-call(s32[1]{0:T(128)} %bitcast.where_ref, s32[1,4]{1,0:T(1,128)} %lengths_ref.9, bf16[3,144,4096]{2,1,0:T(8,128)(2,1)} %bitcast.31, bf16[3,144,4096]{2,1,0:T(8,128)(2,1)} %bitcast.32, bf16[3,144,4096]{2,1,0:T(8,128)(2,1)} %bitcast.33, bf16[3,7,4096]{2,1,0:T(8,128)(2,1)} %taps_ref.5, ...), custom_call_target="tpu_custom_call" | custom-call | tf_op jit(solution)/shard_map/mixer/pallas_call | solution.py:242
  80.9 3.7 %merge_part.2.refs_0_ = bf16[144,4096]{1,0:T(8,128)(2,1)} custom-call(s32[1]{0:T(128)} %bitcast.where_ref, f32[144,2048]{1,0:T(8,128)} %get-tuple-element.38.own_ref, f32[144,128]{1,0:T(8,128)} %get-tuple-element.39.own_peak_ref, f32[144,128]{1,0:T(8,128)} %get-tuple-element.40.own_total_ref, bf16[152,2176]{1,0:T(8,128)(2,1)} %collective-permute-done.7.near_ref.refs_1_, ...), custom_call_target="tpu_custom_call" | custom-call | tf_op jit(solution)/shard_map/merge_part/pallas_call | solution.py:478
  84.6 7.9 %mixer.3 = bf16[144,4096]{1,0:T(8,128)(2,1)} custom-call(s32[1]{0:T(128)} %bitcast.where_ref, s32[1,4]{1,0:T(1,128)} %lengths_ref.9, bf16[3,144,4096]{2,1,0:T(8,128)(2,1)} %bitcast.34, bf16[3,144,4096]{2,1,0:T(8,128)(2,1)} %bitcast.35, bf16[3,144,4096]{2,1,0:T(8,128)(2,1)} %bitcast.36, ...), custom_call_target="tpu_custom_call", output_to_operand_aliasing={{}: (10, {})} | custom-call | tf_op jit(solution)/shard_map/mixer/pallas_call | solution.py:242
  92.5 12.2 %collective-permute-done.8.near_ref = bf16[144,2176]{1,0:T(8,128)(2,1)S(1)} collective-permute-done((bf16[144,2176]{1,0:T(8,128)(2,1)}, bf16[144,2176]{1,0:T(8,128)(2,1)S(1)}, u32[]{:S(2)}, u32[]{:S(2)}) %collective-permute-start.8) | collective-permute-done | bytes 626720 | tf_op jit(solution)/shard_map/ppermute | solution.py:516
  105.8 3.7 %merge_part.3 = bf16[144,4096]{1,0:T(8,128)(2,1)} custom-call(s32[1]{0:T(128)} %bitcast.where_ref, f32[144,2048]{1,0:T(8,128)} %get-tuple-element.57.own_ref, f32[144,128]{1,0:T(8,128)} %get-tuple-element.58.own_peak_ref, f32[144,128]{1,0:T(8,128)} %get-tuple-element.59.own_total_ref, bf16[144,2176]{1,0:T(8,128)(2,1)} %copy-done.5, ...), custom_call_target="tpu_custom_call", output_to_operand_aliasing={{}: (6, {})} | custom-call | tf_op jit(solution)/shard_map/merge_part/pallas_call | solution.py:478
  (26 shorter events, 5.1 us)
Async XLA Ops:
  4.1 30.7 %collective-permute-start.2 = (bf16[144,4096]{1,0:T(8,128)(2,1)}, bf16[144,4096]{1,0:T(8,128)(2,1)}, u32[]{:S(2)}, u32[]{:S(2)}) collective-permute-start(bf16[144,4096]{1,0:T(8,128)(2,1)} %pad_maximum_fusion), channel_id=1, source_target_pairs={{0,4},{1,5},{2,6},{3,7},{16,20},{17,21},{18,22},{19,23}} | collective-permute-start | bytes 3538952 | tf_op jit(solution)/shard_map/ppermute | solution.py:513
  5.8 16.4 %collective-permute-start = (bf16[144,2048]{1,0:T(8,128)(2,1)}, bf16[144,2048]{1,0:T(8,128)(2,1)}, u32[]{:S(2)}, u32[]{:S(2)}) collective-permute-start(bf16[144,2048]{1,0:T(8,128)(2,1)} %get-tuple-element.64), channel_id=1, source_target_pairs={{8,4},{12,8},{9,5},{13,9},{10,6},{14,10},{11,7},{15,11},{24,20},{2... | collective-permute-start | bytes 1769480 | tf_op jit(solution)/shard_map/ppermute | solution.py:507
  9.0 25.9 %collective-permute-start.1 = (bf16[144,2048]{1,0:T(8,128)(2,1)}, bf16[144,2048]{1,0:T(8,128)(2,1)}, u32[]{:S(2)}, u32[]{:S(2)}) collective-permute-start(bf16[144,2048]{1,0:T(8,128)(2,1)} %get-tuple-element.64), channel_id=1, source_target_pairs={{12,4},{13,5},{14,6},{15,7},{28,20},{29,21},{30,22},{31,23}} | collective-permute-start | bytes 1769480 | tf_op jit(solution)/shard_map/ppermute | solution.py:508
  11.1 11.1 %copy-start = (bf16[1,144,3,4096]{3,1,2,0:T(8,128)(2,1)S(1)}, bf16[1,144,3,4096]{3,1,2,0:T(8,128)(2,1)}, u32[]{:S(2)}) copy-start(bf16[1,144,3,4096]{3,1,2,0:T(8,128)(2,1)} %param.8) | copy-start | bytes 10616836
  11.1 23.8 %copy-start.3 = (s32[1,4]{1,0:T(1,128)S(1)}, s32[1,4]{1,0:T(1,128)}, u32[]{:S(2)}) copy-start(s32[1,4]{1,0:T(1,128)} %lengths_ref.9) | copy-start | bytes 52
  18.6 43.3 %collective-permute-start.5 = (bf16[152,4096]{1,0:T(8,128)(2,1)}, bf16[152,4096]{1,0:T(8,128)(2,1)S(1)}, u32[]{:S(2)}, u32[]{:S(2)}) collective-permute-start(bf16[152,4096]{1,0:T(8,128)(2,1)} %get-tuple-element.42), channel_id=1, source_target_pairs={{0,4},{4,8},{8,12},{1,5},{5,9},{9,13},{2,6},{6,10},{10,14},{3,7},{... | collective-permute-start | bytes 3735560 | tf_op jit(solution)/shard_map/ppermute | solution.py:516
  22.2 31.4 %collective-permute-start.3 = (bf16[144,2048]{1,0:T(8,128)(2,1)S(1)}, bf16[144,2048]{1,0:T(8,128)(2,1)S(1)}, u32[]{:S(2)}, u32[]{:S(2)}) collective-permute-start(bf16[144,2048]{1,0:T(8,128)(2,1)S(1)} %slice_bitcast_fusion.4), channel_id=1, source_target_pairs={{8,4},{12,8},{9,5},{13,9},{10,6},{14,10},{11,7},{15,11},{24,20},{2... | collective-permute-start | bytes 1769480 | tf_op jit(solution)/shard_map/ppermute | solution.py:516
  34.8 1.3 %copy-start.1 = (bf16[152,4096]{1,0:T(8,128)(2,1)S(1)}, bf16[152,4096]{1,0:T(8,128)(2,1)}, u32[]{:S(2)}) copy-start(bf16[152,4096]{1,0:T(8,128)(2,1)} %get-tuple-element.55.refs_3_.refs_4_.tail_ref) | copy-start | bytes 3735556
  42.4 26.4 %collective-permute-start.6 = (bf16[152,2176]{1,0:T(8,128)(2,1)S(1)}, bf16[152,2176]{1,0:T(8,128)(2,1)S(1)}, u32[]{:S(2)}, u32[]{:S(2)}) collective-permute-start(bf16[152,2176]{1,0:T(8,128)(2,1)S(1)} %get-tuple-element.43), channel_id=1, source_target_pairs={{0,4},{4,12},{1,5},{5,13},{2,6},{6,14},{3,7},{7,15},{16,20},{20,28... | collective-permute-start | bytes 1984520 | tf_op jit(solution)/shard_map/ppermute | solution.py:516
  43.7 19.1 %collective-permute-start.4 = (bf16[144,2048]{1,0:T(8,128)(2,1)S(1)}, bf16[144,2048]{1,0:T(8,128)(2,1)S(1)}, u32[]{:S(2)}, u32[]{:S(2)}) collective-permute-start(bf16[144,2048]{1,0:T(8,128)(2,1)S(1)} %slice_bitcast_fusion.3), channel_id=1, source_target_pairs={{12,4},{13,5},{14,6},{15,7},{28,20},{29,21},{30,22},{31,23}} | collective-permute-start | bytes 1769480 | tf_op jit(solution)/shard_map/ppermute | solution.py:516
  52.4 28.6 %collective-permute-start.7 = (bf16[152,2176]{1,0:T(8,128)(2,1)}, bf16[152,2176]{1,0:T(8,128)(2,1)}, u32[]{:S(2)}, u32[]{:S(2)}) collective-permute-start(bf16[152,2176]{1,0:T(8,128)(2,1)} %get-tuple-element.51), channel_id=1, source_target_pairs={{0,4},{4,8},{8,12},{1,5},{5,9},{9,13},{2,6},{6,10},{10,14},{3,7},{... | collective-permute-start | bytes 1984520 | tf_op jit(solution)/shard_map/ppermute | solution.py:516
  61.8 5.7 %copy-start.2 = (bf16[152,4096]{1,0:T(8,128)(2,1)}, bf16[152,4096]{1,0:T(8,128)(2,1)S(1)}, u32[]{:S(2)}) copy-start(bf16[152,4096]{1,0:T(8,128)(2,1)S(1)} %collective-permute-done.5.refs_2_.refs_0_) | copy-start | bytes 3735556
  67.5 37.1 %collective-permute-start.8 = (bf16[144,2176]{1,0:T(8,128)(2,1)}, bf16[144,2176]{1,0:T(8,128)(2,1)S(1)}, u32[]{:S(2)}, u32[]{:S(2)}) collective-permute-start(bf16[144,2176]{1,0:T(8,128)(2,1)} %get-tuple-element.49), channel_id=1, source_target_pairs={{4,8},{8,12},{5,9},{9,13},{6,10},{10,14},{7,11},{11,15},{20,24},{2... | collective-permute-start | bytes 1880072 | tf_op jit(solution)/shard_map/ppermute | solution.py:516
  68.8 0.8 copy-start.4
  69.7 35.0 %collective-permute-start.9 = (bf16[144,2176]{1,0:T(8,128)(2,1)}, bf16[144,2176]{1,0:T(8,128)(2,1)S(1)}, u32[]{:S(2)}, u32[]{:S(2)}) collective-permute-start(bf16[144,2176]{1,0:T(8,128)(2,1)} %get-tuple-element.60), channel_id=1, source_target_pairs={{4,12},{5,13},{6,14},{7,15},{20,28},{21,29},{22,30},{23,31}} | collective-permute-start | bytes 1880072 | tf_op jit(solution)/shard_map/ppermute | solution.py:516
  104.7 0.8 copy-start.5
  104.7 1.1 copy-start.6

commit v3 on v2

--- a/solution.py
+++ b/solution.py
@@ -14,7 +14,7 @@
 TAIL_BLOCK = 1024
 MIX_BLOCK = 512
 HEADS_AT_ONCE = 8
-SPREAD = LANES // 6
+MERGE_STEPS = 2
 NEG = -1e30
 FLOOR = -1e29
 
@@ -271,6 +271,10 @@
     )(*operands)
 
 
+def in_hbm(array):
+    return pltpu.with_memory_space_constraint(array, pltpu.HBM)
+
+
 def parts_of(value):
     high = value.astype(jnp.bfloat16)
     rest = value - high.astype(jnp.float32)
@@ -325,6 +329,7 @@
                                  preferred_element_type=jnp.float32)
         scores = scores + bias[0:rows, 0:extent]
         peak = jnp.maximum(jnp.max(scores, axis=1, keepdims=True), FLOOR)
+        peak = peak.astype(jnp.bfloat16).astype(jnp.float32)
         weights = jnp.exp2((scores - peak) * rate).astype(jnp.bfloat16)
         wide = jnp.concatenate([values, jnp.ones(values.shape, values.dtype)], axis=1)
         mixed = jnp.dot(weights, wide, preferred_element_type=jnp.float32)
@@ -378,26 +383,29 @@
     for at, g in enumerate(groups):
         if g:
             rows = slice(at * count, (at + 1) * count)
-            packed = jnp.zeros((count, LANES), jnp.float32)
-            for n, piece in enumerate(parts_of(peaks[rows]) + parts_of(totals[rows])):
-                piece = piece.astype(jnp.float32)
-                packed = packed + (pltpu.roll(piece, n * SPREAD, 1) if n else piece)
-            sent_refs[g][0:count, width:width + LANES] = packed.astype(sent_refs[g].dtype)
+            packed = peaks[rows]
+            for n, piece in enumerate(parts_of(totals[rows])):
+                packed = packed + pltpu.roll(piece.astype(jnp.float32), (n + 1) * heads, 1)
+            tiles = [packed[8 * j:8 * j + 8] for j in range(count // 8)]
+            for j in range(heads, len(tiles)):
+                tiles[j - heads] = tiles[j - heads] + pltpu.roll(tiles[j], LANES // 2, 1)
+            low = jnp.concatenate(tiles[:heads], axis=1)
+            sent_refs[g][count:count + 8] = low.astype(sent_refs[g].dtype)
 
     for tail_ref, g in zip(tail_refs, sent):
         @pl.when(index == 0)
         def _():
-            sent_refs[g][:, 0:width] = tail_ref[...]
+            sent_refs[g][...] = tail_ref[...]
 
 
 def attend_part(index, lengths, blocks, groups, queries, priors, part, tails=()):
     slots, count, _ = blocks.shape
     width = queries[0].shape[1]
-    rows = tails[0][0].shape[0] if tails else count
+    rows = count + 8
     whole = lambda i, *_: (0, 0)
     kind = queries[0].dtype
-    out_shape = [jax.ShapeDtypeStruct((rows, width + LANES), kind) for _ in queries]
-    out_specs = [pl.BlockSpec((rows, width + LANES), whole) for _ in queries]
+    out_shape = [jax.ShapeDtypeStruct((rows, width), kind) for _ in queries]
+    out_specs = [pl.BlockSpec((rows, width), whole) for _ in queries]
     if 0 in groups:
         shapes = [(count, width), (count, LANES), (count, LANES)]
         out_shape = [pltpu.HBM(shape, jnp.float32) for shape in shapes] + out_shape
@@ -425,75 +433,103 @@
         ),
         compiler_params=pltpu.CompilerParams(vmem_limit_bytes=24 << 20),
         name="attend_part",
-    )(index, lengths, blocks, *queries, *priors, *[array for array, _ in tails])
-
-
-def merge_kernel(where_ref, own_ref, own_peak_ref, own_total_ref, near_ref, far_ref, *refs):
-    out_ref = refs[-1]
+    )(index, lengths, in_hbm(blocks), *queries, *priors, *[array for array, _ in tails])
+
+
+def merge_kernel(where_ref, own_ref, own_peak_ref, own_total_ref, near_ref, near_low_ref, far_ref,
+                 far_low_ref, *refs):
+    *_, out_ref, parts = refs
     count, width = own_ref.shape
     index = where_ref[0]
     rate = math.log2(math.e) / math.sqrt(LANES)
+    step = pl.program_id(0)
+    heads = near_low_ref.shape[1] // LANES
 
     def stats(ref):
-        packed = ref[:, width:width + LANES].astype(jnp.float32)
-        pieces = [packed] + [pltpu.roll(packed, LANES - at * SPREAD, 1) for at in range(1, 6)]
-        return pieces[0] + pieces[1] + pieces[2], pieces[3] + pieces[4] + pieces[5]
-
-    @pl.when(index < 2)
-    def _():
-        part = 1.0 / jnp.where(own_total_ref[...] > 0.0, own_total_ref[...], 1.0)
-        for h in range(width // LANES):
-            lanes = slice(h * LANES, (h + 1) * LANES)
-            out_ref[:, lanes] = (own_ref[:, lanes] * part[:, h:h + 1]).astype(out_ref.dtype)
-
-    @pl.when(index >= 2)
+        low = ref[...].astype(jnp.float32)
+        tiles = [low[:, j % heads * LANES:(j % heads + 1) * LANES] for j in range(count // 8)]
+        for j in range(heads, len(tiles)):
+            tiles[j] = pltpu.roll(tiles[j], LANES // 2, 1)
+        packed = jnp.concatenate(tiles, axis=0)
+        total = pltpu.roll(packed, LANES - heads, 1) + pltpu.roll(packed, LANES - 2 * heads, 1)
+        return packed, total + pltpu.roll(packed, LANES - 3 * heads, 1)
+
+    @pl.when((step == 0) & (index < 2))
+    def _():
+        total = own_total_ref[...]
+        parts[0] = 1.0 / jnp.where(total > 0.0, total, 1.0)
+
+    @pl.when((step == 0) & (index >= 2))
     def _():
         both = index == 3
+        held = lax.broadcasted_iota(jnp.int32, (count, LANES), 1) < heads
         own, total = own_peak_ref[...], own_total_ref[...]
-        near, near_total = stats(near_ref)
-        far, far_total = stats(far_ref)
-        far = jnp.where(both, far, NEG)
+        near, near_total = stats(near_low_ref)
+        far, far_total = stats(far_low_ref)
+        near = jnp.where(held, near, NEG)
+        far = jnp.where(held & both, far, NEG)
         peak = jnp.maximum(own, jnp.maximum(near, far))
         own_part = jnp.exp2((own - peak) * rate)
         near_part = jnp.exp2((near - peak) * rate)
         far_part = jnp.exp2((far - peak) * rate)
-        whole = own_part * total + near_part * near_total
-        whole = whole + jnp.where(both, far_part * far_total, 0.0)
+        whole = own_part * total + jnp.where(held, near_part * near_total, 0.0)
+        whole = whole + jnp.where(held & both, far_part * far_total, 0.0)
         whole = 1.0 / jnp.where(whole > 0.0, whole, 1.0)
-        own_part, near_part, far_part = own_part * whole, near_part * whole, far_part * whole
-        for h in range(width // LANES):
+        parts[0], parts[1], parts[2] = own_part * whole, near_part * whole, far_part * whole
+
+    here = width // LANES
+    turn = lax.rem(LANES - step * here, LANES)
+
+    @pl.when(index < 2)
+    def _():
+        part = pltpu.roll(parts[0], turn, 1)
+        for h in range(here):
+            lanes = slice(h * LANES, (h + 1) * LANES)
+            out_ref[:, lanes] = (own_ref[:, lanes] * part[:, h:h + 1]).astype(out_ref.dtype)
+
+    @pl.when(index >= 2)
+    def _():
+        own_part, near_part, far_part = [pltpu.roll(parts[n], turn, 1) for n in range(3)]
+        for h in range(here):
             lanes = slice(h * LANES, (h + 1) * LANES)
             mixed = own_ref[:, lanes] * own_part[:, h:h + 1]
             mixed = mixed + near_ref[:, lanes].astype(jnp.float32) * near_part[:, h:h + 1]
             mixed = mixed + jnp.where(
-                both, far_ref[:, lanes].astype(jnp.float32) * far_part[:, h:h + 1], 0.0
+                index == 3, far_ref[:, lanes].astype(jnp.float32) * far_part[:, h:h + 1], 0.0
             )
             out_ref[:, lanes] = mixed.astype(out_ref.dtype)
 
 
 def merge_part(index, own, own_peak, own_total, near, far, first, full, held):
     count, width = own.shape
+    block = width // MERGE_STEPS
+    start = first // block
     whole = lambda i, *_: (0, 0)
     extra = () if held is None else (held,)
+    data = pl.BlockSpec((count, block), lambda i, *_: (0, i))
+    low = pl.BlockSpec((8, width), lambda i, *_: (count // 8, 0))
     return pl.pallas_call(
         merge_kernel,
         out_shape=jax.ShapeDtypeStruct((count, full), near.dtype),
         grid_spec=pltpu.PrefetchScalarGridSpec(
             num_scalar_prefetch=1,
-            grid=(1,),
+            grid=(MERGE_STEPS,),
             in_specs=[
-                pl.BlockSpec((count, width), whole),
+                data,
                 pl.BlockSpec((count, LANES), whole),
                 pl.BlockSpec((count, LANES), whole),
-                pl.BlockSpec((count, width + LANES), whole),
-                pl.BlockSpec((count, width + LANES), whole),
+                data,
+                low,
+                data,
+                low,
             ]
             + [pl.BlockSpec(memory_space=pl.ANY)] * len(extra),
-            out_specs=pl.BlockSpec((count, width), lambda i, *_: (0, first)),
+            out_specs=pl.BlockSpec((count, block), lambda i, *_: (0, start + i)),
+            scratch_shapes=[pltpu.VMEM((3, count, LANES), jnp.float32)],
         ),
-        input_output_aliases={6: 0} if extra else {},
+        input_output_aliases={8: 0} if extra else {},
         name="merge_part",
-    )(index, own, own_peak, own_total, near, far, *extra)
+    )(index, own, own_peak, own_total, in_hbm(near), in_hbm(near), in_hbm(far), in_hbm(far), *extra)
 
 
 def layer_four(index, lengths, inputs, short_filter, base, blocks):
@@ -547,7 +583,7 @@
         index, lengths, inputs, short_filter, base, tail, [(halo, 0), (near_in_a, 0)], 0, half, hyena_out
     )
     held, hyena_out = after((held, hyena_out))
-    held = merge_part(index, *own_b, near_in_b, far_in_b, 1, width, held)
+    held = merge_part(index, *own_b, near_in_b, far_in_b, half, width, held)
     return hyena_out, held
 
 

time: 110 us -> 105 us (0.955)
  waiting for transfers between devices: 31.9 us -> 27.9 us
  starting transfers between devices: 26.4 us -> 25.2 us
    ppermute x7, waiting for transfers between devices: 21.4 us -> 17.7 us  [send(): return lax.ppermute(part, 'ctx', axis_pairs)]
    unnamed x15, local copies, waits for them, and re-layouts: 4.16 us -> 2.26 us
  transfers between devices with their start and end apart: 10 -> 10, of which waited for: 5 -> 4; matrix products, arithmetic and copies ran while one was open for 2% -> 3% of each run, Pallas kernels for 35% -> 37%
where the time goes in v3:
time: 105 us; the launch traced here: 104 us
  Pallas kernels  42.1 us (40%)
  waiting for transfers between devices  27.9 us (27%)
  starting transfers between devices  25.2 us (24%)
  local copies, waits for them, and re-layouts  7.13 us (7%)
    ppermute x7, starting transfers between devices, send(): return lax.ppermute(part, 'ctx', axis_pairs)  19.6 us
    ppermute x7, waiting for transfers between devices, send(): return lax.ppermute(part, 'ctx', axis_pairs)  17.7 us
    pallas_call x2, Pallas kernels, mixer(): pl.pallas_call(partial(mixer_kernel, len(halos)), out_shape=jax.ShapeDtyp...  15.8 us
    pallas_call x2, Pallas kernels, attend_part(): pl.pallas_call(partial(attend_kernel, groups, len(priors), len(tails)), o...  12 us
    ppermute x1, waiting for transfers between devices, queries(): return (near, lax.ppermute(mine, 'ctx', [(3, 1)]))  7.24 us
    pallas_call x1, Pallas kernels, mixer_tail(): pl.pallas_call(tail_kernel, out_shape=(out,) * (1 + len(extra)), grid_spe...  7.23 us
    pallas_call x2, Pallas kernels, merge_part(): pl.pallas_call(merge_kernel, out_shape=jax.ShapeDtypeStruct((count, full)...  7.1 us
    ppermute x1, waiting for transfers between devices, queries(): near = lax.ppermute(mine, 'ctx', [(2, 1), (3, 2)])  2.94 us
  transfers between devices with their start and end apart: 10, of which 4 were waited for; matrix products, arithmetic and copies ran while one was open for 3% of the time, Pallas kernels for 37%

profile of v3, /device:TPU:24, one launch (start us, length us, event | category | flops | bytes accessed | tf_op | source)
XLA Modules:
  0.0 104.1 jit_solution(1797775440779899938)
XLA Ops:
  0.6 2.4 %slice_bitcast_fusion.1 = (bf16[144,2048]{1,0:T(8,128)(2,1)S(1)}, bf16[144,2048]{1,0:T(8,128)(2,1)S(1)}, bf16[144,2048]{1,0:T(8,128)(2,1)}) fusion(bf16[3,144,4096]{2,1,0:T(8,128)(2,1)} %bitcast.31), kind=kLoop, calls=%fused_computation.2 | loop fusion | bytes 3538944 | tf_op jit(solution)/shard_map/squeeze | solution.py:548
  3.9 2.4 %collective-permute-start = (bf16[144,2048]{1,0:T(8,128)(2,1)}, bf16[144,2048]{1,0:T(8,128)(2,1)S(1)}, u32[]{:S(2)}, u32[]{:S(2)}) collective-permute-start(bf16[144,2048]{1,0:T(8,128)(2,1)} %get-tuple-element.64), channel_id=1, source_target_pairs={{8,4},{12,8},{9,5},{13,9},{10,6},{14,10},{11,7},{15,11},{24,20},{2... | collective-permute-start | bytes 1769480 | tf_op jit(solution)/shard_map/ppermute | solution.py:543
  6.3 2.5 %collective-permute-start.1 = (bf16[144,2048]{1,0:T(8,128)(2,1)}, bf16[144,2048]{1,0:T(8,128)(2,1)}, u32[]{:S(2)}, u32[]{:S(2)}) collective-permute-start(bf16[144,2048]{1,0:T(8,128)(2,1)} %get-tuple-element.64), channel_id=1, source_target_pairs={{12,4},{13,5},{14,6},{15,7},{28,20},{29,21},{30,22},{31,23}} | collective-permute-start | bytes 1769480 | tf_op jit(solution)/shard_map/ppermute | solution.py:544
  8.8 7.2 %mixer_tail.1 = (bf16[152,4096]{1,0:T(8,128)(2,1)}, bf16[152,4096]{1,0:T(8,128)(2,1)}) custom-call(s32[1]{0:T(128)} %bitcast.where_ref, s32[1,4]{1,0:T(1,128)} %lengths_ref.9, bf16[3,144,4096]{2,1,0:T(8,128)(2,1)} %bitcast.22, bf16[3,144,4096]{2,1,0:T(8,128)(2,1)} %bitcast.23, bf16[3,144,4096]{2,1,0:T(8,128)(2,1)} %bitcast.24, bf16[3,7,4096]{2,1,0:T(8,128)(2,1)} %taps_ref.5, ...), custom_call_target="tpu_custom_call" | custom-call | tf_op jit(solution)/shard_map/mixer_tail/pallas_call | solution.py:112
  16.0 1.3 %collective-permute-start.5 = (bf16[152,4096]{1,0:T(8,128)(2,1)}, bf16[152,4096]{1,0:T(8,128)(2,1)S(1)}, u32[]{:S(2)}, u32[]{:S(2)}) collective-permute-start(bf16[152,4096]{1,0:T(8,128)(2,1)} %get-tuple-element.42), channel_id=1, source_target_pairs={{0,4},{4,8},{8,12},{1,5},{5,9},{9,13},{2,6},{6,10},{10,14},{3,7},{... | collective-permute-start | bytes 3735560 | tf_op jit(solution)/shard_map/ppermute | solution.py:552
  17.3 2.9 %collective-permute-done.refs_0_ = bf16[144,2048]{1,0:T(8,128)(2,1)S(1)} collective-permute-done((bf16[144,2048]{1,0:T(8,128)(2,1)}, bf16[144,2048]{1,0:T(8,128)(2,1)S(1)}, u32[]{:S(2)}, u32[]{:S(2)}) %collective-permute-start) | collective-permute-done | bytes 589856 | tf_op jit(solution)/shard_map/ppermute | solution.py:543
  20.2 1.1 %slice_bitcast_fusion.4 = bf16[144,2048]{1,0:T(8,128)(2,1)S(1)} fusion(bf16[3,144,4096]{2,1,0:T(8,128)(2,1)} %bitcast.33), kind=kLoop, calls=%fused_computation.5 | loop fusion | bytes 1179648 | tf_op jit(solution)/shard_map/squeeze | solution.py:560
  21.4 4.3 %collective-permute-start.3 = (bf16[144,2048]{1,0:T(8,128)(2,1)S(1)}, bf16[144,2048]{1,0:T(8,128)(2,1)S(1)}, u32[]{:S(2)}, u32[]{:S(2)}) collective-permute-start(bf16[144,2048]{1,0:T(8,128)(2,1)S(1)} %slice_bitcast_fusion.4), channel_id=1, source_target_pairs={{8,4},{12,8},{9,5},{13,9},{10,6},{14,10},{11,7},{15,11},{24,20},{2... | collective-permute-start | bytes 1769480 | tf_op jit(solution)/shard_map/ppermute | solution.py:552
  25.7 7.2 %collective-permute-done.1.refs_1_ = bf16[144,2048]{1,0:T(8,128)(2,1)} collective-permute-done((bf16[144,2048]{1,0:T(8,128)(2,1)}, bf16[144,2048]{1,0:T(8,128)(2,1)}, u32[]{:S(2)}, u32[]{:S(2)}) %collective-permute-start.1) | collective-permute-done | bytes 589856 | tf_op jit(solution)/shard_map/ppermute | solution.py:544
  32.9 1.3 %copy-done = bf16[152,4096]{1,0:T(8,128)(2,1)S(1)} copy-done((bf16[152,4096]{1,0:T(8,128)(2,1)S(1)}, bf16[152,4096]{1,0:T(8,128)(2,1)}, u32[]{:S(2)}) %copy-start) | copy-done | bytes 1245208
  34.2 6.2 %attend_part.2 = (f32[144,2048]{1,0:T(8,128)}, f32[144,128]{1,0:T(8,128)}, f32[144,128]{1,0:T(8,128)}, bf16[152,2048]{1,0:T(8,128)(2,1)}, bf16[152,2048]{1,0:T(8,128)(2,1)S(1)}) custom-call(s32[1]{0:T(128)} %bitcast.where_ref, s32[1,4]{1,0:T(1,128)S(1)} %copy-done.2, bf16[3,144,4096]{2,1,0:T(8,128)(2,1)} %bitcast.34, ...), custom_call_target="tpu_custom_call" | custom-call | tf_op jit(solution)/shard_map/attend_part/pallas_call | solution.py:417
  40.5 1.3 %collective-permute-start.6 = (bf16[152,2048]{1,0:T(8,128)(2,1)S(1)}, bf16[152,2048]{1,0:T(8,128)(2,1)S(1)}, u32[]{:S(2)}, u32[]{:S(2)}) collective-permute-start(bf16[152,2048]{1,0:T(8,128)(2,1)S(1)} %get-tuple-element.43), channel_id=1, source_target_pairs={{0,4},{4,12},{1,5},{5,13},{2,6},{6,14},{3,7},{7,15},{16,20},{20,28... | collective-permute-start | bytes 1867784 | tf_op jit(solution)/shard_map/ppermute | solution.py:552
  41.8 1.1 %slice_bitcast_fusion.3 = bf16[144,2048]{1,0:T(8,128)(2,1)S(1)} fusion(bf16[3,144,4096]{2,1,0:T(8,128)(2,1)} %bitcast.35), kind=kLoop, calls=%fused_computation.4 | loop fusion | bytes 1179648 | tf_op jit(solution)/shard_map/squeeze | solution.py:562
  42.9 8.5 %collective-permute-start.4 = (bf16[144,2048]{1,0:T(8,128)(2,1)S(1)}, bf16[144,2048]{1,0:T(8,128)(2,1)S(1)}, u32[]{:S(2)}, u32[]{:S(2)}) collective-permute-start(bf16[144,2048]{1,0:T(8,128)(2,1)S(1)} %slice_bitcast_fusion.3), channel_id=1, source_target_pairs={{12,4},{13,5},{14,6},{15,7},{28,20},{29,21},{30,22},{31,23}} | collective-permute-start | bytes 1769480 | tf_op jit(solution)/shard_map/ppermute | solution.py:552
  51.4 1.4 %collective-permute-start.7 = (bf16[152,2048]{1,0:T(8,128)(2,1)}, bf16[152,2048]{1,0:T(8,128)(2,1)S(1)}, u32[]{:S(2)}, u32[]{:S(2)}) collective-permute-start(bf16[152,2048]{1,0:T(8,128)(2,1)} %get-tuple-element.51), channel_id=1, source_target_pairs={{0,4},{4,8},{8,12},{1,5},{5,9},{9,13},{2,6},{6,10},{10,14},{3,7},{... | collective-permute-start | bytes 1867784 | tf_op jit(solution)/shard_map/ppermute | solution.py:552
  52.9 9.0 %collective-permute-done.4.refs_1_ = bf16[144,2048]{1,0:T(8,128)(2,1)S(1)} collective-permute-done((bf16[144,2048]{1,0:T(8,128)(2,1)S(1)}, bf16[144,2048]{1,0:T(8,128)(2,1)S(1)}, u32[]{:S(2)}, u32[]{:S(2)}) %collective-permute-start.4) | collective-permute-done | bytes 589856 | tf_op jit(solution)/shard_map/ppermute | solution.py:552
  61.9 5.8 %attend_part.3 = (f32[144,2048]{1,0:T(8,128)}, f32[144,128]{1,0:T(8,128)}, f32[144,128]{1,0:T(8,128)}, bf16[152,2048]{1,0:T(8,128)(2,1)S(1)}, bf16[152,2048]{1,0:T(8,128)(2,1)S(1)}) custom-call(s32[1]{0:T(128)} %bitcast.where_ref, s32[1,4]{1,0:T(1,128)S(1)} %copy-done.2, bf16[3,144,4096]{2,1,0:T(8,128)(2,1)} %bitcast.36, ...), custom_call_target="tpu_custom_call" | custom-call | tf_op jit(solution)/shard_map/attend_part/pallas_call | solution.py:417
  67.7 1.3 %collective-permute-start.8 = (bf16[152,2048]{1,0:T(8,128)(2,1)S(1)}, bf16[152,2048]{1,0:T(8,128)(2,1)S(1)}, u32[]{:S(2)}, u32[]{:S(2)}) collective-permute-start(bf16[152,2048]{1,0:T(8,128)(2,1)S(1)} %get-tuple-element.49), channel_id=1, source_target_pairs={{4,8},{8,12},{5,9},{9,13},{6,10},{10,14},{7,11},{11,15},{20,24},{2... | collective-permute-start | bytes 1867784 | tf_op jit(solution)/shard_map/ppermute | solution.py:552
  69.0 1.5 %collective-permute-start.9 = (bf16[152,2048]{1,0:T(8,128)(2,1)S(1)}, bf16[152,2048]{1,0:T(8,128)(2,1)}, u32[]{:S(2)}, u32[]{:S(2)}) collective-permute-start(bf16[152,2048]{1,0:T(8,128)(2,1)S(1)} %get-tuple-element.60), channel_id=1, source_target_pairs={{4,12},{5,13},{6,14},{7,15},{20,28},{21,29},{22,30},{23,31}} | collective-permute-start | bytes 1867784 | tf_op jit(solution)/shard_map/ppermute | solution.py:552
  71.7 7.9 %mixer.2.refs_2_ = bf16[144,4096]{1,0:T(8,128)(2,1)} custom-call(s32[1]{0:T(128)} %bitcast.where_ref, s32[1,4]{1,0:T(1,128)} %lengths_ref.9, bf16[3,144,4096]{2,1,0:T(8,128)(2,1)} %bitcast.25, bf16[3,144,4096]{2,1,0:T(8,128)(2,1)} %bitcast.26, bf16[3,144,4096]{2,1,0:T(8,128)(2,1)} %bitcast.27, bf16[3,7,4096]{2,1,0:T(8,128)(2,1)} %taps_ref.5, ...), custom_call_target="tpu_custom_call" | custom-call | tf_op jit(solution)/shard_map/mixer/pallas_call | solution.py:242
  80.4 3.5 %merge_part.2.refs_0_ = bf16[144,4096]{1,0:T(8,128)(2,1)} custom-call(s32[1]{0:T(128)} %bitcast.where_ref, f32[144,2048]{1,0:T(8,128)} %get-tuple-element.38.own_ref, f32[144,128]{1,0:T(8,128)} %get-tuple-element.39.own_peak_ref, f32[144,128]{1,0:T(8,128)} %get-tuple-element.40.own_total_ref, bf16[152,2048]{1,0:T(8,128)(2,1)} %copy-done.4, ...), custom_call_target="tpu_custom_call" | custom-call | tf_op jit(solution)/shard_map/merge_part/pallas_call | solution.py:511
  83.9 7.9 %mixer.3 = bf16[144,4096]{1,0:T(8,128)(2,1)} custom-call(s32[1]{0:T(128)} %bitcast.where_ref, s32[1,4]{1,0:T(1,128)} %lengths_ref.9, bf16[3,144,4096]{2,1,0:T(8,128)(2,1)} %bitcast.28, bf16[3,144,4096]{2,1,0:T(8,128)(2,1)} %bitcast.29, bf16[3,144,4096]{2,1,0:T(8,128)(2,1)} %bitcast.30, ...), custom_call_target="tpu_custom_call", output_to_operand_aliasing={{}: (10, {})} | custom-call | tf_op jit(solution)/shard_map/mixer/pallas_call | solution.py:242
  91.8 8.7 %collective-permute-done.9.far_ref.far_low_ref = bf16[152,2048]{1,0:T(8,128)(2,1)} collective-permute-done((bf16[152,2048]{1,0:T(8,128)(2,1)S(1)}, bf16[152,2048]{1,0:T(8,128)(2,1)}, u32[]{:S(2)}, u32[]{:S(2)}) %collective-permute-start.9) | collective-permute-done | bytes 622624 | tf_op jit(solution)/shard_map/ppermute | solution.py:552
  100.5 3.6 %merge_part.3 = bf16[144,4096]{1,0:T(8,128)(2,1)} custom-call(s32[1]{0:T(128)} %bitcast.where_ref, f32[144,2048]{1,0:T(8,128)} %get-tuple-element.57.own_ref, f32[144,128]{1,0:T(8,128)} %get-tuple-element.58.own_peak_ref, f32[144,128]{1,0:T(8,128)} %get-tuple-element.59.own_total_ref, bf16[152,2048]{1,0:T(8,128)(2,1)} %copy-done.5, ...), custom_call_target="tpu_custom_call", output_to_operand_aliasing={{}: (8, {})} | custom-call | tf_op jit(solution)/shard_map/merge_part/pallas_call | solution.py:511
  (26 shorter events, 2.9 us)
Async XLA Ops:
  3.1 29.8 %collective-permute-start.2 = (bf16[144,4096]{1,0:T(8,128)(2,1)S(1)}, bf16[144,4096]{1,0:T(8,128)(2,1)S(1)}, u32[]{:S(2)}, u32[]{:S(2)}) collective-permute-start(bf16[144,4096]{1,0:T(8,128)(2,1)S(1)} %pad_maximum_fusion), channel_id=1, source_target_pairs={{0,4},{1,5},{2,6},{3,7},{16,20},{17,21},{18,22},{19,23}} | collective-permute-start | bytes 3538952 | tf_op jit(solution)/shard_map/ppermute | solution.py:549
  3.9 16.4 %collective-permute-start = (bf16[144,2048]{1,0:T(8,128)(2,1)}, bf16[144,2048]{1,0:T(8,128)(2,1)S(1)}, u32[]{:S(2)}, u32[]{:S(2)}) collective-permute-start(bf16[144,2048]{1,0:T(8,128)(2,1)} %get-tuple-element.64), channel_id=1, source_target_pairs={{8,4},{12,8},{9,5},{13,9},{10,6},{14,10},{11,7},{15,11},{24,20},{2... | collective-permute-start | bytes 1769480 | tf_op jit(solution)/shard_map/ppermute | solution.py:543
  6.3 26.7 %collective-permute-start.1 = (bf16[144,2048]{1,0:T(8,128)(2,1)}, bf16[144,2048]{1,0:T(8,128)(2,1)}, u32[]{:S(2)}, u32[]{:S(2)}) collective-permute-start(bf16[144,2048]{1,0:T(8,128)(2,1)} %get-tuple-element.64), channel_id=1, source_target_pairs={{12,4},{13,5},{14,6},{15,7},{28,20},{29,21},{30,22},{31,23}} | collective-permute-start | bytes 1769480 | tf_op jit(solution)/shard_map/ppermute | solution.py:544
  8.8 24.1 %copy-start.2 = (s32[1,4]{1,0:T(1,128)S(1)}, s32[1,4]{1,0:T(1,128)}, u32[]{:S(2)}) copy-start(s32[1,4]{1,0:T(1,128)} %lengths_ref.9) | copy-start | bytes 52
  16.0 36.8 %collective-permute-start.5 = (bf16[152,4096]{1,0:T(8,128)(2,1)}, bf16[152,4096]{1,0:T(8,128)(2,1)S(1)}, u32[]{:S(2)}, u32[]{:S(2)}) collective-permute-start(bf16[152,4096]{1,0:T(8,128)(2,1)} %get-tuple-element.42), channel_id=1, source_target_pairs={{0,4},{4,8},{8,12},{1,5},{5,9},{9,13},{2,6},{6,10},{10,14},{3,7},{... | collective-permute-start | bytes 3735560 | tf_op jit(solution)/shard_map/ppermute | solution.py:552
  21.4 31.5 %collective-permute-start.3 = (bf16[144,2048]{1,0:T(8,128)(2,1)S(1)}, bf16[144,2048]{1,0:T(8,128)(2,1)S(1)}, u32[]{:S(2)}, u32[]{:S(2)}) collective-permute-start(bf16[144,2048]{1,0:T(8,128)(2,1)S(1)} %slice_bitcast_fusion.4), channel_id=1, source_target_pairs={{8,4},{12,8},{9,5},{13,9},{10,6},{14,10},{11,7},{15,11},{24,20},{2... | collective-permute-start | bytes 1769480 | tf_op jit(solution)/shard_map/ppermute | solution.py:552
  32.9 1.3 %copy-start = (bf16[152,4096]{1,0:T(8,128)(2,1)S(1)}, bf16[152,4096]{1,0:T(8,128)(2,1)}, u32[]{:S(2)}) copy-start(bf16[152,4096]{1,0:T(8,128)(2,1)} %get-tuple-element.55.refs_3_.refs_4_.tail_ref) | copy-start | bytes 3735556
  40.5 28.5 %collective-permute-start.6 = (bf16[152,2048]{1,0:T(8,128)(2,1)S(1)}, bf16[152,2048]{1,0:T(8,128)(2,1)S(1)}, u32[]{:S(2)}, u32[]{:S(2)}) collective-permute-start(bf16[152,2048]{1,0:T(8,128)(2,1)S(1)} %get-tuple-element.43), channel_id=1, source_target_pairs={{0,4},{4,12},{1,5},{5,13},{2,6},{6,14},{3,7},{7,15},{16,20},{20,28... | collective-permute-start | bytes 1867784 | tf_op jit(solution)/shard_map/ppermute | solution.py:552
  42.9 19.0 %collective-permute-start.4 = (bf16[144,2048]{1,0:T(8,128)(2,1)S(1)}, bf16[144,2048]{1,0:T(8,128)(2,1)S(1)}, u32[]{:S(2)}, u32[]{:S(2)}) collective-permute-start(bf16[144,2048]{1,0:T(8,128)(2,1)S(1)} %slice_bitcast_fusion.3), channel_id=1, source_target_pairs={{12,4},{13,5},{14,6},{15,7},{28,20},{29,21},{30,22},{31,23}} | collective-permute-start | bytes 1769480 | tf_op jit(solution)/shard_map/ppermute | solution.py:552
  51.4 19.1 %copy-start.6 = (bf16[128,256]{1,0:T(8,128)(2,1)S(1)}, bf16[128,256]{1,0:T(8,128)(2,1)}, u32[]{:S(2)}) copy-start(bf16[128,256]{1,0:T(8,128)(2,1)} %param.7) | copy-start | bytes 196612
  51.4 28.1 %collective-permute-start.7 = (bf16[152,2048]{1,0:T(8,128)(2,1)}, bf16[152,2048]{1,0:T(8,128)(2,1)S(1)}, u32[]{:S(2)}, u32[]{:S(2)}) collective-permute-start(bf16[152,2048]{1,0:T(8,128)(2,1)} %get-tuple-element.51), channel_id=1, source_target_pairs={{0,4},{4,8},{8,12},{1,5},{5,9},{9,13},{2,6},{6,10},{10,14},{3,7},{... | collective-permute-start | bytes 1867784 | tf_op jit(solution)/shard_map/ppermute | solution.py:552
  52.9 14.8 %copy-start.1 = (bf16[152,4096]{1,0:T(8,128)(2,1)}, bf16[152,4096]{1,0:T(8,128)(2,1)S(1)}, u32[]{:S(2)}) copy-start(bf16[152,4096]{1,0:T(8,128)(2,1)S(1)} %collective-permute-done.5.refs_2_.refs_0_) | copy-start | bytes 3735556
  67.7 24.1 %collective-permute-start.8 = (bf16[152,2048]{1,0:T(8,128)(2,1)S(1)}, bf16[152,2048]{1,0:T(8,128)(2,1)S(1)}, u32[]{:S(2)}, u32[]{:S(2)}) collective-permute-start(bf16[152,2048]{1,0:T(8,128)(2,1)S(1)} %get-tuple-element.49), channel_id=1, source_target_pairs={{4,8},{8,12},{5,9},{9,13},{6,10},{10,14},{7,11},{11,15},{20,24},{2... | collective-permute-start | bytes 1867784 | tf_op jit(solution)/shard_map/ppermute | solution.py:552
  69.0 2.7 %copy-start.3 = (bf16[152,2048]{1,0:T(8,128)(2,1)}, bf16[152,2048]{1,0:T(8,128)(2,1)S(1)}, u32[]{:S(2)}) copy-start(bf16[152,2048]{1,0:T(8,128)(2,1)S(1)} %collective-permute-done.6.refs_1_.far_ref.far_low_ref) | copy-start | bytes 1867780
  69.0 31.5 %collective-permute-start.9 = (bf16[152,2048]{1,0:T(8,128)(2,1)S(1)}, bf16[152,2048]{1,0:T(8,128)(2,1)}, u32[]{:S(2)}, u32[]{:S(2)}) collective-permute-start(bf16[152,2048]{1,0:T(8,128)(2,1)S(1)} %get-tuple-element.60), channel_id=1, source_target_pairs={{4,12},{5,13},{6,14},{7,15},{20,28},{21,29},{22,30},{23,31}} | collective-permute-start | bytes 1867784 | tf_op jit(solution)/shard_map/ppermute | solution.py:552
  79.6 0.8 copy-start.4
  91.8 8.7 %copy-start.5 = (bf16[152,2048]{1,0:T(8,128)(2,1)}, bf16[152,2048]{1,0:T(8,128)(2,1)S(1)}, u32[]{:S(2)}) copy-start(bf16[152,2048]{1,0:T(8,128)(2,1)S(1)} %collective-permute-done.8.near_ref.near_low_ref) | copy-start | bytes 1867780

commit v4 on v3

--- a/solution.py
+++ b/solution.py
@@ -392,10 +392,10 @@
             low = jnp.concatenate(tiles[:heads], axis=1)
             sent_refs[g][count:count + 8] = low.astype(sent_refs[g].dtype)
 
-    for tail_ref, g in zip(tail_refs, sent):
+    for n, (tail_ref, g) in enumerate(zip(tail_refs, sent)):
         @pl.when(index == 0)
         def _():
-            sent_refs[g][...] = tail_ref[...]
+            pltpu.sync_copy(tail_ref.at[:, n * width:(n + 1) * width], sent_refs[g])
 
 
 def attend_part(index, lengths, blocks, groups, queries, priors, part, tails=()):
@@ -411,9 +411,6 @@
         out_shape = [pltpu.HBM(shape, jnp.float32) for shape in shapes] + out_shape
         out_specs = [pl.BlockSpec(shape, whole) for shape in shapes] + out_specs
 
-    def tail_spec(at):
-        return pl.BlockSpec((rows, width), lambda i, *_: (0, at))
-
     return pl.pallas_call(
         partial(attend_kernel, groups, len(priors), len(tails)),
         out_shape=out_shape,
@@ -423,7 +420,7 @@
             in_specs=[pl.BlockSpec((slots, count, width), lambda i, *_: (0, 0, part))]
             + [pl.BlockSpec((count, width), whole) for _ in queries]
             + [pl.BlockSpec(prior.shape, whole) for prior in priors]
-            + [tail_spec(at) for _, at in tails],
+            + [pl.BlockSpec(memory_space=pl.ANY) for _ in tails],
             out_specs=out_specs,
             scratch_shapes=[
                 pltpu.VMEM((len(groups) * count, 2 * count), jnp.float32),
@@ -433,7 +430,7 @@
         ),
         compiler_params=pltpu.CompilerParams(vmem_limit_bytes=24 << 20),
         name="attend_part",
-    )(index, lengths, in_hbm(blocks), *queries, *priors, *[array for array, _ in tails])
+    )(index, lengths, in_hbm(blocks), *queries, *priors, *[in_hbm(tail) for tail in tails])
 
 
 def merge_kernel(where_ref, own_ref, own_peak_ref, own_total_ref, near_ref, near_low_ref, far_ref,
@@ -561,7 +558,7 @@
     held, far_a, prior_a = after((held, far_a, prior_a))
     far_b = send(held[0, :, half:], [(3, 1)])
     *own_a, near_out, far_out = attend_part(
-        index, lengths, blocks, (0, 1, 2), [near_a, far_a], [prior_a], 0, [(tail, 0), (tail, 1)]
+        index, lengths, blocks, (0, 1, 2), [near_a, far_a], [prior_a], 0, [tail, tail]
     )
     near_in_a = send(near_out, forward)
     far_in_a = send(far_out, [(0, 1), (1, 3)])

time: 105 us -> 105 us (level)
  waiting for transfers between devices: 27.9 us -> 29.1 us
    ppermute x7, waiting for transfers between devices: 17.7 us -> 18.9 us  [send(): return lax.ppermute(part, 'ctx', axis_pairs)]
    unnamed x15 -> x13, local copies, waits for them, and re-layouts: 2.26 us -> 1.76 us
  transfers between devices with their start and end apart: 10 -> 10, of which waited for: 4 -> 5; matrix products, arithmetic and copies ran while one was open for 3% -> 3% of each run, Pallas kernels for 37% -> 37%
where the time goes in v4:
time: 105 us
  Pallas kernels  42.1 us (40%)
  waiting for transfers between devices  29.1 us (28%)
  starting transfers between devices  25.2 us (24%)
  local copies, waits for them, and re-layouts  6.63 us (6%)
    ppermute x7, starting transfers between devices, send(): return lax.ppermute(part, 'ctx', axis_pairs)  19.6 us
    ppermute x7, waiting for transfers between devices, send(): return lax.ppermute(part, 'ctx', axis_pairs)  18.9 us
    pallas_call x2, Pallas kernels, mixer(): pl.pallas_call(partial(mixer_kernel, len(halos)), out_shape=jax.ShapeDtyp...  15.8 us
    pallas_call x2, Pallas kernels, attend_part(): pl.pallas_call(partial(attend_kernel, groups, len(priors), len(tails)), o...  12 us
    pallas_call x1, Pallas kernels, mixer_tail(): pl.pallas_call(tail_kernel, out_shape=(out,) * (1 + len(extra)), grid_spe...  7.25 us
    ppermute x1, waiting for transfers between devices, queries(): return (near, lax.ppermute(mine, 'ctx', [(3, 1)]))  7.24 us
    pallas_call x2, Pallas kernels, merge_part(): pl.pallas_call(merge_kernel, out_shape=jax.ShapeDtypeStruct((count, full)...  7.08 us
    ppermute x1, waiting for transfers between devices, queries(): near = lax.ppermute(mine, 'ctx', [(2, 1), (3, 2)])  2.92 us
  transfers between devices with their start and end apart: 10, of which 5 were waited for; matrix products, arithmetic and copies ran while one was open for 3% of the time, Pallas kernels for 37%

profile of v4, /device:TPU:24, one launch (start us, length us, event | category | flops | bytes accessed | tf_op | source)
XLA Modules:
  0.0 104.7 jit_solution(12359733527402753224)
XLA Ops:
  0.6 2.4 %slice_bitcast_fusion.1 = (bf16[144,2048]{1,0:T(8,128)(2,1)S(1)}, bf16[144,2048]{1,0:T(8,128)(2,1)S(1)}, bf16[144,2048]{1,0:T(8,128)(2,1)}) fusion(bf16[3,144,4096]{2,1,0:T(8,128)(2,1)} %bitcast.31), kind=kLoop, calls=%fused_computation.2 | loop fusion | bytes 3538944 | tf_op jit(solution)/shard_map/squeeze | solution.py:545
  3.9 2.4 %collective-permute-start = (bf16[144,2048]{1,0:T(8,128)(2,1)}, bf16[144,2048]{1,0:T(8,128)(2,1)S(1)}, u32[]{:S(2)}, u32[]{:S(2)}) collective-permute-start(bf16[144,2048]{1,0:T(8,128)(2,1)} %get-tuple-element.64), channel_id=1, source_target_pairs={{8,4},{12,8},{9,5},{13,9},{10,6},{14,10},{11,7},{15,11},{24,20},{2... | collective-permute-start | bytes 1769480 | tf_op jit(solution)/shard_map/ppermute | solution.py:540
  6.3 2.5 %collective-permute-start.1 = (bf16[144,2048]{1,0:T(8,128)(2,1)}, bf16[144,2048]{1,0:T(8,128)(2,1)}, u32[]{:S(2)}, u32[]{:S(2)}) collective-permute-start(bf16[144,2048]{1,0:T(8,128)(2,1)} %get-tuple-element.64), channel_id=1, source_target_pairs={{12,4},{13,5},{14,6},{15,7},{28,20},{29,21},{30,22},{31,23}} | collective-permute-start | bytes 1769480 | tf_op jit(solution)/shard_map/ppermute | solution.py:541
  8.8 7.2 %mixer_tail.1 = (bf16[152,4096]{1,0:T(8,128)(2,1)}, bf16[152,4096]{1,0:T(8,128)(2,1)}) custom-call(s32[1]{0:T(128)} %bitcast.where_ref, s32[1,4]{1,0:T(1,128)} %lengths_ref.9, bf16[3,144,4096]{2,1,0:T(8,128)(2,1)} %bitcast.22, bf16[3,144,4096]{2,1,0:T(8,128)(2,1)} %bitcast.23, bf16[3,144,4096]{2,1,0:T(8,128)(2,1)} %bitcast.24, bf16[3,7,4096]{2,1,0:T(8,128)(2,1)} %taps_ref.5, ...), custom_call_target="tpu_custom_call" | custom-call | tf_op jit(solution)/shard_map/mixer_tail/pallas_call | solution.py:112
  16.0 1.3 %collective-permute-start.5 = (bf16[152,4096]{1,0:T(8,128)(2,1)}, bf16[152,4096]{1,0:T(8,128)(2,1)S(1)}, u32[]{:S(2)}, u32[]{:S(2)}) collective-permute-start(bf16[152,4096]{1,0:T(8,128)(2,1)} %get-tuple-element.42), channel_id=1, source_target_pairs={{0,4},{4,8},{8,12},{1,5},{5,9},{9,13},{2,6},{6,10},{10,14},{3,7},{... | collective-permute-start | bytes 3735560 | tf_op jit(solution)/shard_map/ppermute | solution.py:549
  17.3 2.9 %collective-permute-done.refs_0_ = bf16[144,2048]{1,0:T(8,128)(2,1)S(1)} collective-permute-done((bf16[144,2048]{1,0:T(8,128)(2,1)}, bf16[144,2048]{1,0:T(8,128)(2,1)S(1)}, u32[]{:S(2)}, u32[]{:S(2)}) %collective-permute-start) | collective-permute-done | bytes 589856 | tf_op jit(solution)/shard_map/ppermute | solution.py:540
  20.2 1.1 %slice_bitcast_fusion.4 = bf16[144,2048]{1,0:T(8,128)(2,1)S(1)} fusion(bf16[3,144,4096]{2,1,0:T(8,128)(2,1)} %bitcast.33), kind=kLoop, calls=%fused_computation.5 | loop fusion | bytes 1179648 | tf_op jit(solution)/shard_map/squeeze | solution.py:557
  21.4 4.3 %collective-permute-start.3 = (bf16[144,2048]{1,0:T(8,128)(2,1)S(1)}, bf16[144,2048]{1,0:T(8,128)(2,1)S(1)}, u32[]{:S(2)}, u32[]{:S(2)}) collective-permute-start(bf16[144,2048]{1,0:T(8,128)(2,1)S(1)} %slice_bitcast_fusion.4), channel_id=1, source_target_pairs={{8,4},{12,8},{9,5},{13,9},{10,6},{14,10},{11,7},{15,11},{24,20},{2... | collective-permute-start | bytes 1769480 | tf_op jit(solution)/shard_map/ppermute | solution.py:549
  25.7 7.2 %collective-permute-done.1.refs_1_ = bf16[144,2048]{1,0:T(8,128)(2,1)} collective-permute-done((bf16[144,2048]{1,0:T(8,128)(2,1)}, bf16[144,2048]{1,0:T(8,128)(2,1)}, u32[]{:S(2)}, u32[]{:S(2)}) %collective-permute-start.1) | collective-permute-done | bytes 589856 | tf_op jit(solution)/shard_map/ppermute | solution.py:541
  32.9 6.2 %attend_part.2 = (f32[144,2048]{1,0:T(8,128)}, f32[144,128]{1,0:T(8,128)}, f32[144,128]{1,0:T(8,128)}, bf16[152,2048]{1,0:T(8,128)(2,1)}, bf16[152,2048]{1,0:T(8,128)(2,1)S(1)}) custom-call(s32[1]{0:T(128)} %bitcast.where_ref, s32[1,4]{1,0:T(1,128)S(1)} %copy-done.1, bf16[3,144,4096]{2,1,0:T(8,128)(2,1)} %bitcast.34, ...), custom_call_target="tpu_custom_call" | custom-call | tf_op jit(solution)/shard_map/attend_part/pallas_call | solution.py:414
  39.2 1.3 %collective-permute-start.6 = (bf16[152,2048]{1,0:T(8,128)(2,1)S(1)}, bf16[152,2048]{1,0:T(8,128)(2,1)S(1)}, u32[]{:S(2)}, u32[]{:S(2)}) collective-permute-start(bf16[152,2048]{1,0:T(8,128)(2,1)S(1)} %get-tuple-element.43), channel_id=1, source_target_pairs={{0,4},{4,12},{1,5},{5,13},{2,6},{6,14},{3,7},{7,15},{16,20},{20,28... | collective-permute-start | bytes 1867784 | tf_op jit(solution)/shard_map/ppermute | solution.py:549
  40.5 1.1 %slice_bitcast_fusion.3 = bf16[144,2048]{1,0:T(8,128)(2,1)S(1)} fusion(bf16[3,144,4096]{2,1,0:T(8,128)(2,1)} %bitcast.35), kind=kLoop, calls=%fused_computation.4 | loop fusion | bytes 1179648 | tf_op jit(solution)/shard_map/squeeze | solution.py:559
  41.6 8.5 %collective-permute-start.4 = (bf16[144,2048]{1,0:T(8,128)(2,1)S(1)}, bf16[144,2048]{1,0:T(8,128)(2,1)S(1)}, u32[]{:S(2)}, u32[]{:S(2)}) collective-permute-start(bf16[144,2048]{1,0:T(8,128)(2,1)S(1)} %slice_bitcast_fusion.3), channel_id=1, source_target_pairs={{12,4},{13,5},{14,6},{15,7},{28,20},{29,21},{30,22},{31,23}} | collective-permute-start | bytes 1769480 | tf_op jit(solution)/shard_map/ppermute | solution.py:549
  50.1 1.4 %collective-permute-start.7 = (bf16[152,2048]{1,0:T(8,128)(2,1)}, bf16[152,2048]{1,0:T(8,128)(2,1)S(1)}, u32[]{:S(2)}, u32[]{:S(2)}) collective-permute-start(bf16[152,2048]{1,0:T(8,128)(2,1)} %get-tuple-element.51), channel_id=1, source_target_pairs={{0,4},{4,8},{8,12},{1,5},{5,9},{9,13},{2,6},{6,10},{10,14},{3,7},{... | collective-permute-start | bytes 1867784 | tf_op jit(solution)/shard_map/ppermute | solution.py:549
  51.6 8.0 %collective-permute-done.5.refs_2_.refs_0_ = bf16[152,4096]{1,0:T(8,128)(2,1)S(1)} collective-permute-done((bf16[152,4096]{1,0:T(8,128)(2,1)}, bf16[152,4096]{1,0:T(8,128)(2,1)S(1)}, u32[]{:S(2)}, u32[]{:S(2)}) %collective-permute-start.5) | collective-permute-done | bytes 1245216 | tf_op jit(solution)/shard_map/ppermute | solution.py:549
  59.6 1.1 %collective-permute-done.4.refs_1_ = bf16[144,2048]{1,0:T(8,128)(2,1)S(1)} collective-permute-done((bf16[144,2048]{1,0:T(8,128)(2,1)S(1)}, bf16[144,2048]{1,0:T(8,128)(2,1)S(1)}, u32[]{:S(2)}, u32[]{:S(2)}) %collective-permute-start.4) | collective-permute-done | bytes 589856 | tf_op jit(solution)/shard_map/ppermute | solution.py:549
  60.6 5.8 %attend_part.3 = (f32[144,2048]{1,0:T(8,128)}, f32[144,128]{1,0:T(8,128)}, f32[144,128]{1,0:T(8,128)}, bf16[152,2048]{1,0:T(8,128)(2,1)S(1)}, bf16[152,2048]{1,0:T(8,128)(2,1)S(1)}) custom-call(s32[1]{0:T(128)} %bitcast.where_ref, s32[1,4]{1,0:T(1,128)S(1)} %copy-done.1, bf16[3,144,4096]{2,1,0:T(8,128)(2,1)} %bitcast.36, ...), custom_call_target="tpu_custom_call" | custom-call | tf_op jit(solution)/shard_map/attend_part/pallas_call | solution.py:414
  66.4 1.3 %collective-permute-start.8 = (bf16[152,2048]{1,0:T(8,128)(2,1)S(1)}, bf16[152,2048]{1,0:T(8,128)(2,1)S(1)}, u32[]{:S(2)}, u32[]{:S(2)}) collective-permute-start(bf16[152,2048]{1,0:T(8,128)(2,1)S(1)} %get-tuple-element.49), channel_id=1, source_target_pairs={{4,8},{8,12},{5,9},{9,13},{6,10},{10,14},{7,11},{11,15},{20,24},{2... | collective-permute-start | bytes 1867784 | tf_op jit(solution)/shard_map/ppermute | solution.py:549
  67.7 1.5 %collective-permute-start.9 = (bf16[152,2048]{1,0:T(8,128)(2,1)S(1)}, bf16[152,2048]{1,0:T(8,128)(2,1)}, u32[]{:S(2)}, u32[]{:S(2)}) collective-permute-start(bf16[152,2048]{1,0:T(8,128)(2,1)S(1)} %get-tuple-element.60), channel_id=1, source_target_pairs={{4,12},{5,13},{6,14},{7,15},{20,28},{21,29},{22,30},{23,31}} | collective-permute-start | bytes 1867784 | tf_op jit(solution)/shard_map/ppermute | solution.py:549
  70.4 7.9 %mixer.2.refs_2_ = bf16[144,4096]{1,0:T(8,128)(2,1)} custom-call(s32[1]{0:T(128)} %bitcast.where_ref, s32[1,4]{1,0:T(1,128)} %lengths_ref.9, bf16[3,144,4096]{2,1,0:T(8,128)(2,1)} %bitcast.25, bf16[3,144,4096]{2,1,0:T(8,128)(2,1)} %bitcast.26, bf16[3,144,4096]{2,1,0:T(8,128)(2,1)} %bitcast.27, bf16[3,7,4096]{2,1,0:T(8,128)(2,1)} %taps_ref.5, ...), custom_call_target="tpu_custom_call" | custom-call | tf_op jit(solution)/shard_map/mixer/pallas_call | solution.py:242
  79.1 3.5 %merge_part.2.refs_0_ = bf16[144,4096]{1,0:T(8,128)(2,1)} custom-call(s32[1]{0:T(128)} %bitcast.where_ref, f32[144,2048]{1,0:T(8,128)} %get-tuple-element.38.own_ref, f32[144,128]{1,0:T(8,128)} %get-tuple-element.39.own_peak_ref, f32[144,128]{1,0:T(8,128)} %get-tuple-element.40.own_total_ref, bf16[152,2048]{1,0:T(8,128)(2,1)} %copy-done.3, ...), custom_call_target="tpu_custom_call" | custom-call | tf_op jit(solution)/shard_map/merge_part/pallas_call | solution.py:508
  82.6 7.9 %mixer.3 = bf16[144,4096]{1,0:T(8,128)(2,1)} custom-call(s32[1]{0:T(128)} %bitcast.where_ref, s32[1,4]{1,0:T(1,128)} %lengths_ref.9, bf16[3,144,4096]{2,1,0:T(8,128)(2,1)} %bitcast.28, bf16[3,144,4096]{2,1,0:T(8,128)(2,1)} %bitcast.29, bf16[3,144,4096]{2,1,0:T(8,128)(2,1)} %bitcast.30, ...), custom_call_target="tpu_custom_call", output_to_operand_aliasing={{}: (10, {})} | custom-call | tf_op jit(solution)/shard_map/mixer/pallas_call | solution.py:242
  90.5 9.8 %collective-permute-done.8.near_ref.near_low_ref = bf16[152,2048]{1,0:T(8,128)(2,1)S(1)} collective-permute-done((bf16[152,2048]{1,0:T(8,128)(2,1)S(1)}, bf16[152,2048]{1,0:T(8,128)(2,1)S(1)}, u32[]{:S(2)}, u32[]{:S(2)}) %collective-permute-start.8) | collective-permute-done | bytes 622624 | tf_op jit(solution)/shard_map/ppermute | solution.py:549
  101.2 3.5 %merge_part.3 = bf16[144,4096]{1,0:T(8,128)(2,1)} custom-call(s32[1]{0:T(128)} %bitcast.where_ref, f32[144,2048]{1,0:T(8,128)} %get-tuple-element.57.own_ref, f32[144,128]{1,0:T(8,128)} %get-tuple-element.58.own_peak_ref, f32[144,128]{1,0:T(8,128)} %get-tuple-element.59.own_total_ref, bf16[152,2048]{1,0:T(8,128)(2,1)} %copy-done.4, ...), custom_call_target="tpu_custom_call", output_to_operand_aliasing={{}: (8, {})} | custom-call | tf_op jit(solution)/shard_map/merge_part/pallas_call | solution.py:508
  (24 shorter events, 3.6 us)
Async XLA Ops:
  3.1 29.8 %collective-permute-start.2 = (bf16[144,4096]{1,0:T(8,128)(2,1)S(1)}, bf16[144,4096]{1,0:T(8,128)(2,1)S(1)}, u32[]{:S(2)}, u32[]{:S(2)}) collective-permute-start(bf16[144,4096]{1,0:T(8,128)(2,1)S(1)} %pad_maximum_fusion), channel_id=1, source_target_pairs={{0,4},{1,5},{2,6},{3,7},{16,20},{17,21},{18,22},{19,23}} | collective-permute-start | bytes 3538952 | tf_op jit(solution)/shard_map/ppermute | solution.py:546
  3.9 16.4 %collective-permute-start = (bf16[144,2048]{1,0:T(8,128)(2,1)}, bf16[144,2048]{1,0:T(8,128)(2,1)S(1)}, u32[]{:S(2)}, u32[]{:S(2)}) collective-permute-start(bf16[144,2048]{1,0:T(8,128)(2,1)} %get-tuple-element.64), channel_id=1, source_target_pairs={{8,4},{12,8},{9,5},{13,9},{10,6},{14,10},{11,7},{15,11},{24,20},{2... | collective-permute-start | bytes 1769480 | tf_op jit(solution)/shard_map/ppermute | solution.py:540
  6.3 26.7 %collective-permute-start.1 = (bf16[144,2048]{1,0:T(8,128)(2,1)}, bf16[144,2048]{1,0:T(8,128)(2,1)}, u32[]{:S(2)}, u32[]{:S(2)}) collective-permute-start(bf16[144,2048]{1,0:T(8,128)(2,1)} %get-tuple-element.64), channel_id=1, source_target_pairs={{12,4},{13,5},{14,6},{15,7},{28,20},{29,21},{30,22},{31,23}} | collective-permute-start | bytes 1769480 | tf_op jit(solution)/shard_map/ppermute | solution.py:541
  8.8 24.1 %copy-start.1 = (s32[1,4]{1,0:T(1,128)S(1)}, s32[1,4]{1,0:T(1,128)}, u32[]{:S(2)}) copy-start(s32[1,4]{1,0:T(1,128)} %lengths_ref.9) | copy-start | bytes 52
  16.0 43.5 %collective-permute-start.5 = (bf16[152,4096]{1,0:T(8,128)(2,1)}, bf16[152,4096]{1,0:T(8,128)(2,1)S(1)}, u32[]{:S(2)}, u32[]{:S(2)}) collective-permute-start(bf16[152,4096]{1,0:T(8,128)(2,1)} %get-tuple-element.42), channel_id=1, source_target_pairs={{0,4},{4,8},{8,12},{1,5},{5,9},{9,13},{2,6},{6,10},{10,14},{3,7},{... | collective-permute-start | bytes 3735560 | tf_op jit(solution)/shard_map/ppermute | solution.py:549
  21.4 30.2 %collective-permute-start.3 = (bf16[144,2048]{1,0:T(8,128)(2,1)S(1)}, bf16[144,2048]{1,0:T(8,128)(2,1)S(1)}, u32[]{:S(2)}, u32[]{:S(2)}) collective-permute-start(bf16[144,2048]{1,0:T(8,128)(2,1)S(1)} %slice_bitcast_fusion.4), channel_id=1, source_target_pairs={{8,4},{12,8},{9,5},{13,9},{10,6},{14,10},{11,7},{15,11},{24,20},{2... | collective-permute-start | bytes 1769480 | tf_op jit(solution)/shard_map/ppermute | solution.py:549
  39.2 28.5 %collective-permute-start.6 = (bf16[152,2048]{1,0:T(8,128)(2,1)S(1)}, bf16[152,2048]{1,0:T(8,128)(2,1)S(1)}, u32[]{:S(2)}, u32[]{:S(2)}) collective-permute-start(bf16[152,2048]{1,0:T(8,128)(2,1)S(1)} %get-tuple-element.43), channel_id=1, source_target_pairs={{0,4},{4,12},{1,5},{5,13},{2,6},{6,14},{3,7},{7,15},{16,20},{20,28... | collective-permute-start | bytes 1867784 | tf_op jit(solution)/shard_map/ppermute | solution.py:549
  41.6 19.0 %collective-permute-start.4 = (bf16[144,2048]{1,0:T(8,128)(2,1)S(1)}, bf16[144,2048]{1,0:T(8,128)(2,1)S(1)}, u32[]{:S(2)}, u32[]{:S(2)}) collective-permute-start(bf16[144,2048]{1,0:T(8,128)(2,1)S(1)} %slice_bitcast_fusion.3), channel_id=1, source_target_pairs={{12,4},{13,5},{14,6},{15,7},{28,20},{29,21},{30,22},{31,23}} | collective-permute-start | bytes 1769480 | tf_op jit(solution)/shard_map/ppermute | solution.py:549
  50.1 19.1 %copy-start.5 = (bf16[128,256]{1,0:T(8,128)(2,1)S(1)}, bf16[128,256]{1,0:T(8,128)(2,1)}, u32[]{:S(2)}) copy-start(bf16[128,256]{1,0:T(8,128)(2,1)} %param.7) | copy-start | bytes 196612
  50.1 28.1 %collective-permute-start.7 = (bf16[152,2048]{1,0:T(8,128)(2,1)}, bf16[152,2048]{1,0:T(8,128)(2,1)S(1)}, u32[]{:S(2)}, u32[]{:S(2)}) collective-permute-start(bf16[152,2048]{1,0:T(8,128)(2,1)} %get-tuple-element.51), channel_id=1, source_target_pairs={{0,4},{4,8},{8,12},{1,5},{5,9},{9,13},{2,6},{6,10},{10,14},{3,7},{... | collective-permute-start | bytes 1867784 | tf_op jit(solution)/shard_map/ppermute | solution.py:549
  59.6 6.8 %copy-start = (bf16[152,4096]{1,0:T(8,128)(2,1)}, bf16[152,4096]{1,0:T(8,128)(2,1)S(1)}, u32[]{:S(2)}) copy-start(bf16[152,4096]{1,0:T(8,128)(2,1)S(1)} %collective-permute-done.5.refs_2_.refs_0_) | copy-start | bytes 3735556
  66.4 33.9 %collective-permute-start.8 = (bf16[152,2048]{1,0:T(8,128)(2,1)S(1)}, bf16[152,2048]{1,0:T(8,128)(2,1)S(1)}, u32[]{:S(2)}, u32[]{:S(2)}) collective-permute-start(bf16[152,2048]{1,0:T(8,128)(2,1)S(1)} %get-tuple-element.49), channel_id=1, source_target_pairs={{4,8},{8,12},{5,9},{9,13},{6,10},{10,14},{7,11},{11,15},{20,24},{2... | collective-permute-start | bytes 1867784 | tf_op jit(solution)/shard_map/ppermute | solution.py:549
  67.7 2.7 %copy-start.2 = (bf16[152,2048]{1,0:T(8,128)(2,1)}, bf16[152,2048]{1,0:T(8,128)(2,1)S(1)}, u32[]{:S(2)}) copy-start(bf16[152,2048]{1,0:T(8,128)(2,1)S(1)} %collective-permute-done.6.refs_1_.far_ref.far_low_ref) | copy-start | bytes 1867780
  67.7 32.6 %collective-permute-start.9 = (bf16[152,2048]{1,0:T(8,128)(2,1)S(1)}, bf16[152,2048]{1,0:T(8,128)(2,1)}, u32[]{:S(2)}, u32[]{:S(2)}) collective-permute-start(bf16[152,2048]{1,0:T(8,128)(2,1)S(1)} %get-tuple-element.60), channel_id=1, source_target_pairs={{4,12},{5,13},{6,14},{7,15},{20,28},{21,29},{22,30},{23,31}} | collective-permute-start | bytes 1867784 | tf_op jit(solution)/shard_map/ppermute | solution.py:549
  78.3 0.8 copy-start.3
  100.3 0.8 copy-start.4
